TPU v7x, 256 devices: a whole 4x4x8 slice. The times are simulated.
256 devices in a mesh: row: 8 (over x, core), col: 32 (over y, z).
Axes of the slice: x: 4, y: 4, z: 8, core: 2. Of those that a mesh axis runs over, the one named last changes fastest.
Arguments:
- matrix: float32 [16384, 16384], P('row', 'col'), as said below
- panel: float32 [16384, 256], P(('row', 'col')), may hold values from -0.046875 to 0.046875
- factor: float32 [256, 256], replicated, as said below
Outputs:
- updated: float32 [16384, 16384], P('row', 'col')
- correction: float32 [16384, 256], P(('row', 'col'))
Inputs may be any that keep to these rules, and one draw needn't show every extreme that they name: `matrix`: symmetric. `factor`: upper triangular with a positive diagonal.
All inputs are finite; a program needn't handle non-finite values.
Results may differ from a plain program's by a relative error of at most 0.000071.
Values sent between devices are 32-bit elements; how exact they have to be, the bound alone decides.
No kernel may reach another device: no remote copies, remote signals or barrier semaphores. Data moves between devices by JAX's collectives and lax.ppermute only.
A program may use at most 64 MiB of HBM per device.

v0:
```python
import jax
import jax.numpy as jnp
from jax import lax
from jax.sharding import PartitionSpec as P


def from_root(value, axis, source):
    kept = jnp.where(lax.axis_index(axis) == source, value, 0).astype(value.dtype)
    return lax.psum(kept, axis)


def mult(left, right):
    return jnp.dot(left, right, precision=lax.Precision.HIGHEST, preferred_element_type=jnp.float32)


def per_device(matrix, panel, factor):
    ncols = lax.axis_size("col")
    nrows = lax.axis_size("row")
    blocks = panel.shape[0]
    col_index = lax.axis_index("col")
    col_rows = blocks * nrows
    offset = col_index * nrows % ncols * blocks
    owner = col_index * nrows // ncols
    row_panel = lax.all_gather(panel, "col", axis=0, tiled=True)
    col_panel = from_root(lax.dynamic_slice_in_dim(row_panel, offset, col_rows, 0), "row", owner)
    product = lax.psum_scatter(mult(matrix, col_panel), "col", scatter_dimension=0, tiled=True)
    scaled = mult(product, factor)
    small = lax.psum(mult(panel.T, scaled), ("row", "col"))
    correction = scaled - 0.5 * mult(panel, mult(factor.T, small))
    row_corr = lax.all_gather(correction, "col", axis=0, tiled=True)
    col_corr = from_root(lax.dynamic_slice_in_dim(row_corr, offset, col_rows, 0), "row", owner)
    updated = matrix - mult(row_panel, col_corr.T) - mult(row_corr, col_panel.T)
    return (updated, correction)


def solution(mesh):
    in_specs = (P("row", "col"), P(("row", "col"), None), P())
    out_specs = (P("row", "col"), P(("row", "col"), None))
    return jax.shard_map(
        per_device, mesh=mesh, in_specs=in_specs, out_specs=out_specs, check_vma=False
    )
```

profile of v0, /device:TPU:2, one launch (start us, length us, event | category | flops | bytes accessed | tf_op | source)
XLA Modules:
  0.0 800.6 jit_solution(14840826598810947577)
XLA Ops:
  7.2 0.0 copy-start
  7.2 0.0 all-gather.3.cloned.1.call-start
  7.2 0.7 all-gather.3.cloned.1.call-update
  7.9 0.0 all-reduce.4.cloned.1.call-start
  8.0 83.5 %all-gather.3.cloned.1.call-done = f32[2048,256]{1,0:T(8,128)} async-done(((f32[64,256]{1,0:T(8,128)}), f32[2048,256]{1,0:T(8,128)}) %all-gather.3.cloned.1.call-update) | async-done | bytes 2097168 | tf_op jit(solution)/shard_map/all_gather | solution.py:24
  91.5 1.9 dynamic-slice_select_fusion.1
  93.4 0.0 all-reduce.4.cloned.1.call-update
  93.4 0.0 reduce-scatter.4.cloned.1.call-start
  93.5 61.7 %all-reduce.4.cloned.1.call-done = f32[512,256]{1,0:T(8,128)} async-done(((f32[512,256]{1,0:T(8,128)}), f32[512,256]{1,0:T(8,128)}) %all-reduce.4.cloned.1.call-update) | async-done | bytes 524304 | tf_op jit(solution)/shard_map/psum | solution.py:9
  155.2 8.7 %convolution_bitcast_fusion = f32[2048,256]{0,1:T(8,128)S(1)} fusion(f32[512,256]{1,0:T(8,128)} %all-reduce.4.cloned.1.call-done, f32[2048,512]{1,0:T(8,128)} %param.3), kind=kOutput, calls=%fused_computation.2 | convolution fusion | flops 3221225472 | bytes 6815744 | tf_op jit(solution)/shard_map/dot_general | solution.py:13
  163.9 0.0 copy-start.3
  163.9 1.8 copy.12
  165.7 0.0 reduce-scatter.4.cloned.1.call-update
  165.7 0.0 all-reduce.6.cloned.1.call-start
  165.8 217.9 %reduce-scatter.4.cloned.1.call-done = f32[64,256]{1,0:T(8,128)} async-done(((f32[2048,256]{1,0:T(8,128)}), f32[64,256]{1,0:T(8,128)}) %reduce-scatter.4.cloned.1.call-update) | async-done | bytes 65552
  383.7 0.0 copy-done
  383.7 1.1 fusion.3
  384.8 0.0 copy-done.3
  384.8 1.1 convolution_bitcast_fusion.1
  385.9 0.0 all-reduce.6.cloned.1.call-update
  386.0 0.0 all-gather.5.cloned.1.call-start
  386.0 252.1 %all-reduce.6.cloned.1.call-done = f32[256,256]{0,1:T(8,128)} async-done(((f32[256,256]{0,1:T(8,128)}), f32[256,256]{0,1:T(8,128)}) %all-reduce.6.cloned.1.call-update) | async-done | bytes 262160 | tf_op jit(solution)/shard_map/psum | solution.py:28
  638.1 1.3 fusion.4
  639.4 1.0 fusion.2
  640.4 0.0 all-gather.5.cloned.1.call-update
  640.4 0.0 copy-start.2
  640.5 0.0 all-reduce.8.cloned.1.call-start
  640.5 5.4 copy.8
  645.9 0.0 copy-start.1
  645.9 71.8 %all-gather.5.cloned.1.call-done = f32[2048,256]{1,0:T(8,128)} async-done(((f32[64,256]{1,0:T(8,128)}), f32[2048,256]{1,0:T(8,128)}) %all-gather.5.cloned.1.call-update) | async-done | bytes 2097168 | tf_op jit(solution)/shard_map/all_gather | solution.py:30
  717.7 1.9 dynamic-slice_select_fusion
  719.6 0.0 all-reduce.8.cloned.1.call-update
  719.6 0.0 copy-done.2
  719.6 6.9 fusion.5
  726.6 54.1 %all-reduce.8.cloned.1.call-done = f32[512,256]{1,0:T(8,128)} async-done(((f32[512,256]{1,0:T(8,128)}), f32[512,256]{1,0:T(8,128)}) %all-reduce.8.cloned.1.call-update) | async-done | bytes 524304 | tf_op jit(solution)/shard_map/psum | solution.py:9
  780.7 0.0 copy-done.1
  780.7 7.7 fusion
  788.4 5.3 copy.10
Async XLA Ops:
  7.2 376.5 %copy-start = (f32[256,256]{1,0:T(8,128)S(1)}, f32[256,256]{1,0:T(8,128)}, u32[]{:S(2)}) copy-start(f32[256,256]{1,0:T(8,128)} %param.5) | copy-start | bytes 786436
  7.2 84.3 %all-gather.3.cloned.1.call-start = ((), (), s32[]{:S(2)}) async-start(), calls=%async_computation.1 | async-start | bytes 2162688 | tf_op jit(solution)/shard_map/all_gather | solution.py:24
  7.9 147.3 %all-reduce.4.cloned.1.call-start = ((), (), s32[]{:S(2)}) async-start(), calls=%async_computation.2 | async-start | bytes 1048576 | tf_op jit(solution)/shard_map/psum | solution.py:9
  93.4 290.3 %reduce-scatter.4.cloned.1.call-start = ((), (), s32[]{:S(2)}) async-start(), calls=%async_computation.6 | async-start | bytes 2162688
  163.9 220.9 %copy-start.3 = (f32[64,256]{1,0:T(8,128)S(1)}, f32[64,256]{1,0:T(8,128)}, u32[]{:S(2)}) copy-start(f32[64,256]{1,0:T(8,128)} %param.4) | copy-start | bytes 196612
  165.7 472.3 %all-reduce.6.cloned.1.call-start = ((), (), s32[]{:S(2)}) async-start(), calls=%async_computation.3 | async-start | bytes 524288 | tf_op jit(solution)/shard_map/psum | solution.py:28
  386.0 331.8 %all-gather.5.cloned.1.call-start = ((), (), s32[]{:S(2)}) async-start(), calls=%async_computation.4 | async-start | bytes 2162688 | tf_op jit(solution)/shard_map/all_gather | solution.py:30
  640.4 79.2 %copy-start.2 = (f32[512,256]{1,0:T(8,128)S(1)}, f32[512,256]{1,0:T(8,128)}, u32[]{:S(2)}) copy-start(f32[512,256]{1,0:T(8,128)} %all-reduce.4.cloned.1.call-done) | copy-start | bytes 1572868
  640.5 140.2 %all-reduce.8.cloned.1.call-start = ((), (), s32[]{:S(2)}) async-start(), calls=%async_computation.5 | async-start | bytes 1048576 | tf_op jit(solution)/shard_map/psum | solution.py:9
  645.9 134.7 %copy-start.1 = (f32[2048,256]{1,0:T(8,128)S(1)}, f32[2048,256]{1,0:T(8,128)}, u32[]{:S(2)}) copy-start(f32[2048,256]{1,0:T(8,128)} %all-gather.3.cloned.1.call-done) | copy-start | bytes 6291460
Sparse Core Ops, SparseCore 0:
  10.6 80.8 all-gather.2
  94.4 60.7 all-reduce.3
  165.8 217.8 reduce-scatter.3
  389.6 248.4 all-reduce.5
  641.1 76.5 all-gather.4
  719.9 60.7 all-reduce.7
where the time goes:
time: 803 us; the launch traced here: 801 us
  waiting for transfers between devices  742 us (92%)
  matrix products  27.9 us (3%)
  between operations  14.2 us (2%)
  local copies, waits for them, and re-layouts  12.6 us (2%)
    psum x1, waiting for transfers between devices, per_device(): small = lax.psum(mult(panel.T, scaled), ('row', 'col'))  252 us
    unnamed x7, waiting for transfers between devices  219 us
    psum x2, waiting for transfers between devices, from_root(): return lax.psum(kept, axis)  116 us
    all_gather x1, waiting for transfers between devices, per_device(): row_panel = lax.all_gather(panel, 'col', axis=0, tiled=True)  83.5 us
    all_gather x1, waiting for transfers between devices, per_device(): row_corr = lax.all_gather(correction, 'col', axis=0, tiled=True)  71.8 us
    dot_general x7, matrix products, mult(): jnp.dot(left, right, precision=lax.Precision.HIGHEST, preferred_element_t...  27.9 us
  transfers between devices with their start and end apart: 6, of which 6 were waited for; matrix products, arithmetic and copies ran while one was open for 2% of the time, Pallas kernels for 0%

commit v1 on v0

v1 whole, which is shorter than its diff:
```python
import jax
import jax.numpy as jnp
from jax import lax
from jax.sharding import PartitionSpec as P

NY, NZ = 4, 8
HIGH = lax.Precision.HIGH
Z_GROUPS = [[y * NZ + z for z in range(NZ)] for y in range(NY)]
Y_GROUPS = [[y * NZ + z for y in range(NY)] for z in range(NZ)]


def dot(left, right, contract):
    return lax.dot_general(
        left, right, (contract, ((), ())), precision=HIGH, preferred_element_type=jnp.float32
    )


def spread(value, groups):
    count = len(groups[0])
    copies = jnp.broadcast_to(value, (count,) + value.shape)
    return lax.all_to_all(copies, "col", 0, 0, axis_index_groups=groups)


def y_shift(value, step):
    perm = [(y * NZ + z, (y + step) % NY * NZ + z) for y in range(NY) for z in range(NZ)]
    return lax.ppermute(value, "col", perm)


def home_to_column(nrows):
    pairs = []
    for r in range(nrows):
        for y in range(NY):
            for z in range(NZ):
                block = y * NZ + z
                pairs.append(((block // NY * NY + block % NY) * NZ + r, r * NY * NZ + block))
    return pairs


def per_device(matrix, panel, factor):
    nrows = lax.axis_size("row")
    rows, width = panel.shape
    block = rows * NZ
    row, col = lax.axis_index("row"), lax.axis_index("col")
    y, z = col // NZ, col % NZ
    to_column = home_to_column(nrows)
    to_home = [(b, a) for a, b in to_column]

    own_block = spread(panel, Z_GROUPS).reshape(block, width)
    col_panel = lax.ppermute(own_block, ("row", "col"), to_column)
    row_panel = spread(own_block, Y_GROUPS).reshape(block * NY, width)

    partial = dot(matrix, row_panel, ((0,), (0,)))
    partial = dot(partial, factor, ((1,), (0,)))
    parts = lax.all_to_all(partial.reshape(nrows, rows, width), "row", 0, 0)
    chunk = jnp.sum(parts, axis=0)
    col_scaled = lax.all_gather(chunk, "row", axis=0, tiled=True)

    home = lax.ppermute(col_scaled, ("row", "col"), to_home)
    others = [y_shift(home, step) for step in (1, 2, 3)]
    inner = dot(col_panel, col_scaled, ((0,), (0,)))
    depth = width // nrows
    inner = lax.dynamic_slice_in_dim(inner, row * depth, depth, 0)
    inner = jnp.sum(spread(inner, Z_GROUPS), axis=0)
    inner = jnp.sum(spread(inner, Y_GROUPS), axis=0)
    small = lax.all_gather(inner, "row", axis=0, tiled=True)
    kernel = 0.5 * dot(factor, small, ((0,), (0,)))

    scaled = lax.dynamic_slice_in_dim(home, z * rows, rows, 0)
    correction = scaled - dot(panel, kernel, ((1,), (0,)))
    left = col_scaled - dot(col_panel, kernel + kernel.T, ((1,), (0,)))
    stacked = jnp.stack([home, others[2], others[1], others[0]])
    row_scaled = jnp.roll(stacked, y, axis=0).reshape(block * NY, width)
    updated = (
        matrix
        - dot(row_panel, left, ((1,), (1,)))
        - dot(row_scaled, col_panel, ((1,), (1,)))
    )
    return updated, correction


def solution(mesh):
    in_specs = (P("row", "col"), P(("row", "col"), None), P())
    out_specs = (P("row", "col"), P(("row", "col"), None))
    return jax.shard_map(
        per_device, mesh=mesh, in_specs=in_specs, out_specs=out_specs, check_vma=False
    )
```

time: 803 us -> 223 us (0.28)
  waiting for transfers between devices: 742 us -> 16 us
  blocking collectives: 0 us -> 103 us
  starting transfers between devices: 0.24 us -> 58 us
  local copies, waits for them, and re-layouts: 12.6 us -> 26.1 us
  between operations: 14.2 us -> 0.85 us
  matrix products: 27.9 us -> 15.7 us
    psum x3 -> x0, waiting for transfers between devices: 368 us -> none  [the longest x1 252 us: per_device(): small = lax.psum(mult(panel.T, scaled), ('row', 'col'))]
    unnamed x7 -> x0, waiting for transfers between devices: 219 us -> none
    all_gather x2 -> x0, waiting for transfers between devices: 155 us -> none  [the longest x1 83.5 us: per_device(): row_panel = lax.all_gather(panel, 'col', axis=0, tiled=True)]
    all_to_all x0 -> x2, blocking collectives: none -> 54.8 us  [spread(): return lax.all_to_all(copies, 'col', 0, 0, axis_index_groups=groups)]
    all_to_all x0 -> x3, starting transfers between devices: none -> 49.3 us  [the longest x2 44.5 us: spread(): return lax.all_to_all(copies, 'col', 0, 0, axis_index_groups=groups)]
    all_gather x0 -> x2, blocking collectives: none -> 47.8 us  [the longest x1 27.5 us: per_device(): col_scaled = lax.all_gather(chunk, 'row', axis=0, tiled=True)]
    all_to_all x0 -> x3, waiting for transfers between devices: none -> 16 us  [the longest x1 8.63 us: per_device(): parts = lax.all_to_all(partial.reshape(nrows, rows, width), 'row', 0, 0)]
    dot_general x7 -> x8, matrix products: 27.9 us -> 15.7 us  [dot(): lax.dot_general(left, right, (contract, ((), ())), precision=HIGH, prefer...]
  transfers between devices with their start and end apart: 6 -> 8, of which waited for: 6 -> 2; matrix products, arithmetic and copies ran while one was open for 2% -> 10% of each run, Pallas kernels for 0% -> 0%
where the time goes in v1:
time: 223 us; the launch traced here: 221 us
  blocking collectives  103 us (46%)
  starting transfers between devices  58 us (26%)
  local copies, waits for them, and re-layouts  26.1 us (12%)
  waiting for transfers between devices  16 us (7%)
  matrix products  15.7 us (7%)
    all_to_all x2, blocking collectives, spread(): return lax.all_to_all(copies, 'col', 0, 0, axis_index_groups=groups)  54.8 us
    all_to_all x2, starting transfers between devices, spread(): return lax.all_to_all(copies, 'col', 0, 0, axis_index_groups=groups)  44.5 us
    all_gather x1, blocking collectives, per_device(): col_scaled = lax.all_gather(chunk, 'row', axis=0, tiled=True)  27.5 us
    all_gather x1, blocking collectives, per_device(): small = lax.all_gather(inner, 'row', axis=0, tiled=True)  20.3 us
    unnamed x21, local copies, waits for them, and re-layouts  19.4 us
    dot_general x8, matrix products, dot(): lax.dot_general(left, right, (contract, ((), ())), precision=HIGH, prefer...  15.7 us
    all_to_all x1, waiting for transfers between devices, per_device(): parts = lax.all_to_all(partial.reshape(nrows, rows, width), 'row', 0, 0)  8.63 us
    all_to_all x2, waiting for transfers between devices, spread(): return lax.all_to_all(copies, 'col', 0, 0, axis_index_groups=groups)  7.33 us
  transfers between devices with their start and end apart: 8, of which 2 were waited for; matrix products, arithmetic and copies ran while one was open for 10% of the time, Pallas kernels for 0%

profile of v1, /device:TPU:2, one launch (start us, length us, event | category | flops | bytes accessed | tf_op | source)
XLA Modules:
  0.0 220.9 jit_solution(6294064425700137475)
XLA Ops:
  0.6 0.0 copy-start
  0.6 0.0 copy-start.1
  0.7 1.0 broadcast_in_dim.12
  1.7 26.0 %all_to_all.25 = f32[8,64,256]{2,1,0:T(8,128)} all-to-all(f32[8,64,256]{2,1,0:T(8,128)S(1)} %broadcast_in_dim.12), channel_id=1, replica_groups={{0,1,2,3,4,5,6,7},{8,9,10,11,12,13,14,15},{16,17,18,19,20,21,22,23},{24..., dimensions={0} | all-to-all | bytes 1048576 | tf_op jit(solution)/shard_map/all_to_all | solution.py:21
  27.7 1.2 broadcast_in_dim.13
  28.9 28.8 %all_to_all.26 = f32[4,512,256]{2,1,0:T(8,128)S(1)} all-to-all(f32[4,512,256]{2,1,0:T(8,128)S(1)} %broadcast_in_dim.13), channel_id=1, replica_groups={{0,8,16,24},{1,9,17,25},{2,10,18,26},{3,11,19,27},{4,12,20,28},{5,13,21..., dimensions={0} | all-to-all | bytes 4194304 | tf_op jit(solution)/shard_map/all_to_all | solution.py:21
  57.7 0.0 copy-done.1
  57.7 3.6 %fusion.2 = f32[512,256]{1,0:T(8,128)S(1)} fusion(f32[2048,512]{1,0:T(8,128)S(1)} %copy-done.1, f32[2048,256]{1,0:T(8,128)S(1)} %bitcast.46), kind=kOutput, calls=%fused_computation.18 | convolution fusion | flops 1610612736 | bytes 6815744 | tf_op jit(solution)/shard_map/dot_general | solution.py:13
  61.3 0.0 copy-done
  61.4 1.2 fusion.3
  62.5 4.8 %all-to-all-start.2 = ((f32[8,64,256]{2,1,0:T(8,128)}), f32[8,64,256]{2,1,0:T(8,128)S(1)}, u32[]{:S(2)}, u32[]{:S(2)}) async-start(f32[8,64,256]{2,1,0:T(8,128)} %bitcast.2), calls=%async_computation.2 | async-start | bytes 1048576 | tf_op jit(solution)/shard_map/all_to_all | solution.py:54
  67.4 1.9 collective-permute-start
  69.3 8.6 %all-to-all-done.2 = f32[8,64,256]{2,1,0:T(8,128)S(1)} async-done(((f32[8,64,256]{2,1,0:T(8,128)}), f32[8,64,256]{2,1,0:T(8,128)S(1)}, u32[]{:S(2)}, u32[]{:S(2)}) %all-to-all-start.2) | async-done | bytes 524320 | tf_op jit(solution)/shard_map/all_to_all | solution.py:54
  78.0 27.5 %all_gather.6 = f32[512,256]{1,0:T(8,128)S(1)} all-gather(f32[64,256]{1,0:T(8,128)S(1)} %reduce_sum.27), channel_id=1, replica_groups=mesh['row'=8,'col'=32] {'row'}, dimensions={0}, use_global_device_ids=true | all-gather | bytes 589824 | tf_op jit(solution)/shard_map/all_gather | solution.py:56
  105.5 1.9 collective-permute-start.1
  107.4 0.0 collective-permute-done
  107.4 0.6 fusion.4
  108.1 0.7 broadcast_in_dim.14
  108.8 41.2 %all-to-all-start.3 = ((f32[8,32,256]{2,1,0:T(8,128)}), f32[8,32,256]{2,1,0:T(8,128)}, u32[]{:S(2)}, u32[]{:S(2)}) async-start(f32[8,32,256]{2,1,0:T(8,128)} %broadcast_in_dim.14), calls=%async_computation.3 | async-start | bytes 524288 | tf_op jit(solution)/shard_map/all_to_all | solution.py:21
  150.0 5.3 %copy.11 = f32[2048,512]{0,1:T(8,128)} copy(f32[2048,512]{1,0:T(8,128)} %param.3) | data formatting | bytes 8388608 | tf_op args[0]
  155.3 7.3 %all-to-all-done.3 = f32[8,32,256]{2,1,0:T(8,128)} async-done(((f32[8,32,256]{2,1,0:T(8,128)}), f32[8,32,256]{2,1,0:T(8,128)}, u32[]{:S(2)}, u32[]{:S(2)}) %all-to-all-start.3) | async-done | bytes 262176 | tf_op jit(solution)/shard_map/all_to_all | solution.py:21
  162.6 1.0 reduce_sum.28
  163.6 0.7 broadcast_in_dim.15
  164.3 3.3 %all-to-all-start.4 = ((f32[4,32,256]{2,1,0:T(8,128)}), f32[4,32,256]{2,1,0:T(8,128)S(1)}, u32[]{:S(2)}, u32[]{:S(2)}) async-start(f32[4,32,256]{2,1,0:T(8,128)} %broadcast_in_dim.15), calls=%async_computation.4 | async-start | bytes 262144 | tf_op jit(solution)/shard_map/all_to_all | solution.py:21
  167.6 0.0 collective-permute-done.1
  167.6 3.2 %collective-permute-start.2 = (f32[512,256]{1,0:T(8,128)}, f32[512,256]{1,0:T(8,128)}, u32[]{:S(2)}, u32[]{:S(2)}) collective-permute-start(f32[512,256]{1,0:T(8,128)} %collective-permute-done.1), channel_id=1, source_target_pairs={{0,24},{1,25},{2,26},{3,27},{4,28},{5,29},{6,30},{7,31},{8,0},{9,1... | collective-permute-start | bytes 1572872 | tf_op jit(solution)/shard_map/ppermute | solution.py:26
  170.8 1.9 bitcast_dynamic-update-slice_fusion.6
  172.7 0.9 collective-permute-start.3
  173.6 0.9 collective-permute-start.4
  174.4 0.0 all-to-all-done.4
  174.4 0.6 reduce_sum.29
  175.1 20.3 %all_gather.7 = f32[256,256]{1,0:T(8,128)S(1)} all-gather(f32[32,256]{1,0:T(8,128)} %reduce_sum.29), channel_id=1, replica_groups=mesh['row'=8,'col'=32] {'row'}, dimensions={0}, use_global_device_ids=true | all-gather | bytes 294912 | tf_op jit(solution)/shard_map/all_gather | solution.py:65
  195.3 1.1 convolution_multiply_fusion
  196.4 1.8 copy.10
  198.2 0.0 copy-start.3
  198.2 0.0 copy-start.5
  198.2 0.0 copy-start.4
  198.2 1.6 fusion.1
  199.8 1.9 fusion.5
  201.7 0.0 copy-done.3
  201.7 0.0 copy-done.5
  201.7 1.7 dynamic-slice_subtract_fusion
  203.5 0.0 collective-permute-done.2
  203.5 0.0 copy-done.4
  203.5 1.1 bitcast_dynamic-update-slice_fusion.4
  204.5 0.0 collective-permute-done.3
  204.5 1.1 bitcast_dynamic-update-slice_fusion.2
  205.6 0.0 collective-permute-done.4
  205.6 1.1 bitcast_dynamic-update-slice_fusion
  206.7 0.0 copy-start.2
  206.7 1.2 bitcast_dynamic-update-slice_fusion.7
  208.0 1.3 bitcast_dynamic-update-slice_fusion.5
  209.2 1.1 bitcast_dynamic-update-slice_fusion.3
  210.3 1.1 bitcast_dynamic-update-slice_fusion.1
  211.4 0.1 constant_dynamic-slice_fusion
  211.5 0.0 copy-done.2
  211.5 4.0 %fusion = f32[2048,512]{0,1:T(8,128)} fusion(f32[2048,512]{0,1:T(8,128)S(1)} %copy-done.2, f32[512,2048]{1,0:T(8,128)S(1)} %fusion.5, f32[2048,256]{1,0:T(8,128)S(1)} %bitcast.48, f32[512,256]{1,0:T(8,128)S(1)} %collective-permute-done), kind=kOutput, calls=%fused_computation.1 | convolution fusion | flops 1612709888 | bytes 15204352 | tf_op jit(solution)/shard_map/dot_general | solution.py:13
  215.6 5.3 %copy.13 = f32[2048,512]{1,0:T(8,128)} copy(f32[2048,512]{0,1:T(8,128)} %fusion) | data formatting | bytes 8388608
  (2 shorter events, 0.0 us)
Async XLA Ops:
  0.6 60.7 %copy-start = (f32[256,256]{1,0:T(8,128)S(1)}, f32[256,256]{1,0:T(8,128)}, u32[]{:S(2)}) copy-start(f32[256,256]{1,0:T(8,128)} %param.5) | copy-start | bytes 786436
  0.6 57.1 %copy-start.1 = (f32[2048,512]{1,0:T(8,128)S(1)}, f32[2048,512]{1,0:T(8,128)}, u32[]{:S(2)}) copy-start(f32[2048,512]{1,0:T(8,128)} %param.3) | copy-start | bytes 12582916
  62.5 15.4 %all-to-all-start.2 = ((f32[8,64,256]{2,1,0:T(8,128)}), f32[8,64,256]{2,1,0:T(8,128)S(1)}, u32[]{:S(2)}, u32[]{:S(2)}) async-start(f32[8,64,256]{2,1,0:T(8,128)} %bitcast.2), calls=%async_computation.2 | async-start | bytes 1048576 | tf_op jit(solution)/shard_map/all_to_all | solution.py:54
  67.4 40.1 %collective-permute-start = (f32[512,256]{1,0:T(8,128)}, f32[512,256]{1,0:T(8,128)S(1)}, u32[]{:S(2)}, u32[]{:S(2)}) collective-permute-start(f32[512,256]{1,0:T(8,128)} %bitcast), channel_id=1, source_target_pairs={{0,0},{8,1},{16,2},{24,3},{32,4},{40,5},{48,6},{56,7},{64,8},{72,9... | collective-permute-start | bytes 1572872 | tf_op jit(solution)/shard_map/ppermute | solution.py:49
  105.5 62.1 %collective-permute-start.1 = (f32[512,256]{1,0:T(8,128)S(1)}, f32[512,256]{1,0:T(8,128)}, u32[]{:S(2)}, u32[]{:S(2)}) collective-permute-start(f32[512,256]{1,0:T(8,128)S(1)} %all_gather.6), channel_id=1, source_target_pairs={{0,0},{1,8},{2,16},{3,24},{4,32},{5,40},{6,48},{7,56},{8,64},{9,72... | collective-permute-start | bytes 1572872 | tf_op jit(solution)/shard_map/ppermute | solution.py:58
  108.8 53.8 %all-to-all-start.3 = ((f32[8,32,256]{2,1,0:T(8,128)}), f32[8,32,256]{2,1,0:T(8,128)}, u32[]{:S(2)}, u32[]{:S(2)}) async-start(f32[8,32,256]{2,1,0:T(8,128)} %broadcast_in_dim.14), calls=%async_computation.3 | async-start | bytes 524288 | tf_op jit(solution)/shard_map/all_to_all | solution.py:21
  164.3 10.2 %all-to-all-start.4 = ((f32[4,32,256]{2,1,0:T(8,128)}), f32[4,32,256]{2,1,0:T(8,128)S(1)}, u32[]{:S(2)}, u32[]{:S(2)}) async-start(f32[4,32,256]{2,1,0:T(8,128)} %broadcast_in_dim.15), calls=%async_computation.4 | async-start | bytes 262144 | tf_op jit(solution)/shard_map/all_to_all | solution.py:21
  167.6 35.8 %collective-permute-start.2 = (f32[512,256]{1,0:T(8,128)}, f32[512,256]{1,0:T(8,128)}, u32[]{:S(2)}, u32[]{:S(2)}) collective-permute-start(f32[512,256]{1,0:T(8,128)} %collective-permute-done.1), channel_id=1, source_target_pairs={{0,24},{1,25},{2,26},{3,27},{4,28},{5,29},{6,30},{7,31},{8,0},{9,1... | collective-permute-start | bytes 1572872 | tf_op jit(solution)/shard_map/ppermute | solution.py:26
  172.7 31.8 %collective-permute-start.3 = (f32[512,256]{1,0:T(8,128)}, f32[512,256]{1,0:T(8,128)}, u32[]{:S(2)}, u32[]{:S(2)}) collective-permute-start(f32[512,256]{1,0:T(8,128)} %collective-permute-done.1), channel_id=1, source_target_pairs={{0,16},{1,17},{2,18},{3,19},{4,20},{5,21},{6,22},{7,23},{8,24},{9,... | collective-permute-start | bytes 1572872 | tf_op jit(solution)/shard_map/ppermute | solution.py:26
  173.6 32.1 %collective-permute-start.4 = (f32[512,256]{1,0:T(8,128)}, f32[512,256]{1,0:T(8,128)}, u32[]{:S(2)}, u32[]{:S(2)}) collective-permute-start(f32[512,256]{1,0:T(8,128)} %collective-permute-done.1), channel_id=1, source_target_pairs={{0,8},{1,9},{2,10},{3,11},{4,12},{5,13},{6,14},{7,15},{8,16},{9,17... | collective-permute-start | bytes 1572872 | tf_op jit(solution)/shard_map/ppermute | solution.py:26
  198.2 3.5 %copy-start.3 = (f32[256,256]{1,0:T(8,128)S(1)}, f32[256,256]{1,0:T(8,128)}, u32[]{:S(2)}) copy-start(f32[256,256]{1,0:T(8,128)} %convolution_multiply_fusion) | copy-start | bytes 786436
  198.2 3.5 %copy-start.5 = (f32[64,256]{1,0:T(8,128)S(1)}, f32[64,256]{1,0:T(8,128)}, u32[]{:S(2)}) copy-start(f32[64,256]{1,0:T(8,128)} %param.4) | copy-start | bytes 196612
  198.2 5.3 %copy-start.4 = (f32[8,512,256]{2,1,0:T(8,128)S(1)}, f32[8,512,256]{2,1,0:T(8,128)}, u32[]{:S(2)}) copy-start(f32[8,512,256]{2,1,0:T(8,128)} %bitcast_dynamic-update-slice_fusion.6) | copy-start | bytes 12582916
  206.7 4.8 %copy-start.2 = (f32[2048,512]{0,1:T(8,128)S(1)}, f32[2048,512]{0,1:T(8,128)}, u32[]{:S(2)}) copy-start(f32[2048,512]{0,1:T(8,128)} %copy.11) | copy-start | bytes 12582916

commit v2 on v0

v2 whole, which is shorter than its diff:
```python
import jax
import jax.numpy as jnp
from jax import lax
from jax.experimental import pallas as pl
from jax.experimental.pallas import tpu as pltpu
from jax.sharding import PartitionSpec as P

NY, NZ = 4, 8
HIGH = lax.Precision.HIGH
Z_GROUPS = [[y * NZ + z for z in range(NZ)] for y in range(NY)]
Y_GROUPS = [[y * NZ + z for y in range(NY)] for z in range(NZ)]
TILE = 256


def dot(left, right, contract):
    return lax.dot_general(
        left, right, (contract, ((), ())), precision=HIGH, preferred_element_type=jnp.float32
    )


def spread(value, axis, groups=None):
    count = lax.axis_size(axis) if groups is None else len(groups[0])
    copies = jnp.broadcast_to(value, (count,) + value.shape)
    return lax.all_to_all(copies, axis, 0, 0, axis_index_groups=groups)


def y_shift(value, step):
    perm = [(y * NZ + z, (y + step) % NY * NZ + z) for y in range(NY) for z in range(NZ)]
    return lax.ppermute(value, "col", perm)


def y_blocks(value):
    return [value] + [y_shift(value, step) for step in range(1, NY)]


def after(value, *others):
    return lax.optimization_barrier((value,) + others)[0]


def halves(value):
    high = value.astype(jnp.bfloat16)
    return high, (value - high.astype(jnp.float32)).astype(jnp.bfloat16)


def update_kernel(y_ref, matrix, right, *refs):
    panels, scaleds = refs[:NY], refs[NY : 2 * NY]
    out, left, right_high, right_low = refs[2 * NY :]
    step = pl.program_id(0)

    @pl.when((step == 0) & (pl.program_id(1) == 0))
    def _():
        right_high[...], right_low[...] = halves(right[...])

    width = left.shape[1] // 2
    for k in range(NY):

        @pl.when(step == k)
        def _():
            left[:, :width] = panels[k][...]
            left[:, width:] = scaleds[k][...]

    left_high, left_low = halves(left[...])
    total = jnp.dot(left_high, right_low[...], preferred_element_type=jnp.float32)
    total += jnp.dot(left_low, right_high[...], preferred_element_type=jnp.float32)
    total += jnp.dot(left_high, right_high[...], preferred_element_type=jnp.float32)
    out[...] = matrix[...] - total


def update(y, matrix, panels, scaleds, right):
    rows, cols = matrix.shape
    block, width = panels[0].shape
    tiles = block // TILE

    def moving(s, h, y_ref):
        return (lax.rem(y_ref[0] + (NY - s), NY) * tiles + h, 0)

    def part(k):
        def index(s, h, y_ref):
            return (jnp.where(s == k, h, jnp.where(s < k, 0, tiles - 1)), 0)

        return pl.BlockSpec((TILE, width), index)

    parts = [part(k) for k in range(NY)]
    return pl.pallas_call(
        update_kernel,
        out_shape=jax.ShapeDtypeStruct((rows, cols), jnp.float32),
        grid_spec=pltpu.PrefetchScalarGridSpec(
            num_scalar_prefetch=1,
            grid=(NY, tiles),
            in_specs=[
                pl.BlockSpec((TILE, cols), moving),
                pl.BlockSpec((2 * width, cols), lambda s, h, y_ref: (0, 0)),
            ]
            + parts
            + parts,
            out_specs=pl.BlockSpec((TILE, cols), moving),
            scratch_shapes=[
                pltpu.VMEM((TILE, 2 * width), jnp.float32),
                pltpu.VMEM((2 * width, cols), jnp.bfloat16),
                pltpu.VMEM((2 * width, cols), jnp.bfloat16),
            ],
        ),
        cost_estimate=pl.CostEstimate(
            flops=12 * rows * cols * width,
            bytes_accessed=8 * rows * cols + 8 * rows * width,
            transcendentals=0,
        ),
        compiler_params=pltpu.CompilerParams(vmem_limit_bytes=24 << 20),
    )(y.reshape(1), matrix, right, *panels, *scaleds)


def per_device(matrix, panel, factor):
    nrows, ncols = lax.axis_size("row"), lax.axis_size("col")
    rows, width = panel.shape
    block = NZ * rows
    depth = width // nrows
    y = lax.axis_index("col") // NZ
    total = nrows * ncols
    to_column = [(g, g % nrows * ncols + g // nrows) for g in range(total)]
    to_home = [(b, a) for a, b in to_column]

    moved = lax.ppermute(panel, ("row", "col"), to_column)
    own_panel = spread(panel, "col", Z_GROUPS).reshape(block, width)
    panels = y_blocks(own_panel)
    col_panel = spread(after(moved, own_panel), "row").reshape(nrows * rows, width)

    partial = 0.0
    for step in range(NY):
        start = lax.rem(y + (NY - step), NY) * block
        piece = lax.dynamic_slice_in_dim(matrix, start, block, 0)
        partial += dot(piece, panels[step], ((0,), (0,)))
    partial = dot(partial, factor, ((1,), (0,)))
    inner = dot(col_panel, partial, ((0,), (0,)))
    parts = jnp.concatenate(
        [partial.reshape(nrows, rows, width), inner.reshape(nrows, depth, width)], axis=1
    )
    parts = jnp.sum(lax.all_to_all(parts, "row", 0, 0), axis=0)
    chunk, inner = parts[:rows], parts[rows:]

    home = lax.ppermute(chunk, ("row", "col"), to_home)
    inner = jnp.sum(spread(inner, "col", Z_GROUPS), axis=0)
    own_scaled = spread(after(home, inner), "col", Z_GROUPS).reshape(block, width)
    inner = sum(y_blocks(inner))
    scaleds = y_blocks(own_scaled)
    gathered = spread(after(jnp.concatenate([chunk, inner]), own_scaled), "row")
    col_scaled = gathered[:, :rows].reshape(nrows * rows, width)
    small = gathered[:, rows:].reshape(width, width)

    kernel = 0.5 * dot(factor, small, ((0,), (0,)))
    correction = home - dot(panel, kernel, ((1,), (0,)))
    left = col_scaled - dot(col_panel, kernel + kernel.T, ((1,), (0,)))
    right = jnp.concatenate([left.T, col_panel.T], axis=0)
    return update(y, matrix, panels, scaleds, right), correction


def solution(mesh):
    in_specs = (P("row", "col"), P(("row", "col"), None), P())
    out_specs = (P("row", "col"), P(("row", "col"), None))
    return jax.shard_map(
        per_device, mesh=mesh, in_specs=in_specs, out_specs=out_specs, check_vma=False
    )
```

time: 803 us -> 174 us (0.22)
  waiting for transfers between devices: 742 us -> 57.1 us
  starting transfers between devices: 0.24 us -> 59.1 us
  blocking collectives: 0 us -> 16.5 us
  between operations: 14.2 us -> 0.83 us
  matrix products: 27.9 us -> 15.7 us
  Pallas kernels: 0 us -> 8.32 us
    psum x3 -> x0, waiting for transfers between devices: 368 us -> none  [the longest x1 252 us: per_device(): small = lax.psum(mult(panel.T, scaled), ('row', 'col'))]
    unnamed x7 -> x0, waiting for transfers between devices: 219 us -> none
    all_gather x2 -> x0, waiting for transfers between devices: 155 us -> none  [the longest x1 83.5 us: per_device(): row_panel = lax.all_gather(panel, 'col', axis=0, tiled=True)]
    all_to_all x0 -> x5, starting transfers between devices: none -> 36.4 us  [spread(): return lax.all_to_all(copies, axis, 0, 0, axis_index_groups=groups)]
    all_to_all x0 -> x5, waiting for transfers between devices: none -> 35.5 us  [spread(): return lax.all_to_all(copies, axis, 0, 0, axis_index_groups=groups)]
    ppermute x0 -> x11, starting transfers between devices: none -> 22.8 us  [the longest x9 13.6 us: y_shift(): return lax.ppermute(value, 'col', perm)]
    ppermute x0 -> x11, waiting for transfers between devices: none -> 21.6 us  [the longest x9 21.6 us: y_shift(): return lax.ppermute(value, 'col', perm)]
    all_to_all x0 -> x1, blocking collectives: none -> 16.5 us  [per_device(): parts = jnp.sum(lax.all_to_all(parts, 'row', 0, 0), axis=0)]
  transfers between devices with their start and end apart: 6 -> 16, of which waited for: 6 -> 11; matrix products, arithmetic and copies ran while one was open for 2% -> 13% of each run, Pallas kernels for 0% -> 0%
where the time goes in v2:
time: 174 us; the launch traced here: 172 us
  starting transfers between devices  59.1 us (34%)
  waiting for transfers between devices  57.1 us (33%)
  blocking collectives  16.5 us (9%)
  matrix products  15.7 us (9%)
  local copies, waits for them, and re-layouts  11.9 us (7%)
  Pallas kernels  8.32 us (5%)
  other arithmetic  2.39 us (1%)
    all_to_all x5, starting transfers between devices, spread(): return lax.all_to_all(copies, axis, 0, 0, axis_index_groups=groups)  36.4 us
    all_to_all x5, waiting for transfers between devices, spread(): return lax.all_to_all(copies, axis, 0, 0, axis_index_groups=groups)  35.5 us
    ppermute x9, waiting for transfers between devices, y_shift(): return lax.ppermute(value, 'col', perm)  21.6 us
    all_to_all x1, blocking collectives, per_device(): parts = jnp.sum(lax.all_to_all(parts, 'row', 0, 0), axis=0)  16.5 us
    dot_general x9, matrix products, dot(): lax.dot_general(left, right, (contract, ((), ())), precision=HIGH, prefer...  15.7 us
    ppermute x9, starting transfers between devices, y_shift(): return lax.ppermute(value, 'col', perm)  13.6 us
    pallas_call x1, Pallas kernels, update(): pl.pallas_call(update_kernel, out_shape=jax.ShapeDtypeStruct((rows, cols)...  8.32 us
    ppermute x1, starting transfers between devices, per_device(): home = lax.ppermute(chunk, ('row', 'col'), to_home)  5.73 us
  transfers between devices with their start and end apart: 16, of which 11 were waited for; matrix products, arithmetic and copies ran while one was open for 13% of the time, Pallas kernels for 0%

profile of v2, /device:TPU:2, one launch (start us, length us, event | category | flops | bytes accessed | tf_op | source)
XLA Modules:
  0.0 171.9 jit_solution(13618540475660251122)
XLA Ops:
  0.6 0.0 copy-start
  0.6 1.7 broadcast_in_dim.15
  2.4 8.5 %all-to-all-start = ((f32[8,64,256]{2,1,0:T(8,128)}), f32[8,64,256]{2,1,0:T(8,128)S(1)}, u32[]{:S(2)}, u32[]{:S(2)}) async-start(f32[8,64,256]{2,1,0:T(8,128)} %broadcast_in_dim.15), calls=%async_computation | async-start | bytes 1048576 | tf_op jit(solution)/shard_map/all_to_all | solution.py:24
  10.8 3.4 %collective-permute-start.3 = (f32[64,256]{1,0:T(8,128)}, f32[64,256]{1,0:T(8,128)S(1)}, u32[]{:S(2)}, u32[]{:S(2)}) collective-permute-start(f32[64,256]{1,0:T(8,128)} %param.4), channel_id=1, source_target_pairs={{0,0},{1,32},{2,64},{3,96},{4,128},{5,160},{6,192},{7,224},{8,1},{... | collective-permute-start | bytes 196616 | tf_op jit(solution)/shard_map/ppermute | solution.py:122
  14.3 13.1 %all-to-all-done = f32[8,64,256]{2,1,0:T(8,128)S(1)} async-done(((f32[8,64,256]{2,1,0:T(8,128)}), f32[8,64,256]{2,1,0:T(8,128)S(1)}, u32[]{:S(2)}, u32[]{:S(2)}) %all-to-all-start) | async-done | bytes 524320 | tf_op jit(solution)/shard_map/all_to_all | solution.py:24
  27.4 3.2 %collective-permute-start.2 = (f32[512,256]{1,0:T(8,128)S(1)}, f32[512,256]{1,0:T(8,128)S(1)}, u32[]{:S(2)}, u32[]{:S(2)}) collective-permute-start(f32[512,256]{1,0:T(8,128)S(1)} %bitcast.34), channel_id=1, source_target_pairs={{0,24},{1,25},{2,26},{3,27},{4,28},{5,29},{6,30},{7,31},{8,0},{9,1... | collective-permute-start | bytes 1572872 | tf_op jit(solution)/shard_map/ppermute | solution.py:29
  30.5 0.0 collective-permute-done.3
  30.5 0.8 broadcast_in_dim.16
  31.4 4.8 %all-to-all-start.1 = ((f32[8,64,256]{2,1,0:T(8,128)}), f32[8,64,256]{2,1,0:T(8,128)S(1)}, u32[]{:S(2)}, u32[]{:S(2)}) async-start(f32[8,64,256]{2,1,0:T(8,128)} %broadcast_in_dim.16), calls=%async_computation.1 | async-start | bytes 1048576 | tf_op jit(solution)/shard_map/all_to_all | solution.py:24
  36.2 0.9 collective-permute-start
  37.1 3.6 %collective-permute-start.1 = (f32[512,256]{1,0:T(8,128)S(1)}, f32[512,256]{1,0:T(8,128)S(1)}, u32[]{:S(2)}, u32[]{:S(2)}) collective-permute-start(f32[512,256]{1,0:T(8,128)S(1)} %bitcast.36), channel_id=1, source_target_pairs={{0,16},{1,17},{2,18},{3,19},{4,20},{5,21},{6,22},{7,23},{8,24},{9,... | collective-permute-start | bytes 1572872 | tf_op jit(solution)/shard_map/ppermute | solution.py:29
  40.7 3.0 %fusion.7 = f32[512,256]{1,0:T(8,128)} fusion(f32[512,256]{1,0:T(8,128)S(1)} %bitcast.37, f32[2048,512]{1,0:T(8,128)} %matrix.1, s32[]{:T(128)S(6)} %select_n.18), kind=kOutput, calls=%fused_computation.13 | convolution fusion | flops 402653184 | bytes 2097156 | tf_op jit(solution)/shard_map/dot_general | solution.py:16
  43.7 1.4 all-to-all-done.1
  45.1 0.2 copy.11
  45.3 0.0 copy-start.3
  45.3 0.0 collective-permute-done.2.refs_3_
  45.3 2.4 %fusion.3 = f32[512,256]{1,0:T(8,128)S(1)} fusion(f32[512,256]{1,0:T(8,128)S(1)} %collective-permute-done.2.refs_3_, f32[2048,512]{1,0:T(8,128)} %matrix.1, s32[]{:T(128)S(6)} %select_n.21), kind=kOutput, calls=%fused_computation.9 | convolution fusion | flops 402653184 | bytes 2097156 | tf_op jit(solution)/shard_map/dot_general | solution.py:16
  47.7 3.7 %collective-permute-done.refs_1_ = f32[512,256]{1,0:T(8,128)S(1)} collective-permute-done((f32[512,256]{1,0:T(8,128)S(1)}, f32[512,256]{1,0:T(8,128)S(1)}, u32[]{:S(2)}, u32[]{:S(2)}) %collective-permute-start) | collective-permute-done | bytes 524320 | tf_op jit(solution)/shard_map/ppermute | solution.py:29
  51.5 2.4 %convolution_add_fusion.1 = f32[512,256]{1,0:T(8,128)S(1)} fusion(f32[512,256]{1,0:T(8,128)} %fusion.7, f32[512,256]{1,0:T(8,128)S(1)} %collective-permute-done.refs_1_, f32[2048,512]{1,0:T(8,128)} %matrix.1, s32[]{:T(128)S(6)} %select_n.19), kind=kOutput, calls=%fused_computation.1 | convolution fusion | flops 402784256 | bytes 2621444 | tf_op jit(solution)/shard_map/dot_general | solution.py:16
  53.9 10.0 %collective-permute-done.1.refs_2_ = f32[512,256]{1,0:T(8,128)S(1)} collective-permute-done((f32[512,256]{1,0:T(8,128)S(1)}, f32[512,256]{1,0:T(8,128)S(1)}, u32[]{:S(2)}, u32[]{:S(2)}) %collective-permute-start.1) | collective-permute-done | bytes 524320 | tf_op jit(solution)/shard_map/ppermute | solution.py:29
  63.9 2.2 %fusion = f32[512,256]{1,0:T(8,128)S(1)} fusion(f32[512,256]{1,0:T(8,128)S(1)} %fusion.3, f32[512,256]{1,0:T(8,128)S(1)} %convolution_add_fusion.1, f32[512,256]{1,0:T(8,128)S(1)} %collective-permute-done.1.refs_2_, f32[2048,512]{1,0:T(8,128)} %matrix.1, s32[]{:T(128)S(6)} %select_n.20), kind=kOutput, calls=%fused_computation.2 | convolution fusion | flops 402915328 | bytes 3145732 | tf_op jit(solution)/shard_map/dot_general | solution.py:16
  66.1 0.0 copy-done.2
  66.1 0.0 copy-done
  66.2 0.4 fusion.15
  66.5 0.0 copy-done.3
  66.5 0.4 fusion.9
  66.9 0.1 pad_maximum_fusion.1
  67.0 16.5 %all_to_all.30 = f32[8,96,256]{2,1,0:T(8,128)} all-to-all(f32[8,96,256]{2,1,0:T(8,128)S(1)} %pad_maximum_fusion.1), channel_id=1, replica_groups=mesh['row'=8,'col'=32] {'row'}, dimensions={0} | all-to-all | bytes 1572864 | tf_op jit(solution)/shard_map/all_to_all | solution.py:137
  83.5 1.2 reduce_sum.18
  84.7 0.7 broadcast_in_dim.17
  85.4 7.3 %all-to-all-start.3 = ((f32[8,32,256]{2,1,0:T(8,128)}), f32[8,32,256]{2,1,0:T(8,128)S(1)}, u32[]{:S(2)}, u32[]{:S(2)}) async-start(f32[8,32,256]{2,1,0:T(8,128)} %broadcast_in_dim.17), calls=%async_computation.3 | async-start | bytes 524288 | tf_op jit(solution)/shard_map/all_to_all | solution.py:24
  92.8 5.7 %collective-permute-start.7 = (f32[64,256]{1,0:T(8,128)S(1)}, f32[64,256]{1,0:T(8,128)S(1)}, u32[]{:S(2)}, u32[]{:S(2)}) collective-permute-start(f32[64,256]{1,0:T(8,128)S(1)} %slice.16), channel_id=1, source_target_pairs={{0,0},{32,1},{64,2},{96,3},{128,4},{160,5},{192,6},{224,7},{1,8},{... | collective-permute-start | bytes 196616 | tf_op jit(solution)/shard_map/ppermute | solution.py:140
  98.5 5.4 %all-to-all-done.3 = f32[8,32,256]{2,1,0:T(8,128)S(1)} async-done(((f32[8,32,256]{2,1,0:T(8,128)}), f32[8,32,256]{2,1,0:T(8,128)S(1)}, u32[]{:S(2)}, u32[]{:S(2)}) %all-to-all-start.3) | async-done | bytes 262176 | tf_op jit(solution)/shard_map/all_to_all | solution.py:24
  104.0 0.0 collective-permute-done.7
  104.0 0.8 broadcast_in_dim.18
  104.8 7.9 %all-to-all-start.4 = ((f32[8,64,256]{2,1,0:T(8,128)}), f32[8,64,256]{2,1,0:T(8,128)S(1)}, u32[]{:S(2)}, u32[]{:S(2)}) async-start(f32[8,64,256]{2,1,0:T(8,128)} %broadcast_in_dim.18), calls=%async_computation.4 | async-start | bytes 1048576 | tf_op jit(solution)/shard_map/all_to_all | solution.py:24
  112.7 0.0 collective-permute-start.6
  112.7 0.1 collective-permute-start.5
  112.8 1.9 %collective-permute-start.4 = (f32[32,256]{1,0:T(8,128)S(1)}, f32[32,256]{1,0:T(8,128)S(1)}, u32[]{:S(2)}, u32[]{:S(2)}) collective-permute-start(f32[32,256]{1,0:T(8,128)S(1)} %reduce_sum.19), channel_id=1, source_target_pairs={{0,8},{1,9},{2,10},{3,11},{4,12},{5,13},{6,14},{7,15},{8,16},{9,17... | collective-permute-start | bytes 98312 | tf_op jit(solution)/shard_map/ppermute | solution.py:29
  114.7 1.9 %collective-permute-done.6 = f32[32,256]{1,0:T(8,128)S(1)} collective-permute-done((f32[32,256]{1,0:T(8,128)S(1)}, f32[32,256]{1,0:T(8,128)S(1)}, u32[]{:S(2)}, u32[]{:S(2)}) %collective-permute-start.6) | collective-permute-done | bytes 32800 | tf_op jit(solution)/shard_map/ppermute | solution.py:29
  116.6 1.6 collective-permute-done.5
  118.2 1.1 collective-permute-done.4
  119.3 7.7 %all-to-all-done.4 = f32[8,64,256]{2,1,0:T(8,128)S(1)} async-done(((f32[8,64,256]{2,1,0:T(8,128)}), f32[8,64,256]{2,1,0:T(8,128)S(1)}, u32[]{:S(2)}, u32[]{:S(2)}) %all-to-all-start.4) | async-done | bytes 524320 | tf_op jit(solution)/shard_map/all_to_all | solution.py:24
  127.0 0.9 broadcast_in_dim.19
  127.9 7.9 %all-to-all-start.5 = ((f32[8,96,256]{2,1,0:T(8,128)}), f32[8,96,256]{2,1,0:T(8,128)}, u32[]{:S(2)}, u32[]{:S(2)}) async-start(f32[8,96,256]{2,1,0:T(8,128)} %broadcast_in_dim.19), calls=%async_computation.5 | async-start | bytes 1572864 | tf_op jit(solution)/shard_map/all_to_all | solution.py:24
  135.8 0.0 copy-start.4
  135.8 1.3 collective-permute-start.10
  137.0 1.3 collective-permute-start.9
  138.3 1.3 collective-permute-start.8
  139.7 7.9 %all-to-all-done.5 = f32[8,96,256]{2,1,0:T(8,128)} async-done(((f32[8,96,256]{2,1,0:T(8,128)}), f32[8,96,256]{2,1,0:T(8,128)}, u32[]{:S(2)}, u32[]{:S(2)}) %all-to-all-start.5) | async-done | bytes 786464 | tf_op jit(solution)/shard_map/all_to_all | solution.py:24
  147.6 1.9 %slice.18 = f32[8,64,256]{2,1,0:T(8,128)} slice(f32[8,96,256]{2,1,0:T(8,128)} %all-to-all-done.5), slice={[0:8], [0:64], [0:256]} | slice | bytes 1048576 | tf_op jit(solution)/shard_map/slice | solution.py:146
  149.5 2.0 %copy.13 = f32[512,256]{0,1:T(8,128)} copy(f32[512,256]{1,0:T(8,128)} %bitcast.48) | data formatting | bytes 1048576 | tf_op jit(solution)/shard_map/reshape | solution.py:146
  151.5 1.0 slice.19
  152.5 1.1 convolution_multiply_fusion
  153.6 1.8 %copy.12 = f32[256,256]{0,1:T(8,128)} copy(f32[256,256]{1,0:T(8,128)} %convolution_multiply_fusion) | data formatting | bytes 524288 | tf_op jit(solution)/shard_map/mul | solution.py:149
  155.4 1.9 %fusion.1 = f32[256,512]{1,0:T(8,128)S(1)} fusion(f32[512,256]{0,1:T(8,128)} %copy.13, f32[512,256]{1,0:T(8,128)} %bitcast.45, f32[256,256]{1,0:T(8,128)} %convolution_multiply_fusion, f32[256,256]{0,1:T(8,128)} %copy.12), kind=kOutput, calls=%fused_computation.4 | convolution fusion | flops 201523200 | bytes 2097152 | tf_op jit(solution)/shard_map/dot_general | solution.py:16
  157.3 1.1 pad_maximum_fusion.right
  158.4 0.0 copy-done.4
  158.4 1.9 %fusion.2 = f32[64,256]{1,0:T(8,128)} fusion(f32[64,256]{1,0:T(8,128)S(1)} %collective-permute-done.7, f32[256,256]{1,0:T(8,128)} %convolution_multiply_fusion, f32[64,256]{1,0:T(8,128)S(1)} %copy-done.4), kind=kOutput, calls=%fused_computation.7 | convolution fusion | flops 25182208 | bytes 458752 | tf_op jit(solution)/shard_map/dot_general | solution.py:16
  160.3 0.0 collective-permute-done.10.refs_7_
  160.3 0.0 collective-permute-done.9.refs_6_
  160.3 3.3 %collective-permute-done.8.refs_5_ = f32[512,256]{1,0:T(8,128)} collective-permute-done((f32[512,256]{1,0:T(8,128)S(1)}, f32[512,256]{1,0:T(8,128)}, u32[]{:S(2)}, u32[]{:S(2)}) %collective-permute-start.8) | collective-permute-done | bytes 524320 | tf_op jit(solution)/shard_map/ppermute | solution.py:29
  163.6 0.0 copy-done.1
  163.6 8.3 %shard_map.50 = f32[2048,512]{1,0:T(8,128)} custom-call(s32[1]{0:T(128)} %bitcast.y_ref, f32[2048,512]{1,0:T(8,128)S(1)} %copy-done.1, f32[512,512]{1,0:T(8,128)S(1)} %pad_maximum_fusion.right, f32[512,256]{1,0:T(8,128)S(1)} %bitcast.38, f32[512,256]{1,0:T(8,128)S(1)} %collective-permute-done.refs_1_, f32[512,256]{1,0:T(8,128)S(1)} %collective-permute-done.1.refs_2_, ...), custom_call_target="tpu_custom_call" | custom-call | flops 3221225472 | bytes 12582912 | tf_op jit(solution)/shard_map/pallas_call | solution.py:84
  (7 shorter events, 0.1 us)
Async XLA Ops:
  0.6 65.5 %copy-start = (f32[256,256]{1,0:T(8,128)S(1)}, f32[256,256]{1,0:T(8,128)}, u32[]{:S(2)}) copy-start(f32[256,256]{1,0:T(8,128)} %param.5) | copy-start | bytes 786436
  2.4 25.0 %all-to-all-start = ((f32[8,64,256]{2,1,0:T(8,128)}), f32[8,64,256]{2,1,0:T(8,128)S(1)}, u32[]{:S(2)}, u32[]{:S(2)}) async-start(f32[8,64,256]{2,1,0:T(8,128)} %broadcast_in_dim.15), calls=%async_computation | async-start | bytes 1048576 | tf_op jit(solution)/shard_map/all_to_all | solution.py:24
  10.8 19.7 %collective-permute-start.3 = (f32[64,256]{1,0:T(8,128)}, f32[64,256]{1,0:T(8,128)S(1)}, u32[]{:S(2)}, u32[]{:S(2)}) collective-permute-start(f32[64,256]{1,0:T(8,128)} %param.4), channel_id=1, source_target_pairs={{0,0},{1,32},{2,64},{3,96},{4,128},{5,160},{6,192},{7,224},{8,1},{... | collective-permute-start | bytes 196616 | tf_op jit(solution)/shard_map/ppermute | solution.py:122
  27.4 17.9 %collective-permute-start.2 = (f32[512,256]{1,0:T(8,128)S(1)}, f32[512,256]{1,0:T(8,128)S(1)}, u32[]{:S(2)}, u32[]{:S(2)}) collective-permute-start(f32[512,256]{1,0:T(8,128)S(1)} %bitcast.34), channel_id=1, source_target_pairs={{0,24},{1,25},{2,26},{3,27},{4,28},{5,29},{6,30},{7,31},{8,0},{9,1... | collective-permute-start | bytes 1572872 | tf_op jit(solution)/shard_map/ppermute | solution.py:29
  31.4 13.7 %all-to-all-start.1 = ((f32[8,64,256]{2,1,0:T(8,128)}), f32[8,64,256]{2,1,0:T(8,128)S(1)}, u32[]{:S(2)}, u32[]{:S(2)}) async-start(f32[8,64,256]{2,1,0:T(8,128)} %broadcast_in_dim.16), calls=%async_computation.1 | async-start | bytes 1048576 | tf_op jit(solution)/shard_map/all_to_all | solution.py:24
  36.2 15.3 %collective-permute-start = (f32[512,256]{1,0:T(8,128)S(1)}, f32[512,256]{1,0:T(8,128)S(1)}, u32[]{:S(2)}, u32[]{:S(2)}) collective-permute-start(f32[512,256]{1,0:T(8,128)S(1)} %bitcast.35), channel_id=1, source_target_pairs={{0,8},{1,9},{2,10},{3,11},{4,12},{5,13},{6,14},{7,15},{8,16},{9,17... | collective-permute-start | bytes 1572872 | tf_op jit(solution)/shard_map/ppermute | solution.py:29
  37.1 26.8 %collective-permute-start.1 = (f32[512,256]{1,0:T(8,128)S(1)}, f32[512,256]{1,0:T(8,128)S(1)}, u32[]{:S(2)}, u32[]{:S(2)}) collective-permute-start(f32[512,256]{1,0:T(8,128)S(1)} %bitcast.36), channel_id=1, source_target_pairs={{0,16},{1,17},{2,18},{3,19},{4,20},{5,21},{6,22},{7,23},{8,24},{9,... | collective-permute-start | bytes 1572872 | tf_op jit(solution)/shard_map/ppermute | solution.py:29
  45.1 21.0 %copy-start.2 = (f32[8,64,256]{2,1,0:T(8,128)}, f32[8,64,256]{2,1,0:T(8,128)S(1)}, u32[]{:S(2)}) copy-start(f32[8,64,256]{2,1,0:T(8,128)S(1)} %all-to-all-done.1) | copy-start | bytes 1572868
  45.3 21.2 %copy-start.3 = (f32[512,256]{0,1:T(8,128)}, f32[512,256]{0,1:T(8,128)S(1)}, u32[]{:S(2)}) copy-start(f32[512,256]{0,1:T(8,128)S(1)} %copy.11) | copy-start | bytes 1572868
  85.4 18.5 %all-to-all-start.3 = ((f32[8,32,256]{2,1,0:T(8,128)}), f32[8,32,256]{2,1,0:T(8,128)S(1)}, u32[]{:S(2)}, u32[]{:S(2)}) async-start(f32[8,32,256]{2,1,0:T(8,128)} %broadcast_in_dim.17), calls=%async_computation.3 | async-start | bytes 524288 | tf_op jit(solution)/shard_map/all_to_all | solution.py:24
  92.8 11.2 %collective-permute-start.7 = (f32[64,256]{1,0:T(8,128)S(1)}, f32[64,256]{1,0:T(8,128)S(1)}, u32[]{:S(2)}, u32[]{:S(2)}) collective-permute-start(f32[64,256]{1,0:T(8,128)S(1)} %slice.16), channel_id=1, source_target_pairs={{0,0},{32,1},{64,2},{96,3},{128,4},{160,5},{192,6},{224,7},{1,8},{... | collective-permute-start | bytes 196616 | tf_op jit(solution)/shard_map/ppermute | solution.py:140
  104.8 22.2 %all-to-all-start.4 = ((f32[8,64,256]{2,1,0:T(8,128)}), f32[8,64,256]{2,1,0:T(8,128)S(1)}, u32[]{:S(2)}, u32[]{:S(2)}) async-start(f32[8,64,256]{2,1,0:T(8,128)} %broadcast_in_dim.18), calls=%async_computation.4 | async-start | bytes 1048576 | tf_op jit(solution)/shard_map/all_to_all | solution.py:24
  112.7 3.9 %collective-permute-start.6 = (f32[32,256]{1,0:T(8,128)S(1)}, f32[32,256]{1,0:T(8,128)S(1)}, u32[]{:S(2)}, u32[]{:S(2)}) collective-permute-start(f32[32,256]{1,0:T(8,128)S(1)} %reduce_sum.19), channel_id=1, source_target_pairs={{0,24},{1,25},{2,26},{3,27},{4,28},{5,29},{6,30},{7,31},{8,0},{9,1... | collective-permute-start | bytes 98312 | tf_op jit(solution)/shard_map/ppermute | solution.py:29
  112.7 5.5 %collective-permute-start.5 = (f32[32,256]{1,0:T(8,128)S(1)}, f32[32,256]{1,0:T(8,128)S(1)}, u32[]{:S(2)}, u32[]{:S(2)}) collective-permute-start(f32[32,256]{1,0:T(8,128)S(1)} %reduce_sum.19), channel_id=1, source_target_pairs={{0,16},{1,17},{2,18},{3,19},{4,20},{5,21},{6,22},{7,23},{8,24},{9,... | collective-permute-start | bytes 98312 | tf_op jit(solution)/shard_map/ppermute | solution.py:29
  112.8 6.5 %collective-permute-start.4 = (f32[32,256]{1,0:T(8,128)S(1)}, f32[32,256]{1,0:T(8,128)S(1)}, u32[]{:S(2)}, u32[]{:S(2)}) collective-permute-start(f32[32,256]{1,0:T(8,128)S(1)} %reduce_sum.19), channel_id=1, source_target_pairs={{0,8},{1,9},{2,10},{3,11},{4,12},{5,13},{6,14},{7,15},{8,16},{9,17... | collective-permute-start | bytes 98312 | tf_op jit(solution)/shard_map/ppermute | solution.py:29
  127.9 19.7 %all-to-all-start.5 = ((f32[8,96,256]{2,1,0:T(8,128)}), f32[8,96,256]{2,1,0:T(8,128)}, u32[]{:S(2)}, u32[]{:S(2)}) async-start(f32[8,96,256]{2,1,0:T(8,128)} %broadcast_in_dim.19), calls=%async_computation.5 | async-start | bytes 1572864 | tf_op jit(solution)/shard_map/all_to_all | solution.py:24
  135.8 22.6 %copy-start.4 = (f32[64,256]{1,0:T(8,128)S(1)}, f32[64,256]{1,0:T(8,128)}, u32[]{:S(2)}) copy-start(f32[64,256]{1,0:T(8,128)} %param.4) | copy-start | bytes 196612
  135.8 24.5 %collective-permute-start.10 = (f32[512,256]{1,0:T(8,128)S(1)}, f32[512,256]{1,0:T(8,128)S(1)}, u32[]{:S(2)}, u32[]{:S(2)}) collective-permute-start(f32[512,256]{1,0:T(8,128)S(1)} %bitcast.39), channel_id=1, source_target_pairs={{0,24},{1,25},{2,26},{3,27},{4,28},{5,29},{6,30},{7,31},{8,0},{9,1... | collective-permute-start | bytes 1572872 | tf_op jit(solution)/shard_map/ppermute | solution.py:29
  137.0 23.3 %collective-permute-start.9 = (f32[512,256]{1,0:T(8,128)S(1)}, f32[512,256]{1,0:T(8,128)}, u32[]{:S(2)}, u32[]{:S(2)}) collective-permute-start(f32[512,256]{1,0:T(8,128)S(1)} %bitcast.40), channel_id=1, source_target_pairs={{0,16},{1,17},{2,18},{3,19},{4,20},{5,21},{6,22},{7,23},{8,24},{9,... | collective-permute-start | bytes 1572872 | tf_op jit(solution)/shard_map/ppermute | solution.py:29
  138.3 25.2 %collective-permute-start.8 = (f32[512,256]{1,0:T(8,128)S(1)}, f32[512,256]{1,0:T(8,128)}, u32[]{:S(2)}, u32[]{:S(2)}) collective-permute-start(f32[512,256]{1,0:T(8,128)S(1)} %bitcast.41), channel_id=1, source_target_pairs={{0,8},{1,9},{2,10},{3,11},{4,12},{5,13},{6,14},{7,15},{8,16},{9,17... | collective-permute-start | bytes 1572872 | tf_op jit(solution)/shard_map/ppermute | solution.py:29
  155.4 8.2 %copy-start.1 = (f32[2048,512]{1,0:T(8,128)S(1)}, f32[2048,512]{1,0:T(8,128)}, u32[]{:S(2)}) copy-start(f32[2048,512]{1,0:T(8,128)} %matrix.1) | copy-start | bytes 12582916

commit v3 on v0

v3 whole, which is shorter than its diff:
```python
import jax
import jax.numpy as jnp
from jax import lax
from jax.experimental import pallas as pl
from jax.experimental.pallas import tpu as pltpu
from jax.sharding import PartitionSpec as P

NX, NY, NZ, CORES = 4, 4, 8, 2
Z_GROUPS = [[y * NZ + z for z in range(NZ)] for y in range(NY)]
WHOLE = pl.BlockSpec(memory_space=pltpu.VMEM)
SCALARS = pl.BlockSpec(memory_space=pltpu.SMEM)
FREE = pl.CostEstimate(flops=1, bytes_accessed=1, transcendentals=0)
PARAMS = pltpu.CompilerParams(vmem_limit_bytes=28 << 20)


def after(value, *others):
    return lax.optimization_barrier((value,) + others)[0]


def exact(left, right, contract):
    return lax.dot_general(
        left,
        right,
        (contract, ((), ())),
        precision=lax.Precision.HIGHEST,
        preferred_element_type=jnp.float32,
    )


def halves(value):
    high = value.astype(jnp.bfloat16)
    return high, (value - high.astype(jnp.float32)).astype(jnp.bfloat16)


def three_pass(left, right, contract):
    def one(a, b):
        return lax.dot_general(a, b, (contract, ((), ())), preferred_element_type=jnp.float32)

    return one(left[0], right[1]) + one(left[1], right[0]) + one(left[0], right[0])


def spread(value, groups):
    copies = jnp.broadcast_to(value, (len(groups[0]),) + value.shape)
    return lax.all_to_all(copies, "col", 0, 0, axis_index_groups=groups)


def y_blocks(value):
    def shifted(step):
        perm = [(y * NZ + z, (y + step) % NY * NZ + z) for y in range(NY) for z in range(NZ)]
        return lax.ppermute(value, "col", perm)

    return [value] + [shifted(step) for step in range(1, NY)]


def z_sum(value):
    bit = 1
    while bit < NZ:
        perm = [(y * NZ + z, y * NZ + (z ^ bit)) for y in range(NY) for z in range(NZ)]
        value += lax.ppermute(value, "col", perm)
        bit *= 2
    return value


def x_blocks(value):
    size = NX * CORES

    def shifted(step):
        perm = [(i, (i - CORES * step) % size) for i in range(size)]
        return lax.ppermute(value, "row", perm)

    return [value] + [shifted(step) for step in range(1, NX)]


def other_core(values):
    perm = [(i, i ^ 1) for i in range(NX * CORES)]
    return lax.ppermute(jnp.stack(values), "row", perm)


def assemble(place, mine, other, out):
    for k in range(NX):
        slot = lax.rem(place[0] + k, NX) * CORES
        out[slot + place[1]] = mine[k][...]
        out[slot + 1 - place[1]] = other[k]


def assemble_kernel(place, *refs):
    assemble(place, refs[:NX], refs[NX], refs[NX + 1])


def row_blocks(place, mine, other):
    shape = (NX * CORES,) + mine[0].shape
    return pl.pallas_call(
        assemble_kernel,
        out_shape=jax.ShapeDtypeStruct(shape, mine[0].dtype),
        in_specs=[SCALARS] + [WHOLE] * (NX + 1),
        out_specs=WHOLE,
        cost_estimate=FREE,
        compiler_params=PARAMS,
    )(place, *mine, other)


def product_kernel(y_ref, matrix, factor, col_panel, *refs):
    panels, out, total = refs[:NY], refs[NY], refs[NY + 1]
    step = pl.program_id(0)
    for k in range(NY):

        @pl.when(step == k)
        def _():
            piece = three_pass(halves(panels[k][...]), halves(matrix[...]), ((0,), (0,)))
            if k == 0:
                total[...] = piece
            else:
                total[...] += piece

    @pl.when(step == NY - 1)
    def _():
        count, rows, width = out.shape
        width_rows = width // count
        scaled = exact(total[...], factor[...], ((0,), (0,)))
        inner = exact(col_panel[...], scaled, ((0,), (0,)))
        out[:, : rows - width_rows, :] = scaled.reshape(count, rows - width_rows, width)
        out[:, rows - width_rows :, :] = inner.reshape(count, width_rows, width)


def product(y, matrix, factor, col_panel, panels, count):
    rows, cols = matrix.shape
    block, width = panels[0].shape
    out_shape = (count, (cols + width) // count, width)

    def moving(s, y_ref):
        return (lax.rem(y_ref[0] + (NY - s), NY), 0)

    def fixed(s, y_ref):
        return (0, 0)

    return pl.pallas_call(
        product_kernel,
        out_shape=jax.ShapeDtypeStruct(out_shape, jnp.float32),
        grid_spec=pltpu.PrefetchScalarGridSpec(
            num_scalar_prefetch=1,
            grid=(NY,),
            in_specs=[
                pl.BlockSpec((block, cols), moving),
                pl.BlockSpec((width, width), fixed),
                pl.BlockSpec((cols, width), fixed),
            ]
            + [pl.BlockSpec((block, width), fixed)] * NY,
            out_specs=pl.BlockSpec(out_shape, lambda s, y_ref: (0, 0, 0)),
            scratch_shapes=[pltpu.VMEM((width, cols), jnp.float32)],
        ),
        cost_estimate=FREE,
        compiler_params=PARAMS,
    )(y, matrix, factor, col_panel, *panels)


def middle_kernel(place, factor, panel, home, col_panel, col_scaled, *refs):
    mine, other = refs[:NX], refs[NX]
    left, correction, small = refs[NX + 1 :]
    assemble(place, mine, other, small)
    width = factor.shape[0]
    kernel = 0.5 * exact(factor[...], small[...].reshape(width, width), ((0,), (0,)))
    correction[...] = home[...] - exact(panel[...], kernel, ((1,), (0,)))
    both = kernel + kernel.T
    left[...] = col_scaled[...] - exact(col_panel[...], both, ((1,), (0,)))


def middle(place, factor, panel, home, col_panel, col_scaled, mine, other):
    shapes = [col_scaled.shape, home.shape]
    return pl.pallas_call(
        middle_kernel,
        out_shape=[jax.ShapeDtypeStruct(shape, jnp.float32) for shape in shapes],
        in_specs=[SCALARS] + [WHOLE] * (5 + NX + 1),
        out_specs=[WHOLE] * 2,
        scratch_shapes=[pltpu.VMEM((NX * CORES,) + mine[0].shape, jnp.float32)],
        cost_estimate=FREE,
        compiler_params=PARAMS,
    )(place, factor, panel, home, col_panel, col_scaled, *mine, other)


def update_kernel(y_ref, matrix, right, *refs):
    parts = refs[:NY]
    out, right_high, right_low = refs[NY:]
    step = pl.program_id(0)

    @pl.when(step == 0)
    def _():
        right_high[...], right_low[...] = halves(right[...])

    for k in range(NY):

        @pl.when(step == k)
        def _():
            pair = right_high[...], right_low[...]
            out[...] = matrix[...] - three_pass(halves(parts[k][...]), pair, ((1,), (1,)))


def update(y, matrix, parts, right, in_place):
    rows, cols = matrix.shape
    block, width = parts[0].shape

    def moving(s, y_ref):
        return (lax.rem(y_ref[0] + (NY - s), NY), 0)

    def fixed(s, y_ref):
        return (0, 0)

    return pl.pallas_call(
        update_kernel,
        out_shape=jax.ShapeDtypeStruct((rows, cols), jnp.float32),
        grid_spec=pltpu.PrefetchScalarGridSpec(
            num_scalar_prefetch=1,
            grid=(NY,),
            in_specs=[pl.BlockSpec((block, cols), moving), pl.BlockSpec((cols, width), fixed)]
            + [pl.BlockSpec((block, width), fixed)] * NY,
            out_specs=pl.BlockSpec((block, cols), moving),
            scratch_shapes=[pltpu.VMEM((cols, width), jnp.bfloat16)] * 2,
        ),
        input_output_aliases={1: 0} if in_place else {},
        cost_estimate=FREE,
        compiler_params=PARAMS,
    )(y, matrix, right, *parts)


def per_device(matrix, panel, factor):
    nrows, ncols = lax.axis_size("row"), lax.axis_size("col")
    rows, width = panel.shape
    block = NZ * rows
    row = lax.axis_index("row")
    y = (lax.axis_index("col") // NZ).reshape(1)
    place = jnp.stack([row // CORES, row % CORES])
    total = nrows * ncols
    to_column = [(g, g % nrows * ncols + g // nrows) for g in range(total)]
    to_home = [(b, a) for a, b in to_column]

    mine = x_blocks(lax.ppermute(panel, ("row", "col"), to_column))
    own_panel = spread(panel, Z_GROUPS).reshape(block, width)
    panels = y_blocks(own_panel)
    col_panel = row_blocks(place, mine, other_core(mine)).reshape(nrows * rows, width)

    parts = product(y, matrix, factor, col_panel, panels, nrows)
    parts = jnp.sum(lax.all_to_all(parts, "row", 0, 0), axis=0)
    chunk, inner = parts[:rows], parts[rows:]

    home = lax.ppermute(chunk, ("row", "col"), to_home)
    inner = sum(y_blocks(inner))
    own_scaled = spread(after(home, inner), Z_GROUPS).reshape(block, width)
    mine = x_blocks(after(chunk, home))
    inner = z_sum(inner)
    own_scaled = after(own_scaled, inner)
    col_scaled = row_blocks(place, mine, other_core(mine)).reshape(nrows * rows, width)
    scaleds = y_blocks(own_scaled)

    mine = x_blocks(after(inner, own_scaled))
    left, correction = middle(
        place, factor, panel, home, col_panel, col_scaled, mine, other_core(mine)
    )
    updated = update(y, matrix, panels, left, False)
    return update(y, updated, scaleds, col_panel, True), correction


def solution(mesh):
    in_specs = (P("row", "col"), P(("row", "col"), None), P())
    out_specs = (P("row", "col"), P(("row", "col"), None))
    return jax.shard_map(
        per_device, mesh=mesh, in_specs=in_specs, out_specs=out_specs, check_vma=False
    )
```

time: 803 us -> 169 us (0.21)
  waiting for transfers between devices: 742 us -> 63.7 us
  starting transfers between devices: 0.24 us -> 57.4 us
  matrix products: 27.9 us -> 0 us
  Pallas kernels: 0 us -> 17.4 us
  blocking collectives: 0 us -> 16.6 us
  between operations: 14.2 us -> 0.83 us
    psum x3 -> x0, waiting for transfers between devices: 368 us -> none  [the longest x1 252 us: per_device(): small = lax.psum(mult(panel.T, scaled), ('row', 'col'))]
    unnamed x7 -> x0, waiting for transfers between devices: 219 us -> none
    all_gather x2 -> x0, waiting for transfers between devices: 155 us -> none  [the longest x1 83.5 us: per_device(): row_panel = lax.all_gather(panel, 'col', axis=0, tiled=True)]
    ppermute x0 -> x26, waiting for transfers between devices: none -> 50.6 us  [the longest x3 17.8 us: z_sum(): value += lax.ppermute(value, 'col', perm)]
    ppermute x0 -> x26, starting transfers between devices: none -> 45.4 us  [the longest x9 15.7 us: shifted(): return lax.ppermute(value, 'row', perm)]
    dot_general x7 -> x0, matrix products: 27.9 us -> none  [mult(): jnp.dot(left, right, precision=lax.Precision.HIGHEST, preferred_element_t...]
    pallas_call x0 -> x6, Pallas kernels: none -> 17.4 us  [the longest x2 9.73 us: update(): pl.pallas_call(update_kernel, out_shape=jax.ShapeDtypeStruct((rows, cols)...]
    all_to_all x0 -> x1, blocking collectives: none -> 16.6 us  [per_device(): parts = jnp.sum(lax.all_to_all(parts, 'row', 0, 0), axis=0)]
  transfers between devices with their start and end apart: 6 -> 28, of which waited for: 6 -> 17; matrix products, arithmetic and copies ran while one was open for 2% -> 0% of each run, Pallas kernels for 0% -> 4%
where the time goes in v3:
time: 169 us; the launch traced here: 167 us
  waiting for transfers between devices  63.7 us (38%)
  starting transfers between devices  57.4 us (34%)
  Pallas kernels  17.4 us (10%)
  blocking collectives  16.6 us (10%)
  local copies, waits for them, and re-layouts  9.54 us (6%)
    ppermute x3, waiting for transfers between devices, z_sum(): value += lax.ppermute(value, 'col', perm)  17.8 us
    all_to_all x1, blocking collectives, per_device(): parts = jnp.sum(lax.all_to_all(parts, 'row', 0, 0), axis=0)  16.6 us
    ppermute x9, starting transfers between devices, shifted(): return lax.ppermute(value, 'row', perm)  15.7 us
    ppermute x9, starting transfers between devices, shifted(): return lax.ppermute(value, 'col', perm)  15.2 us
    ppermute x9, waiting for transfers between devices, shifted(): return lax.ppermute(value, 'col', perm)  14 us
    all_to_all x2, waiting for transfers between devices, spread(): return lax.all_to_all(copies, 'col', 0, 0, axis_index_groups=groups)  13.1 us
    all_to_all x2, starting transfers between devices, spread(): return lax.all_to_all(copies, 'col', 0, 0, axis_index_groups=groups)  12 us
    ppermute x9, waiting for transfers between devices, shifted(): return lax.ppermute(value, 'row', perm)  10.7 us
  transfers between devices with their start and end apart: 28, of which 17 were waited for; matrix products, arithmetic and copies ran while one was open for 0% of the time, Pallas kernels for 4%

profile of v3, /device:TPU:2, one launch (start us, length us, event | category | flops | bytes accessed | tf_op | source)
XLA Modules:
  0.0 166.7 jit_solution(808136935169052789)
XLA Ops:
  0.6 1.7 %broadcast_in_dim.6 = f32[8,64,256]{2,1,0:T(8,128)} broadcast(f32[64,256]{1,0:T(8,128)} %panel.1), dimensions={1,2} | broadcast | bytes 589824 | tf_op jit(solution)/shard_map/broadcast_in_dim | solution.py:43
  2.3 8.5 %all-to-all-start = ((f32[8,64,256]{2,1,0:T(8,128)}), f32[8,64,256]{2,1,0:T(8,128)S(1)}, u32[]{:S(2)}, u32[]{:S(2)}) async-start(f32[8,64,256]{2,1,0:T(8,128)} %broadcast_in_dim.6), calls=%async_computation | async-start | bytes 1048576 | tf_op jit(solution)/shard_map/all_to_all | solution.py:44
  10.8 3.4 %collective-permute-start = (f32[64,256]{1,0:T(8,128)}, f32[64,256]{1,0:T(8,128)S(1)}, u32[]{:S(2)}, u32[]{:S(2)}) collective-permute-start(f32[64,256]{1,0:T(8,128)} %panel.1), channel_id=1, source_target_pairs={{0,0},{1,32},{2,64},{3,96},{4,128},{5,160},{6,192},{7,224},{8,1},{... | collective-permute-start | bytes 196616 | tf_op jit(solution)/shard_map/ppermute | solution.py:235
  14.2 13.1 %all-to-all-done = f32[8,64,256]{2,1,0:T(8,128)S(1)} async-done(((f32[8,64,256]{2,1,0:T(8,128)}), f32[8,64,256]{2,1,0:T(8,128)S(1)}, u32[]{:S(2)}, u32[]{:S(2)}) %all-to-all-start) | async-done | bytes 524320 | tf_op jit(solution)/shard_map/all_to_all | solution.py:44
  27.3 3.2 %collective-permute-start.7 = (f32[512,256]{1,0:T(8,128)S(1)}, f32[512,256]{1,0:T(8,128)S(1)}, u32[]{:S(2)}, u32[]{:S(2)}) collective-permute-start(f32[512,256]{1,0:T(8,128)S(1)} %bitcast.22), channel_id=1, source_target_pairs={{0,24},{1,25},{2,26},{3,27},{4,28},{5,29},{6,30},{7,31},{8,0},{9,1... | collective-permute-start | bytes 1572872 | tf_op jit(solution)/shard_map/ppermute | solution.py:50
  30.5 2.9 %collective-permute-start.6 = (f32[512,256]{1,0:T(8,128)S(1)}, f32[512,256]{1,0:T(8,128)S(1)}, u32[]{:S(2)}, u32[]{:S(2)}) collective-permute-start(f32[512,256]{1,0:T(8,128)S(1)} %bitcast.23), channel_id=1, source_target_pairs={{0,16},{1,17},{2,18},{3,19},{4,20},{5,21},{6,22},{7,23},{8,24},{9,... | collective-permute-start | bytes 1572872 | tf_op jit(solution)/shard_map/ppermute | solution.py:50
  33.4 1.0 collective-permute-start.5
  34.4 0.0 collective-permute-done.refs_0_
  34.4 1.5 collective-permute-start.3
  35.9 1.1 collective-permute-start.2
  37.0 2.0 %collective-permute-done.3.refs_3_ = f32[64,256]{1,0:T(8,128)S(1)} collective-permute-done((f32[64,256]{1,0:T(8,128)S(1)}, f32[64,256]{1,0:T(8,128)S(1)}, u32[]{:S(2)}, u32[]{:S(2)}) %collective-permute-start.3) | collective-permute-done | bytes 65568 | tf_op jit(solution)/shard_map/ppermute | solution.py:69
  39.0 1.8 %collective-permute-start.1 = (f32[64,256]{1,0:T(8,128)S(1)}, f32[64,256]{1,0:T(8,128)S(1)}, u32[]{:S(2)}, u32[]{:S(2)}) collective-permute-start(f32[64,256]{1,0:T(8,128)S(1)} %collective-permute-done.refs_0_), channel_id=1, source_target_pairs={{0,192},{32,224},{64,0},{96,32},{128,64},{160,96},{192,128},{224,1... | collective-permute-start | bytes 196616 | tf_op jit(solution)/shard_map/ppermute | solution.py:69
  40.8 0.9 collective-permute-done.2.refs_2_
  41.7 1.5 collective-permute-done.1.refs_1_
  43.3 0.1 collective-permute-start.4
  43.4 0.1 pad_add_fusion.place
  43.5 1.4 collective-permute-done.4.refs_4_
  44.9 0.6 shard_map.50
  45.5 1.4 collective-permute-done.6.refs_2_
  46.9 9.8 %collective-permute-done.5.refs_1_ = f32[512,256]{1,0:T(8,128)S(1)} collective-permute-done((f32[512,256]{1,0:T(8,128)S(1)}, f32[512,256]{1,0:T(8,128)S(1)}, u32[]{:S(2)}, u32[]{:S(2)}) %collective-permute-start.5) | collective-permute-done | bytes 524320 | tf_op jit(solution)/shard_map/ppermute | solution.py:50
  56.6 2.2 %copy-done = f32[2048,512]{1,0:T(8,128)S(1)} copy-done((f32[2048,512]{1,0:T(8,128)S(1)}, f32[2048,512]{1,0:T(8,128)}, u32[]{:S(2)}) %copy-start) | copy-done | bytes 4194328
  58.8 0.9 copy-done.2
  59.8 4.4 %shard_map.51 = f32[8,96,256]{2,1,0:T(8,128)S(1)} custom-call(s32[1]{0:T(128)} %bitcast.y_ref, f32[2048,512]{1,0:T(8,128)S(1)} %copy-done, f32[256,256]{1,0:T(8,128)S(1)} %copy-done.2, f32[512,256]{1,0:T(8,128)S(1)} %bitcast.19, f32[512,256]{1,0:T(8,128)S(1)} %bitcast.25, f32[512,256]{1,0:T(8,128)S(1)} %collective-permute-done.5.refs_1_, ...), custom_call_target="tpu_custom_call" | custom-call | flops 1 | bytes 1 | tf_op jit(solution)/shard_map/pallas_call | solution.py:136
  64.1 0.0 copy-start.3
  64.1 16.6 %all_to_all.15 = f32[8,96,256]{2,1,0:T(8,128)} all-to-all(f32[8,96,256]{2,1,0:T(8,128)S(1)} %shard_map.51), channel_id=1, replica_groups=mesh['row'=8,'col'=32] {'row'}, dimensions={0} | all-to-all | bytes 1572864 | tf_op jit(solution)/shard_map/all_to_all | solution.py:241
  80.8 1.2 reduce_sum.9
  82.0 2.5 %collective-permute-start.14 = (f32[32,256]{1,0:T(8,128)S(1)}, f32[32,256]{1,0:T(8,128)S(1)}, u32[]{:S(2)}, u32[]{:S(2)}) collective-permute-start(f32[32,256]{1,0:T(8,128)S(1)} %slice.9), channel_id=1, source_target_pairs={{0,16},{1,17},{2,18},{3,19},{4,20},{5,21},{6,22},{7,23},{8,24},{9,... | collective-permute-start | bytes 98312 | tf_op jit(solution)/shard_map/ppermute | solution.py:50
  84.5 1.7 %collective-permute-start.15 = (f32[32,256]{1,0:T(8,128)S(1)}, f32[32,256]{1,0:T(8,128)S(1)}, u32[]{:S(2)}, u32[]{:S(2)}) collective-permute-start(f32[32,256]{1,0:T(8,128)S(1)} %slice.9), channel_id=1, source_target_pairs={{0,24},{1,25},{2,26},{3,27},{4,28},{5,29},{6,30},{7,31},{8,0},{9,1... | collective-permute-start | bytes 98312 | tf_op jit(solution)/shard_map/ppermute | solution.py:50
  86.2 0.3 collective-permute-start.13
  86.5 1.9 %collective-permute-start.8 = (f32[64,256]{1,0:T(8,128)S(1)}, f32[64,256]{1,0:T(8,128)S(1)}, u32[]{:S(2)}, u32[]{:S(2)}) collective-permute-start(f32[64,256]{1,0:T(8,128)S(1)} %slice.8.refs_0_), channel_id=1, source_target_pairs={{0,0},{32,1},{64,2},{96,3},{128,4},{160,5},{192,6},{224,7},{1,8},{... | collective-permute-start | bytes 196616 | tf_op jit(solution)/shard_map/ppermute | solution.py:244
  88.4 0.0 collective-permute-done.14
  88.5 2.9 %collective-permute-done.13 = f32[32,256]{1,0:T(8,128)S(1)} collective-permute-done((f32[32,256]{1,0:T(8,128)S(1)}, f32[32,256]{1,0:T(8,128)S(1)}, u32[]{:S(2)}, u32[]{:S(2)}) %collective-permute-start.13) | collective-permute-done | bytes 32800 | tf_op jit(solution)/shard_map/ppermute | solution.py:50
  91.3 5.9 %collective-permute-done.8.home = f32[64,256]{1,0:T(8,128)S(1)} collective-permute-done((f32[64,256]{1,0:T(8,128)S(1)}, f32[64,256]{1,0:T(8,128)S(1)}, u32[]{:S(2)}, u32[]{:S(2)}) %collective-permute-start.8) | collective-permute-done | bytes 65568 | tf_op jit(solution)/shard_map/ppermute | solution.py:244
  97.2 0.8 broadcast_in_dim.7
  98.1 3.5 %all-to-all-start.2 = ((f32[8,64,256]{2,1,0:T(8,128)}), f32[8,64,256]{2,1,0:T(8,128)S(1)}, u32[]{:S(2)}, u32[]{:S(2)}) async-start(f32[8,64,256]{2,1,0:T(8,128)} %broadcast_in_dim.7), calls=%async_computation.2 | async-start | bytes 1048576 | tf_op jit(solution)/shard_map/all_to_all | solution.py:44
  101.6 1.9 %collective-permute-start.16 = (f32[32,256]{1,0:T(8,128)S(1)}, f32[32,256]{1,0:T(8,128)S(1)}, u32[]{:S(2)}, u32[]{:S(2)}) collective-permute-start(f32[32,256]{1,0:T(8,128)S(1)} %add_add_fusion), channel_id=1, source_target_pairs={{0,1},{1,0},{2,3},{3,2},{4,5},{5,4},{6,7},{7,6},{8,9},{9,8},{10,11... | collective-permute-start | bytes 98312 | tf_op jit(solution)/shard_map/ppermute | solution.py:59
  103.5 12.0 %collective-permute-done.16 = f32[32,256]{1,0:T(8,128)S(1)} collective-permute-done((f32[32,256]{1,0:T(8,128)S(1)}, f32[32,256]{1,0:T(8,128)S(1)}, u32[]{:S(2)}, u32[]{:S(2)}) %collective-permute-start.16) | collective-permute-done | bytes 32800 | tf_op jit(solution)/shard_map/ppermute | solution.py:59
  115.5 1.8 %collective-permute-start.17 = (f32[32,256]{1,0:T(8,128)S(1)}, f32[32,256]{1,0:T(8,128)S(1)}, u32[]{:S(2)}, u32[]{:S(2)}) collective-permute-start(f32[32,256]{1,0:T(8,128)S(1)} %add.28), channel_id=1, source_target_pairs={{0,2},{1,3},{2,0},{3,1},{4,6},{5,7},{6,4},{7,5},{8,10},{9,11},{10,... | collective-permute-start | bytes 98312 | tf_op jit(solution)/shard_map/ppermute | solution.py:59
  117.4 3.0 %collective-permute-done.17 = f32[32,256]{1,0:T(8,128)S(1)} collective-permute-done((f32[32,256]{1,0:T(8,128)S(1)}, f32[32,256]{1,0:T(8,128)S(1)}, u32[]{:S(2)}, u32[]{:S(2)}) %collective-permute-start.17) | collective-permute-done | bytes 32800 | tf_op jit(solution)/shard_map/ppermute | solution.py:59
  120.3 5.0 %collective-permute-start.18 = (f32[32,256]{1,0:T(8,128)S(1)}, f32[32,256]{1,0:T(8,128)S(1)}, u32[]{:S(2)}, u32[]{:S(2)}) collective-permute-start(f32[32,256]{1,0:T(8,128)S(1)} %add.29), channel_id=1, source_target_pairs={{0,4},{1,5},{2,6},{3,7},{4,0},{5,1},{6,2},{7,3},{8,12},{9,13},{10,... | collective-permute-start | bytes 98312 | tf_op jit(solution)/shard_map/ppermute | solution.py:59
  125.4 2.8 %collective-permute-done.18 = f32[32,256]{1,0:T(8,128)S(1)} collective-permute-done((f32[32,256]{1,0:T(8,128)S(1)}, f32[32,256]{1,0:T(8,128)S(1)}, u32[]{:S(2)}, u32[]{:S(2)}) %collective-permute-start.18) | collective-permute-done | bytes 32800 | tf_op jit(solution)/shard_map/ppermute | solution.py:59
  128.2 2.6 %collective-permute-start.25 = (f32[512,256]{1,0:T(8,128)S(1)}, f32[512,256]{1,0:T(8,128)S(1)}, u32[]{:S(2)}, u32[]{:S(2)}) collective-permute-start(f32[512,256]{1,0:T(8,128)S(1)} %bitcast.27), channel_id=1, source_target_pairs={{0,24},{1,25},{2,26},{3,27},{4,28},{5,29},{6,30},{7,31},{8,0},{9,1... | collective-permute-start | bytes 1572872 | tf_op jit(solution)/shard_map/ppermute | solution.py:50
  130.8 1.0 collective-permute-start.23
  131.8 2.1 %collective-permute-start.11 = (f32[64,256]{1,0:T(8,128)S(1)}, f32[64,256]{1,0:T(8,128)S(1)}, u32[]{:S(2)}, u32[]{:S(2)}) collective-permute-start(f32[64,256]{1,0:T(8,128)S(1)} %slice.8.refs_0_), channel_id=1, source_target_pairs={{0,64},{32,96},{64,128},{96,160},{128,192},{160,224},{192,0},{224,... | collective-permute-start | bytes 196616 | tf_op jit(solution)/shard_map/ppermute | solution.py:69
  133.9 1.2 collective-permute-start.10
  135.1 1.6 collective-permute-done.11.refs_3_
  136.7 1.8 %collective-permute-start.9 = (f32[64,256]{1,0:T(8,128)S(1)}, f32[64,256]{1,0:T(8,128)S(1)}, u32[]{:S(2)}, u32[]{:S(2)}) collective-permute-start(f32[64,256]{1,0:T(8,128)S(1)} %slice.8.refs_0_), channel_id=1, source_target_pairs={{0,192},{32,224},{64,0},{96,32},{128,64},{160,96},{192,128},{224,1... | collective-permute-start | bytes 196616 | tf_op jit(solution)/shard_map/ppermute | solution.py:69
  138.5 1.1 collective-permute-done.10.refs_2_
  139.6 1.9 %collective-permute-start.21 = (f32[32,256]{1,0:T(8,128)S(1)}, f32[32,256]{1,0:T(8,128)S(1)}, u32[]{:S(2)}, u32[]{:S(2)}) collective-permute-start(f32[32,256]{1,0:T(8,128)S(1)} %add.30.refs_0_), channel_id=1, source_target_pairs={{0,64},{32,96},{64,128},{96,160},{128,192},{160,224},{192,0},{224,... | collective-permute-start | bytes 98312 | tf_op jit(solution)/shard_map/ppermute | solution.py:69
  141.5 0.0 collective-permute-done.9.refs_1_
  141.5 3.9 %collective-permute-start.20 = (f32[32,256]{1,0:T(8,128)S(1)}, f32[32,256]{1,0:T(8,128)S(1)}, u32[]{:S(2)}, u32[]{:S(2)}) collective-permute-start(f32[32,256]{1,0:T(8,128)S(1)} %add.30.refs_0_), channel_id=1, source_target_pairs={{0,128},{32,160},{64,192},{96,224},{128,0},{160,32},{192,64},{224,... | collective-permute-start | bytes 98312 | tf_op jit(solution)/shard_map/ppermute | solution.py:69
  145.4 0.3 collective-permute-start.19
  145.8 1.5 collective-permute-done.20.refs_2_
  147.3 0.0 collective-permute-start.12
  147.3 2.0 %collective-permute-done.19.refs_1_ = f32[32,256]{1,0:T(8,128)S(1)} collective-permute-done((f32[32,256]{1,0:T(8,128)S(1)}, f32[32,256]{1,0:T(8,128)S(1)}, u32[]{:S(2)}, u32[]{:S(2)}) %collective-permute-start.19) | collective-permute-done | bytes 32800 | tf_op jit(solution)/shard_map/ppermute | solution.py:69
  149.4 0.3 collective-permute-start.22
  149.7 0.6 shard_map.52
  150.3 0.7 collective-permute-done.22.refs_4_
  151.0 0.8 copy-done.4
  151.9 0.8 copy-done.6
  152.7 2.1 %shard_map.53 = (f32[512,256]{1,0:T(8,128)S(1)}, f32[64,256]{1,0:T(8,128)}) custom-call(s32[2]{0:T(128)S(1)} %pad_add_fusion.place, f32[256,256]{1,0:T(8,128)S(1)} %copy-done.3, f32[64,256]{1,0:T(8,128)S(1)} %copy-done.4, f32[64,256]{1,0:T(8,128)S(1)} %copy-done.6, f32[512,256]{1,0:T(8,128)S(1)} %bitcast.20, f32[512,256]{1,0:T(8,128)S(1)} %bitcast.31, ...), custom_call_target="tpu_custom_call" | custom-call | flops 1 | bytes 1 | tf_op jit(solution)/shard_map/pallas_call | solution.py:169
  154.8 2.2 %copy-done.1 = f32[2048,512]{1,0:T(8,128)S(1)} copy-done((f32[2048,512]{1,0:T(8,128)S(1)}, f32[2048,512]{1,0:T(8,128)}, u32[]{:S(2)}) %copy-start.1) | copy-done | bytes 4194328
  157.0 3.9 %shard_map.54.matrix = f32[2048,512]{1,0:T(8,128)} custom-call(s32[1]{0:T(128)} %bitcast.y_ref, f32[2048,512]{1,0:T(8,128)S(1)} %copy-done.1, f32[512,256]{1,0:T(8,128)S(1)} %get-tuple-element.12.right, f32[512,256]{1,0:T(8,128)S(1)} %bitcast.26, f32[512,256]{1,0:T(8,128)S(1)} %collective-permute-done.5.refs_1_, ...), custom_call_target="tpu_custom_call" | custom-call | flops 1 | bytes 1 | tf_op jit(solution)/shard_map/pallas_call | solution.py:207
  160.9 5.9 %shard_map.55 = f32[2048,512]{1,0:T(8,128)} custom-call(s32[1]{0:T(128)} %bitcast.y_ref, f32[2048,512]{1,0:T(8,128)} %shard_map.54.matrix, f32[512,256]{1,0:T(8,128)S(1)} %bitcast.21, f32[512,256]{1,0:T(8,128)S(1)} %bitcast.30, f32[512,256]{1,0:T(8,128)S(1)} %collective-permute-done.23.refs_1_, ...), custom_call_target="tpu_custom_call", output_to_operand_aliasing={{}: (1, {})} | custom-call | flops 1 | bytes 1 | tf_op jit(solution)/shard_map/pallas_call | solution.py:207
  (26 shorter events, 0.1 us)
Async XLA Ops:
  2.3 25.0 %all-to-all-start = ((f32[8,64,256]{2,1,0:T(8,128)}), f32[8,64,256]{2,1,0:T(8,128)S(1)}, u32[]{:S(2)}, u32[]{:S(2)}) async-start(f32[8,64,256]{2,1,0:T(8,128)} %broadcast_in_dim.6), calls=%async_computation | async-start | bytes 1048576 | tf_op jit(solution)/shard_map/all_to_all | solution.py:44
  10.8 23.6 %collective-permute-start = (f32[64,256]{1,0:T(8,128)}, f32[64,256]{1,0:T(8,128)S(1)}, u32[]{:S(2)}, u32[]{:S(2)}) collective-permute-start(f32[64,256]{1,0:T(8,128)} %panel.1), channel_id=1, source_target_pairs={{0,0},{1,32},{2,64},{3,96},{4,128},{5,160},{6,192},{7,224},{8,1},{... | collective-permute-start | bytes 196616 | tf_op jit(solution)/shard_map/ppermute | solution.py:235
  27.3 18.2 %collective-permute-start.7 = (f32[512,256]{1,0:T(8,128)S(1)}, f32[512,256]{1,0:T(8,128)S(1)}, u32[]{:S(2)}, u32[]{:S(2)}) collective-permute-start(f32[512,256]{1,0:T(8,128)S(1)} %bitcast.22), channel_id=1, source_target_pairs={{0,24},{1,25},{2,26},{3,27},{4,28},{5,29},{6,30},{7,31},{8,0},{9,1... | collective-permute-start | bytes 1572872 | tf_op jit(solution)/shard_map/ppermute | solution.py:50
  30.5 16.4 %collective-permute-start.6 = (f32[512,256]{1,0:T(8,128)S(1)}, f32[512,256]{1,0:T(8,128)S(1)}, u32[]{:S(2)}, u32[]{:S(2)}) collective-permute-start(f32[512,256]{1,0:T(8,128)S(1)} %bitcast.23), channel_id=1, source_target_pairs={{0,16},{1,17},{2,18},{3,19},{4,20},{5,21},{6,22},{7,23},{8,24},{9,... | collective-permute-start | bytes 1572872 | tf_op jit(solution)/shard_map/ppermute | solution.py:50
  33.4 23.2 %collective-permute-start.5 = (f32[512,256]{1,0:T(8,128)S(1)}, f32[512,256]{1,0:T(8,128)S(1)}, u32[]{:S(2)}, u32[]{:S(2)}) collective-permute-start(f32[512,256]{1,0:T(8,128)S(1)} %bitcast.24), channel_id=1, source_target_pairs={{0,8},{1,9},{2,10},{3,11},{4,12},{5,13},{6,14},{7,15},{8,16},{9,17... | collective-permute-start | bytes 1572872 | tf_op jit(solution)/shard_map/ppermute | solution.py:50
  34.4 4.6 %collective-permute-start.3 = (f32[64,256]{1,0:T(8,128)S(1)}, f32[64,256]{1,0:T(8,128)S(1)}, u32[]{:S(2)}, u32[]{:S(2)}) collective-permute-start(f32[64,256]{1,0:T(8,128)S(1)} %collective-permute-done.refs_0_), channel_id=1, source_target_pairs={{0,64},{32,96},{64,128},{96,160},{128,192},{160,224},{192,0},{224,... | collective-permute-start | bytes 196616 | tf_op jit(solution)/shard_map/ppermute | solution.py:69
  35.9 5.8 %collective-permute-start.2 = (f32[64,256]{1,0:T(8,128)S(1)}, f32[64,256]{1,0:T(8,128)S(1)}, u32[]{:S(2)}, u32[]{:S(2)}) collective-permute-start(f32[64,256]{1,0:T(8,128)S(1)} %collective-permute-done.refs_0_), channel_id=1, source_target_pairs={{0,128},{32,160},{64,192},{96,224},{128,0},{160,32},{192,64},{224,... | collective-permute-start | bytes 196616 | tf_op jit(solution)/shard_map/ppermute | solution.py:69
  39.0 4.3 %collective-permute-start.1 = (f32[64,256]{1,0:T(8,128)S(1)}, f32[64,256]{1,0:T(8,128)S(1)}, u32[]{:S(2)}, u32[]{:S(2)}) collective-permute-start(f32[64,256]{1,0:T(8,128)S(1)} %collective-permute-done.refs_0_), channel_id=1, source_target_pairs={{0,192},{32,224},{64,0},{96,32},{128,64},{160,96},{192,128},{224,1... | collective-permute-start | bytes 196616 | tf_op jit(solution)/shard_map/ppermute | solution.py:69
  43.3 1.6 collective-permute-start.4
  56.6 2.2 %copy-start = (f32[2048,512]{1,0:T(8,128)S(1)}, f32[2048,512]{1,0:T(8,128)}, u32[]{:S(2)}) copy-start(f32[2048,512]{1,0:T(8,128)} %matrix.3) | copy-start | bytes 12582916
  58.8 0.9 copy-start.2
  64.1 86.9 %copy-start.3 = (f32[256,256]{1,0:T(8,128)S(1)}, f32[256,256]{1,0:T(8,128)}, u32[]{:S(2)}) copy-start(f32[256,256]{1,0:T(8,128)} %factor.3) | copy-start | bytes 786436
  82.0 6.4 %collective-permute-start.14 = (f32[32,256]{1,0:T(8,128)S(1)}, f32[32,256]{1,0:T(8,128)S(1)}, u32[]{:S(2)}, u32[]{:S(2)}) collective-permute-start(f32[32,256]{1,0:T(8,128)S(1)} %slice.9), channel_id=1, source_target_pairs={{0,16},{1,17},{2,18},{3,19},{4,20},{5,21},{6,22},{7,23},{8,24},{9,... | collective-permute-start | bytes 98312 | tf_op jit(solution)/shard_map/ppermute | solution.py:50
  84.5 4.0 %collective-permute-start.15 = (f32[32,256]{1,0:T(8,128)S(1)}, f32[32,256]{1,0:T(8,128)S(1)}, u32[]{:S(2)}, u32[]{:S(2)}) collective-permute-start(f32[32,256]{1,0:T(8,128)S(1)} %slice.9), channel_id=1, source_target_pairs={{0,24},{1,25},{2,26},{3,27},{4,28},{5,29},{6,30},{7,31},{8,0},{9,1... | collective-permute-start | bytes 98312 | tf_op jit(solution)/shard_map/ppermute | solution.py:50
  86.2 5.1 %collective-permute-start.13 = (f32[32,256]{1,0:T(8,128)S(1)}, f32[32,256]{1,0:T(8,128)S(1)}, u32[]{:S(2)}, u32[]{:S(2)}) collective-permute-start(f32[32,256]{1,0:T(8,128)S(1)} %slice.9), channel_id=1, source_target_pairs={{0,8},{1,9},{2,10},{3,11},{4,12},{5,13},{6,14},{7,15},{8,16},{9,17... | collective-permute-start | bytes 98312 | tf_op jit(solution)/shard_map/ppermute | solution.py:50
  86.5 10.7 %collective-permute-start.8 = (f32[64,256]{1,0:T(8,128)S(1)}, f32[64,256]{1,0:T(8,128)S(1)}, u32[]{:S(2)}, u32[]{:S(2)}) collective-permute-start(f32[64,256]{1,0:T(8,128)S(1)} %slice.8.refs_0_), channel_id=1, source_target_pairs={{0,0},{32,1},{64,2},{96,3},{128,4},{160,5},{192,6},{224,7},{1,8},{... | collective-permute-start | bytes 196616 | tf_op jit(solution)/shard_map/ppermute | solution.py:244
  97.2 0.8 copy-start.5
  98.1 30.1 %all-to-all-start.2 = ((f32[8,64,256]{2,1,0:T(8,128)}), f32[8,64,256]{2,1,0:T(8,128)S(1)}, u32[]{:S(2)}, u32[]{:S(2)}) async-start(f32[8,64,256]{2,1,0:T(8,128)} %broadcast_in_dim.7), calls=%async_computation.2 | async-start | bytes 1048576 | tf_op jit(solution)/shard_map/all_to_all | solution.py:44
  101.6 14.0 %collective-permute-start.16 = (f32[32,256]{1,0:T(8,128)S(1)}, f32[32,256]{1,0:T(8,128)S(1)}, u32[]{:S(2)}, u32[]{:S(2)}) collective-permute-start(f32[32,256]{1,0:T(8,128)S(1)} %add_add_fusion), channel_id=1, source_target_pairs={{0,1},{1,0},{2,3},{3,2},{4,5},{5,4},{6,7},{7,6},{8,9},{9,8},{10,11... | collective-permute-start | bytes 98312 | tf_op jit(solution)/shard_map/ppermute | solution.py:59
  115.5 4.8 %collective-permute-start.17 = (f32[32,256]{1,0:T(8,128)S(1)}, f32[32,256]{1,0:T(8,128)S(1)}, u32[]{:S(2)}, u32[]{:S(2)}) collective-permute-start(f32[32,256]{1,0:T(8,128)S(1)} %add.28), channel_id=1, source_target_pairs={{0,2},{1,3},{2,0},{3,1},{4,6},{5,7},{6,4},{7,5},{8,10},{9,11},{10,... | collective-permute-start | bytes 98312 | tf_op jit(solution)/shard_map/ppermute | solution.py:59
  120.3 7.8 %collective-permute-start.18 = (f32[32,256]{1,0:T(8,128)S(1)}, f32[32,256]{1,0:T(8,128)S(1)}, u32[]{:S(2)}, u32[]{:S(2)}) collective-permute-start(f32[32,256]{1,0:T(8,128)S(1)} %add.29), channel_id=1, source_target_pairs={{0,4},{1,5},{2,6},{3,7},{4,0},{5,1},{6,2},{7,3},{8,12},{9,13},{10,... | collective-permute-start | bytes 98312 | tf_op jit(solution)/shard_map/ppermute | solution.py:59
  128.2 32.7 %collective-permute-start.25 = (f32[512,256]{1,0:T(8,128)S(1)}, f32[512,256]{1,0:T(8,128)S(1)}, u32[]{:S(2)}, u32[]{:S(2)}) collective-permute-start(f32[512,256]{1,0:T(8,128)S(1)} %bitcast.27), channel_id=1, source_target_pairs={{0,24},{1,25},{2,26},{3,27},{4,28},{5,29},{6,30},{7,31},{8,0},{9,1... | collective-permute-start | bytes 1572872 | tf_op jit(solution)/shard_map/ppermute | solution.py:50
  130.8 30.0 %collective-permute-start.24 = (f32[512,256]{1,0:T(8,128)S(1)}, f32[512,256]{1,0:T(8,128)S(1)}, u32[]{:S(2)}, u32[]{:S(2)}) collective-permute-start(f32[512,256]{1,0:T(8,128)S(1)} %bitcast.28), channel_id=1, source_target_pairs={{0,16},{1,17},{2,18},{3,19},{4,20},{5,21},{6,22},{7,23},{8,24},{9,... | collective-permute-start | bytes 1572872 | tf_op jit(solution)/shard_map/ppermute | solution.py:50
  130.8 30.0 %collective-permute-start.23 = (f32[512,256]{1,0:T(8,128)S(1)}, f32[512,256]{1,0:T(8,128)S(1)}, u32[]{:S(2)}, u32[]{:S(2)}) collective-permute-start(f32[512,256]{1,0:T(8,128)S(1)} %bitcast.29), channel_id=1, source_target_pairs={{0,8},{1,9},{2,10},{3,11},{4,12},{5,13},{6,14},{7,15},{8,16},{9,17... | collective-permute-start | bytes 1572872 | tf_op jit(solution)/shard_map/ppermute | solution.py:50
  131.8 4.9 %collective-permute-start.11 = (f32[64,256]{1,0:T(8,128)S(1)}, f32[64,256]{1,0:T(8,128)S(1)}, u32[]{:S(2)}, u32[]{:S(2)}) collective-permute-start(f32[64,256]{1,0:T(8,128)S(1)} %slice.8.refs_0_), channel_id=1, source_target_pairs={{0,64},{32,96},{64,128},{96,160},{128,192},{160,224},{192,0},{224,... | collective-permute-start | bytes 196616 | tf_op jit(solution)/shard_map/ppermute | solution.py:69
  133.9 5.8 %collective-permute-start.10 = (f32[64,256]{1,0:T(8,128)S(1)}, f32[64,256]{1,0:T(8,128)S(1)}, u32[]{:S(2)}, u32[]{:S(2)}) collective-permute-start(f32[64,256]{1,0:T(8,128)S(1)} %slice.8.refs_0_), channel_id=1, source_target_pairs={{0,128},{32,160},{64,192},{96,224},{128,0},{160,32},{192,64},{224,... | collective-permute-start | bytes 196616 | tf_op jit(solution)/shard_map/ppermute | solution.py:69
  136.7 4.8 %collective-permute-start.9 = (f32[64,256]{1,0:T(8,128)S(1)}, f32[64,256]{1,0:T(8,128)S(1)}, u32[]{:S(2)}, u32[]{:S(2)}) collective-permute-start(f32[64,256]{1,0:T(8,128)S(1)} %slice.8.refs_0_), channel_id=1, source_target_pairs={{0,192},{32,224},{64,0},{96,32},{128,64},{160,96},{192,128},{224,1... | collective-permute-start | bytes 196616 | tf_op jit(solution)/shard_map/ppermute | solution.py:69
  139.6 5.8 %collective-permute-start.21 = (f32[32,256]{1,0:T(8,128)S(1)}, f32[32,256]{1,0:T(8,128)S(1)}, u32[]{:S(2)}, u32[]{:S(2)}) collective-permute-start(f32[32,256]{1,0:T(8,128)S(1)} %add.30.refs_0_), channel_id=1, source_target_pairs={{0,64},{32,96},{64,128},{96,160},{128,192},{160,224},{192,0},{224,... | collective-permute-start | bytes 98312 | tf_op jit(solution)/shard_map/ppermute | solution.py:69
  141.5 5.8 %collective-permute-start.20 = (f32[32,256]{1,0:T(8,128)S(1)}, f32[32,256]{1,0:T(8,128)S(1)}, u32[]{:S(2)}, u32[]{:S(2)}) collective-permute-start(f32[32,256]{1,0:T(8,128)S(1)} %add.30.refs_0_), channel_id=1, source_target_pairs={{0,128},{32,160},{64,192},{96,224},{128,0},{160,32},{192,64},{224,... | collective-permute-start | bytes 98312 | tf_op jit(solution)/shard_map/ppermute | solution.py:69
  145.4 3.9 %collective-permute-start.19 = (f32[32,256]{1,0:T(8,128)S(1)}, f32[32,256]{1,0:T(8,128)S(1)}, u32[]{:S(2)}, u32[]{:S(2)}) collective-permute-start(f32[32,256]{1,0:T(8,128)S(1)} %add.30.refs_0_), channel_id=1, source_target_pairs={{0,192},{32,224},{64,0},{96,32},{128,64},{160,96},{192,128},{224,1... | collective-permute-start | bytes 98312 | tf_op jit(solution)/shard_map/ppermute | solution.py:69
  147.3 2.4 %collective-permute-start.12 = (f32[4,64,256]{2,1,0:T(8,128)S(1)}, f32[4,64,256]{2,1,0:T(8,128)S(1)}, u32[]{:S(2)}, u32[]{:S(2)}) collective-permute-start(f32[4,64,256]{2,1,0:T(8,128)S(1)} %pad_maximum_fusion.1), channel_id=1, source_target_pairs={{0,32},{32,0},{64,96},{96,64},{128,160},{160,128},{192,224},{224,1... | collective-permute-start | bytes 786440 | tf_op jit(solution)/shard_map/ppermute | solution.py:76
  149.4 1.7 collective-permute-start.22
  151.0 0.8 copy-start.4
  151.9 0.8 copy-start.6
  154.8 2.2 %copy-start.1 = (f32[2048,512]{1,0:T(8,128)S(1)}, f32[2048,512]{1,0:T(8,128)}, u32[]{:S(2)}) copy-start(f32[2048,512]{1,0:T(8,128)} %matrix.3) | copy-start | bytes 12582916

commit v4 on v3

v4 whole, which is shorter than its diff:
```python
import jax
import jax.numpy as jnp
from jax import lax
from jax.experimental import pallas as pl
from jax.experimental.pallas import tpu as pltpu
from jax.sharding import PartitionSpec as P

NX, NY, NZ, CORES = 4, 4, 8, 2
Z_GROUPS = [[y * NZ + z for z in range(NZ)] for y in range(NY)]
WHOLE = pl.BlockSpec(memory_space=pltpu.VMEM)
SCALARS = pl.BlockSpec(memory_space=pltpu.SMEM)
TILE = 256
FREE = pl.CostEstimate(flops=1, bytes_accessed=1, transcendentals=0)
PARAMS = pltpu.CompilerParams(vmem_limit_bytes=28 << 20)
LARGE = pltpu.CompilerParams(vmem_limit_bytes=48 << 20)


def after(value, *others):
    return lax.optimization_barrier((value,) + others)[0]


def exact(left, right, contract):
    return lax.dot_general(
        left,
        right,
        (contract, ((), ())),
        precision=lax.Precision.HIGHEST,
        preferred_element_type=jnp.float32,
    )


def halves(value):
    high = value.astype(jnp.bfloat16)
    return high, (value - high.astype(jnp.float32)).astype(jnp.bfloat16)


def three_terms(value, axis, right):
    high, low = halves(value)
    return jnp.concatenate([low, high, high] if right else [high, low, high], axis=axis)


def contracted(left, right, axis):
    contract = (((axis,), (axis,)), ((), ()))
    return lax.dot_general(left, right, contract, preferred_element_type=jnp.float32)


def spread(value, groups):
    copies = jnp.broadcast_to(value, (len(groups[0]),) + value.shape)
    return lax.all_to_all(copies, "col", 0, 0, axis_index_groups=groups)


def y_shift(value, step):
    perm = [(y * NZ + z, (y + step) % NY * NZ + z) for y in range(NY) for z in range(NZ)]
    return lax.ppermute(value, "col", perm)


def y_sum(value):
    return value + y_shift(value, 1) + y_shift(value, 2) + y_shift(value, 3)


def y_halves(value):
    first, second = value[:TILE], value[TILE:]
    up_first, down_second = y_shift(first, 1), y_shift(second, -1)
    up_second, down_first = y_shift(second, 1), y_shift(first, -1)
    far_first, far_second = y_shift(up_first, 1), y_shift(down_second, -1)
    return [first, second, up_first, up_second, far_first, far_second, down_first, down_second]


def z_step(value, bit):
    perm = [(y * NZ + z, y * NZ + (z ^ bit)) for y in range(NY) for z in range(NZ)]
    return value + lax.ppermute(value, "col", perm)


def x_blocks(value):
    size = NX * CORES

    def shifted(step):
        perm = [(i, (i - CORES * step) % size) for i in range(size)]
        return lax.ppermute(value, "row", perm)

    return [value] + [shifted(step) for step in range(1, NX)]


def other_core(values):
    perm = [(i, i ^ 1) for i in range(NX * CORES)]
    return lax.ppermute(jnp.stack(values), "row", perm)


def assemble(place, mine, other, out):
    for k in range(NX):
        slot = lax.rem(place[0] + k, NX) * CORES
        out[slot + place[1]] = mine[k][...]
        out[slot + 1 - place[1]] = other[k]


def assemble_kernel(place, *refs):
    assemble(place, refs[:NX], refs[NX], refs[NX + 1])


def row_blocks(place, mine, other):
    shape = (NX * CORES,) + mine[0].shape
    return pl.pallas_call(
        assemble_kernel,
        out_shape=jax.ShapeDtypeStruct(shape, mine[0].dtype),
        in_specs=[SCALARS] + [WHOLE] * (NX + 1),
        out_specs=WHOLE,
        cost_estimate=FREE,
        compiler_params=PARAMS,
    )(place, *mine, other)


def tile_of(step, y_ref):
    return lax.rem(y_ref[0] + (NY - step // 2), NY) * 2 + step % 2


def product_kernel(y_ref, matrix, factor, col_panel, *refs):
    parts, out, total = refs[: 2 * NY], refs[2 * NY], refs[2 * NY + 1]
    step = pl.program_id(0)
    for k in range(2 * NY):

        @pl.when(step == k)
        def _():
            left = three_terms(parts[k][...], 0, False)
            piece = contracted(left, three_terms(matrix[...], 0, True), 0)
            if k == 0:
                total[...] = piece
            else:
                total[...] += piece

    @pl.when(step == 2 * NY - 1)
    def _():
        count, rows, width = out.shape
        width_rows = width // count
        scaled = exact(total[...], factor[...], ((0,), (0,)))
        inner = exact(col_panel[...], scaled, ((0,), (0,)))
        out[:, : rows - width_rows, :] = scaled.reshape(count, rows - width_rows, width)
        out[:, rows - width_rows :, :] = inner.reshape(count, width_rows, width)


def product(y, matrix, factor, col_panel, parts, count):
    cols, width = matrix.shape[1], factor.shape[0]
    out_shape = (count, (cols + width) // count, width)

    def moving(step, y_ref):
        return (tile_of(step, y_ref), 0)

    def fixed(step, y_ref):
        return (0, 0)

    return pl.pallas_call(
        product_kernel,
        out_shape=jax.ShapeDtypeStruct(out_shape, jnp.float32),
        grid_spec=pltpu.PrefetchScalarGridSpec(
            num_scalar_prefetch=1,
            grid=(2 * NY,),
            in_specs=[
                pl.BlockSpec((TILE, cols), moving),
                pl.BlockSpec((width, width), fixed),
                pl.BlockSpec((cols, width), fixed),
            ]
            + [pl.BlockSpec((TILE, width), fixed)] * (2 * NY),
            out_specs=pl.BlockSpec(out_shape, lambda step, y_ref: (0, 0, 0)),
            scratch_shapes=[pltpu.VMEM((width, cols), jnp.float32)],
        ),
        cost_estimate=FREE,
        compiler_params=LARGE,
    )(y, matrix, factor, col_panel, *parts)


def middle_kernel(place, factor, panel, home, col_panel, col_scaled, *refs):
    mine, other = refs[:NX], refs[NX]
    left, correction, small = refs[NX + 1 :]
    assemble(place, mine, other, small)
    width = factor.shape[0]
    kernel = 0.5 * exact(factor[...], small[...].reshape(width, width), ((0,), (0,)))
    correction[...] = home[...] - exact(panel[...], kernel, ((1,), (0,)))
    both = kernel + kernel.T
    left[...] = col_scaled[...] - exact(col_panel[...], both, ((1,), (0,)))


def middle(place, factor, panel, home, col_panel, col_scaled, mine, other):
    shapes = [col_scaled.shape, home.shape]
    operands = [factor, panel, home, col_panel, col_scaled, *mine, other]

    def whole(shape):
        return pl.BlockSpec(shape, lambda step: (0,) * len(shape))

    return pl.pallas_call(
        middle_kernel,
        out_shape=[jax.ShapeDtypeStruct(shape, jnp.float32) for shape in shapes],
        grid=(1,),
        in_specs=[SCALARS] + [whole(operand.shape) for operand in operands],
        out_specs=[whole(shape) for shape in shapes],
        scratch_shapes=[pltpu.VMEM((NX * CORES,) + mine[0].shape, jnp.float32)],
        cost_estimate=FREE,
        compiler_params=PARAMS,
    )(place, *operands)


def update_kernel(y_ref, matrix, right, *refs):
    parts, (out, terms) = refs[:-2], refs[-2:]
    step = pl.program_id(0)

    @pl.when(step == 0)
    def _():
        terms[...] = three_terms(right[...], 1, True)

    for k in range(len(parts)):

        @pl.when(step == k)
        def _():
            left = three_terms(parts[k][...], 1, False)
            out[...] = matrix[...] - contracted(left, terms[...], 1)


def update(y, matrix, parts, right, first, in_place):
    rows, cols = matrix.shape
    width = right.shape[1]

    def moving(step, y_ref):
        return (tile_of(step + first, y_ref), 0)

    def fixed(step, y_ref):
        return (0, 0)

    return pl.pallas_call(
        update_kernel,
        out_shape=jax.ShapeDtypeStruct((rows, cols), jnp.float32),
        grid_spec=pltpu.PrefetchScalarGridSpec(
            num_scalar_prefetch=1,
            grid=(len(parts),),
            in_specs=[pl.BlockSpec((TILE, cols), moving), pl.BlockSpec((cols, width), fixed)]
            + [pl.BlockSpec((TILE, width), fixed)] * len(parts),
            out_specs=pl.BlockSpec((TILE, cols), moving),
            scratch_shapes=[pltpu.VMEM((cols, 3 * width), jnp.bfloat16)],
        ),
        input_output_aliases={1: 0} if in_place else {},
        cost_estimate=FREE,
        compiler_params=LARGE,
    )(y, matrix, right, *parts)


def per_device(matrix, panel, factor):
    nrows, ncols = lax.axis_size("row"), lax.axis_size("col")
    rows, width = panel.shape
    block = NZ * rows
    row = lax.axis_index("row")
    y = (lax.axis_index("col") // NZ).reshape(1)
    place = jnp.stack([row // CORES, row % CORES])
    total = nrows * ncols
    to_column = [(g, g % nrows * ncols + g // nrows) for g in range(total)]
    to_home = [(b, a) for a, b in to_column]

    moved = lax.ppermute(panel, ("row", "col"), to_column)
    own_panel = after(spread(panel, Z_GROUPS).reshape(block, width), moved)
    panels = y_halves(own_panel)
    mine = x_blocks(after(moved, own_panel))
    col_panel = row_blocks(place, mine, other_core(mine)).reshape(nrows * rows, width)

    parts = product(y, matrix, factor, col_panel, panels, nrows)
    parts = jnp.sum(lax.all_to_all(parts, "row", 0, 0), axis=0)
    chunk, inner = parts[:rows], parts[rows:]

    home = lax.ppermute(chunk, ("row", "col"), to_home)
    inner = z_step(z_step(inner, 1), 2)
    own_scaled = spread(after(home, inner), Z_GROUPS).reshape(block, width)
    inner = y_sum(z_step(inner, 4))
    mine = x_blocks(after(chunk, home))
    own_scaled = after(own_scaled, inner, *mine)
    scaleds = y_halves(own_scaled)
    col_scaled = row_blocks(place, mine, other_core(mine)).reshape(nrows * rows, width)

    mine = x_blocks(after(inner, own_scaled))
    left, correction = middle(
        place, factor, panel, home, col_panel, col_scaled, mine, other_core(mine)
    )
    updated = update(y, matrix, panels, left, 0, False)
    updated = update(y, updated, scaleds[:2], col_panel, 0, True)
    return update(y, updated, scaleds[2:], col_panel, 2, True), correction


def solution(mesh):
    in_specs = (P("row", "col"), P(("row", "col"), None), P())
    out_specs = (P("row", "col"), P(("row", "col"), None))
    return jax.shard_map(
        per_device, mesh=mesh, in_specs=in_specs, out_specs=out_specs, check_vma=False
    )
```

time: 169 us -> 174 us (1.030)
  waiting for transfers between devices: 63.7 us -> 47.2 us
  starting transfers between devices: 57.4 us -> 72.2 us
  Pallas kernels: 17.4 us -> 28.7 us
  local copies, waits for them, and re-layouts: 9.54 us -> 3.68 us
    all_to_all x2, waiting for transfers between devices: 13.1 us -> 2.86 us  [spread(): return lax.all_to_all(copies, 'col', 0, 0, axis_index_groups=groups)]
    ppermute x13 -> x19, starting transfers between devices: 27.4 us -> 35.6 us  [the longest x15 23.6 us: y_shift(): return lax.ppermute(value, 'col', perm)]
    pallas_call x2 -> x3, Pallas kernels: 9.73 us -> 17.1 us  [update(): pl.pallas_call(update_kernel, out_shape=jax.ShapeDtypeStruct((rows, cols)...]
    unnamed x14 -> x4, local copies, waits for them, and re-layouts: 7.01 us -> 0.01 us
    ppermute x1, waiting for transfers between devices: 5.9 us -> 0.01 us  [per_device(): home = lax.ppermute(chunk, ('row', 'col'), to_home)]
    ppermute x13 -> x19, waiting for transfers between devices: 31.8 us -> 37.5 us  [the longest x3 17.1 us: z_step(): return value + lax.ppermute(value, 'col', perm)]
    ppermute x1, starting transfers between devices: 1.91 us -> 7.12 us  [per_device(): home = lax.ppermute(chunk, ('row', 'col'), to_home)]
    ppermute x9, waiting for transfers between devices: 10.7 us -> 6.1 us  [shifted(): return lax.ppermute(value, 'row', perm)]
  transfers between devices with their start and end apart: 28 -> 34, of which waited for: 17 -> 12; matrix products, arithmetic and copies ran while one was open for 0% -> 0% of each run, Pallas kernels for 4% -> 8%
where the time goes in v4:
time: 174 us; the launch traced here: 172 us
  starting transfers between devices  72.2 us (41%)
  waiting for transfers between devices  47.2 us (27%)
  Pallas kernels  28.7 us (16%)
  blocking collectives  17.5 us (10%)
  local copies, waits for them, and re-layouts  3.68 us (2%)
    ppermute x15, starting transfers between devices, y_shift(): return lax.ppermute(value, 'col', perm)  23.6 us
    all_to_all x1, blocking collectives, per_device(): parts = jnp.sum(lax.all_to_all(parts, 'row', 0, 0), axis=0)  17.5 us
    ppermute x3, waiting for transfers between devices, z_step(): return value + lax.ppermute(value, 'col', perm)  17.1 us
    pallas_call x3, Pallas kernels, update(): pl.pallas_call(update_kernel, out_shape=jax.ShapeDtypeStruct((rows, cols)...  17.1 us
    ppermute x9, starting transfers between devices, shifted(): return lax.ppermute(value, 'row', perm)  16.4 us
    all_to_all x2, starting transfers between devices, spread(): return lax.all_to_all(copies, 'col', 0, 0, axis_index_groups=groups)  12.8 us
    ppermute x1, waiting for transfers between devices, per_device(): moved = lax.ppermute(panel, ('row', 'col'), to_column)  10.2 us
    ppermute x15, waiting for transfers between devices, y_shift(): return lax.ppermute(value, 'col', perm)  10.1 us
  transfers between devices with their start and end apart: 34, of which 12 were waited for; matrix products, arithmetic and copies ran while one was open for 0% of the time, Pallas kernels for 8%

profile of v4, /device:TPU:2, one launch (start us, length us, event | category | flops | bytes accessed | tf_op | source)
XLA Modules:
  0.0 171.5 jit_solution(14988936572161928694)
XLA Ops:
  0.6 1.7 %broadcast_in_dim.6 = f32[8,64,256]{2,1,0:T(8,128)} broadcast(f32[64,256]{1,0:T(8,128)} %panel.1), dimensions={1,2} | broadcast | bytes 589824 | tf_op jit(solution)/shard_map/broadcast_in_dim | solution.py:48
  2.4 8.5 %all-to-all-start = ((f32[8,64,256]{2,1,0:T(8,128)}), f32[8,64,256]{2,1,0:T(8,128)S(1)}, u32[]{:S(2)}, u32[]{:S(2)}) async-start(f32[8,64,256]{2,1,0:T(8,128)} %broadcast_in_dim.6), calls=%async_computation | async-start | bytes 1048576 | tf_op jit(solution)/shard_map/all_to_all | solution.py:49
  10.8 3.4 %collective-permute-start = (f32[64,256]{1,0:T(8,128)}, f32[64,256]{1,0:T(8,128)S(1)}, u32[]{:S(2)}, u32[]{:S(2)}) collective-permute-start(f32[64,256]{1,0:T(8,128)} %panel.1), channel_id=1, source_target_pairs={{0,0},{1,32},{2,64},{3,96},{4,128},{5,160},{6,192},{7,224},{8,1},{... | collective-permute-start | bytes 196616 | tf_op jit(solution)/shard_map/ppermute | solution.py:254
  14.3 10.2 %collective-permute-done.refs_0_ = f32[64,256]{1,0:T(8,128)S(1)} collective-permute-done((f32[64,256]{1,0:T(8,128)}, f32[64,256]{1,0:T(8,128)S(1)}, u32[]{:S(2)}, u32[]{:S(2)}) %collective-permute-start) | collective-permute-done | bytes 65568 | tf_op jit(solution)/shard_map/ppermute | solution.py:254
  24.5 2.9 %all-to-all-done = f32[8,64,256]{2,1,0:T(8,128)S(1)} async-done(((f32[8,64,256]{2,1,0:T(8,128)}), f32[8,64,256]{2,1,0:T(8,128)S(1)}, u32[]{:S(2)}, u32[]{:S(2)}) %all-to-all-start) | async-done | bytes 524320 | tf_op jit(solution)/shard_map/all_to_all | solution.py:49
  27.4 4.1 %collective-permute-start.5 = (f32[256,256]{1,0:T(8,128)S(1)}, f32[256,256]{1,0:T(8,128)S(1)}, u32[]{:S(2)}, u32[]{:S(2)}) collective-permute-start(f32[256,256]{1,0:T(8,128)S(1)} %get-tuple-element.21.refs_0_), channel_id=1, source_target_pairs={{0,8},{1,9},{2,10},{3,11},{4,12},{5,13},{6,14},{7,15},{8,16},{9,17... | collective-permute-start | bytes 786440 | tf_op jit(solution)/shard_map/ppermute | solution.py:54
  31.5 0.0 collective-permute-start.8
  31.5 0.5 collective-permute-start.1
  32.0 3.0 %collective-permute-start.2 = (f32[64,256]{1,0:T(8,128)S(1)}, f32[64,256]{1,0:T(8,128)S(1)}, u32[]{:S(2)}, u32[]{:S(2)}) collective-permute-start(f32[64,256]{1,0:T(8,128)S(1)} %collective-permute-done.refs_0_), channel_id=1, source_target_pairs={{0,128},{32,160},{64,192},{96,224},{128,0},{160,32},{192,64},{224,... | collective-permute-start | bytes 196616 | tf_op jit(solution)/shard_map/ppermute | solution.py:79
  35.0 1.8 %collective-permute-start.3 = (f32[64,256]{1,0:T(8,128)S(1)}, f32[64,256]{1,0:T(8,128)S(1)}, u32[]{:S(2)}, u32[]{:S(2)}) collective-permute-start(f32[64,256]{1,0:T(8,128)S(1)} %collective-permute-done.refs_0_), channel_id=1, source_target_pairs={{0,64},{32,96},{64,128},{96,160},{128,192},{160,224},{192,0},{224,... | collective-permute-start | bytes 196616 | tf_op jit(solution)/shard_map/ppermute | solution.py:79
  36.8 2.0 %collective-permute-start.10 = (f32[256,256]{1,0:T(8,128)S(1)}, f32[256,256]{1,0:T(8,128)S(1)}, u32[]{:S(2)}, u32[]{:S(2)}) collective-permute-start(f32[256,256]{1,0:T(8,128)S(1)} %get-tuple-element.21.refs_0_), channel_id=1, source_target_pairs={{0,24},{1,25},{2,26},{3,27},{4,28},{5,29},{6,30},{7,31},{8,0},{9,1... | collective-permute-start | bytes 786440 | tf_op jit(solution)/shard_map/ppermute | solution.py:54
  38.8 0.0 collective-permute-done.2.refs_2_
  38.8 0.5 collective-permute-done.3.refs_3_
  39.3 0.1 collective-permute-start.4
  39.4 1.6 collective-permute-start.6
  41.0 1.6 collective-permute-start.7
  42.5 1.7 collective-permute-start.9
  44.2 0.1 pad_add_fusion.place
  44.3 0.6 shard_map.50
  44.9 0.0 collective-permute-done.10.refs_6_
  44.9 4.9 %collective-permute-done.6.refs_3_ = f32[256,256]{1,0:T(8,128)S(1)} collective-permute-done((f32[256,256]{1,0:T(8,128)S(1)}, f32[256,256]{1,0:T(8,128)S(1)}, u32[]{:S(2)}, u32[]{:S(2)}) %collective-permute-start.6) | collective-permute-done | bytes 262176 | tf_op jit(solution)/shard_map/ppermute | solution.py:54
  49.8 5.2 %collective-permute-done.7.refs_4_ = f32[256,256]{1,0:T(8,128)S(1)} collective-permute-done((f32[256,256]{1,0:T(8,128)S(1)}, f32[256,256]{1,0:T(8,128)S(1)}, u32[]{:S(2)}, u32[]{:S(2)}) %collective-permute-start.7) | collective-permute-done | bytes 262176 | tf_op jit(solution)/shard_map/ppermute | solution.py:54
  54.9 0.0 collective-permute-done.9.refs_5_
  54.9 8.4 %shard_map.51 = f32[8,96,256]{2,1,0:T(8,128)S(1)} custom-call(s32[1]{0:T(128)} %bitcast.y_ref, f32[2048,512]{1,0:T(8,128)} %matrix.3, f32[256,256]{1,0:T(8,128)S(1)} %copy-done, f32[512,256]{1,0:T(8,128)S(1)} %bitcast.19, f32[256,256]{1,0:T(8,128)S(1)} %get-tuple-element.21.refs_0_, f32[256,256]{1,0:T(8,128)S(1)} %get-tuple-element.20.refs_1_, ...), custom_call_target="tpu_custom_call" | custom-call | flops 1 | bytes 1 | tf_op jit(solution)/shard_map/pallas_call | solution.py:150
  63.3 0.0 copy-start.1
  63.3 17.5 %all_to_all.15 = f32[8,96,256]{2,1,0:T(8,128)} all-to-all(f32[8,96,256]{2,1,0:T(8,128)S(1)} %shard_map.51), channel_id=1, replica_groups=mesh['row'=8,'col'=32] {'row'}, dimensions={0} | all-to-all | bytes 1572864 | tf_op jit(solution)/shard_map/all_to_all | solution.py:261
  80.9 1.2 reduce_sum.9
  82.1 2.4 %collective-permute-start.16 = (f32[32,256]{1,0:T(8,128)S(1)}, f32[32,256]{1,0:T(8,128)S(1)}, u32[]{:S(2)}, u32[]{:S(2)}) collective-permute-start(f32[32,256]{1,0:T(8,128)S(1)} %slice.25), channel_id=1, source_target_pairs={{0,1},{1,0},{2,3},{3,2},{4,5},{5,4},{6,7},{7,6},{8,9},{9,8},{10,11... | collective-permute-start | bytes 98312 | tf_op jit(solution)/shard_map/ppermute | solution.py:71
  84.5 7.1 %collective-permute-start.11 = (f32[64,256]{1,0:T(8,128)S(1)}, f32[64,256]{1,0:T(8,128)S(1)}, u32[]{:S(2)}, u32[]{:S(2)}) collective-permute-start(f32[64,256]{1,0:T(8,128)S(1)} %slice.24.refs_0_), channel_id=1, source_target_pairs={{0,0},{32,1},{64,2},{96,3},{128,4},{160,5},{192,6},{224,7},{1,8},{... | collective-permute-start | bytes 196616 | tf_op jit(solution)/shard_map/ppermute | solution.py:264
  91.6 0.0 collective-permute-done.16
  91.7 0.3 collective-permute-start.17
  91.9 4.8 %collective-permute-done.17 = f32[32,256]{1,0:T(8,128)S(1)} collective-permute-done((f32[32,256]{1,0:T(8,128)S(1)}, f32[32,256]{1,0:T(8,128)S(1)}, u32[]{:S(2)}, u32[]{:S(2)}) %collective-permute-start.17) | collective-permute-done | bytes 32800 | tf_op jit(solution)/shard_map/ppermute | solution.py:71
  96.8 0.0 collective-permute-done.11.home
  96.8 0.8 broadcast_in_dim.7
  97.6 4.3 %all-to-all-start.2 = ((f32[8,64,256]{2,1,0:T(8,128)}), f32[8,64,256]{2,1,0:T(8,128)}, u32[]{:S(2)}, u32[]{:S(2)}) async-start(f32[8,64,256]{2,1,0:T(8,128)} %broadcast_in_dim.7), calls=%async_computation.2 | async-start | bytes 1048576 | tf_op jit(solution)/shard_map/all_to_all | solution.py:49
  101.9 5.9 %collective-permute-start.18 = (f32[32,256]{1,0:T(8,128)S(1)}, f32[32,256]{1,0:T(8,128)S(1)}, u32[]{:S(2)}, u32[]{:S(2)}) collective-permute-start(f32[32,256]{1,0:T(8,128)S(1)} %add.26), channel_id=1, source_target_pairs={{0,4},{1,5},{2,6},{3,7},{4,0},{5,1},{6,2},{7,3},{8,12},{9,13},{10,... | collective-permute-start | bytes 98312 | tf_op jit(solution)/shard_map/ppermute | solution.py:71
  107.8 12.3 %collective-permute-done.18 = f32[32,256]{1,0:T(8,128)S(1)} collective-permute-done((f32[32,256]{1,0:T(8,128)S(1)}, f32[32,256]{1,0:T(8,128)S(1)}, u32[]{:S(2)}, u32[]{:S(2)}) %collective-permute-start.18) | collective-permute-done | bytes 32800 | tf_op jit(solution)/shard_map/ppermute | solution.py:71
  120.2 3.4 %collective-permute-start.20 = (f32[32,256]{1,0:T(8,128)S(1)}, f32[32,256]{1,0:T(8,128)S(1)}, u32[]{:S(2)}, u32[]{:S(2)}) collective-permute-start(f32[32,256]{1,0:T(8,128)S(1)} %add.27), channel_id=1, source_target_pairs={{0,16},{1,17},{2,18},{3,19},{4,20},{5,21},{6,22},{7,23},{8,24},{9,... | collective-permute-start | bytes 98312 | tf_op jit(solution)/shard_map/ppermute | solution.py:54
  123.6 0.0 collective-permute-start.21
  123.6 2.7 %collective-permute-start.12 = (f32[64,256]{1,0:T(8,128)S(1)}, f32[64,256]{1,0:T(8,128)S(1)}, u32[]{:S(2)}, u32[]{:S(2)}) collective-permute-start(f32[64,256]{1,0:T(8,128)S(1)} %slice.24.refs_0_), channel_id=1, source_target_pairs={{0,192},{32,224},{64,0},{96,32},{128,64},{160,96},{192,128},{224,1... | collective-permute-start | bytes 196616 | tf_op jit(solution)/shard_map/ppermute | solution.py:79
  126.3 0.8 collective-permute-start.13
  127.2 2.5 %collective-permute-start.14 = (f32[64,256]{1,0:T(8,128)S(1)}, f32[64,256]{1,0:T(8,128)S(1)}, u32[]{:S(2)}, u32[]{:S(2)}) collective-permute-start(f32[64,256]{1,0:T(8,128)S(1)} %slice.24.refs_0_), channel_id=1, source_target_pairs={{0,64},{32,96},{64,128},{96,160},{128,192},{160,224},{192,0},{224,... | collective-permute-start | bytes 196616 | tf_op jit(solution)/shard_map/ppermute | solution.py:79
  129.6 0.0 collective-permute-done.20
  129.7 0.0 collective-permute-done.21
  129.7 2.4 %collective-permute-done.13.refs_2_ = f32[64,256]{1,0:T(8,128)S(1)} collective-permute-done((f32[64,256]{1,0:T(8,128)S(1)}, f32[64,256]{1,0:T(8,128)S(1)}, u32[]{:S(2)}, u32[]{:S(2)}) %collective-permute-start.13) | collective-permute-done | bytes 65568 | tf_op jit(solution)/shard_map/ppermute | solution.py:79
  132.1 1.1 fusion
  133.2 0.6 collective-permute-start.26
  133.8 2.7 %collective-permute-start.29 = (f32[256,256]{1,0:T(8,128)S(1)}, f32[256,256]{1,0:T(8,128)S(1)}, u32[]{:S(2)}, u32[]{:S(2)}) collective-permute-start(f32[256,256]{1,0:T(8,128)S(1)} %get-tuple-element.18.refs_1_), channel_id=1, source_target_pairs={{0,24},{1,25},{2,26},{3,27},{4,28},{5,29},{6,30},{7,31},{8,0},{9,1... | collective-permute-start | bytes 786440 | tf_op jit(solution)/shard_map/ppermute | solution.py:54
  136.5 0.1 collective-permute-start.15
  136.6 2.3 %collective-permute-start.22 = (f32[32,256]{1,0:T(8,128)S(1)}, f32[32,256]{1,0:T(8,128)S(1)}, u32[]{:S(2)}, u32[]{:S(2)}) collective-permute-start(f32[32,256]{1,0:T(8,128)S(1)} %add_add_fusion.refs_0_), channel_id=1, source_target_pairs={{0,192},{32,224},{64,0},{96,32},{128,64},{160,96},{192,128},{224,1... | collective-permute-start | bytes 98312 | tf_op jit(solution)/shard_map/ppermute | solution.py:79
  139.0 1.0 collective-permute-start.23
  140.0 0.7 collective-permute-done.22.refs_1_
  140.6 1.8 %collective-permute-start.24 = (f32[32,256]{1,0:T(8,128)S(1)}, f32[32,256]{1,0:T(8,128)S(1)}, u32[]{:S(2)}, u32[]{:S(2)}) collective-permute-start(f32[32,256]{1,0:T(8,128)S(1)} %add_add_fusion.refs_0_), channel_id=1, source_target_pairs={{0,64},{32,96},{64,128},{96,160},{128,192},{160,224},{192,0},{224,... | collective-permute-start | bytes 98312 | tf_op jit(solution)/shard_map/ppermute | solution.py:79
  142.4 2.0 %collective-permute-done.23.refs_2_ = f32[32,256]{1,0:T(8,128)S(1)} collective-permute-done((f32[32,256]{1,0:T(8,128)S(1)}, f32[32,256]{1,0:T(8,128)S(1)}, u32[]{:S(2)}, u32[]{:S(2)}) %collective-permute-start.23) | collective-permute-done | bytes 32800 | tf_op jit(solution)/shard_map/ppermute | solution.py:79
  144.4 0.5 collective-permute-done.24.refs_3_
  144.9 2.7 %collective-permute-start.31 = (f32[256,256]{1,0:T(8,128)S(1)}, f32[256,256]{1,0:T(8,128)S(1)}, u32[]{:S(2)}, u32[]{:S(2)}) collective-permute-start(f32[256,256]{1,0:T(8,128)S(1)} %get-tuple-element.19.refs_0_), channel_id=1, source_target_pairs={{0,24},{1,25},{2,26},{3,27},{4,28},{5,29},{6,30},{7,31},{8,0},{9,1... | collective-permute-start | bytes 786440 | tf_op jit(solution)/shard_map/ppermute | solution.py:54
  147.6 3.2 %collective-permute-start.30 = (f32[256,256]{1,0:T(8,128)S(1)}, f32[256,256]{1,0:T(8,128)S(1)}, u32[]{:S(2)}, u32[]{:S(2)}) collective-permute-start(f32[256,256]{1,0:T(8,128)S(1)} %collective-permute-done.29.refs_5_), channel_id=1, source_target_pairs={{0,24},{1,25},{2,26},{3,27},{4,28},{5,29},{6,30},{7,31},{8,0},{9,1... | collective-permute-start | bytes 786440 | tf_op jit(solution)/shard_map/ppermute | solution.py:54
  150.9 0.1 collective-permute-start.25
  151.0 0.6 shard_map.52
  151.6 0.7 collective-permute-done.25.refs_4_
  152.3 2.1 %shard_map.53 = (f32[512,256]{1,0:T(8,128)S(1)}, f32[64,256]{1,0:T(8,128)}) custom-call(s32[2]{0:T(128)S(1)} %pad_add_fusion.place, f32[256,256]{1,0:T(8,128)S(1)} %copy-done, f32[64,256]{1,0:T(8,128)S(1)} %copy-done.1, f32[64,256]{1,0:T(8,128)S(1)} %collective-permute-done.11.home, f32[512,256]{1,0:T(8,128)S(1)} %bitcast.20, f32[512,256]{1,0:T(8,128)S(1)} %bitcast.23, ...), custom_call_target="tpu_custom_call" | custom-call | flops 1 | bytes 1 | tf_op jit(solution)/shard_map/pallas_call | solution.py:188
  154.4 8.0 %shard_map.54.matrix = f32[2048,512]{1,0:T(8,128)} custom-call(s32[1]{0:T(128)} %bitcast.y_ref, f32[2048,512]{1,0:T(8,128)} %matrix.3, f32[512,256]{1,0:T(8,128)S(1)} %get-tuple-element.16.right, f32[256,256]{1,0:T(8,128)S(1)} %get-tuple-element.21.refs_0_, f32[256,256]{1,0:T(8,128)S(1)} %get-tuple-element.20.refs_1_, ...), custom_call_target="tpu_custom_call" | custom-call | flops 1 | bytes 1 | tf_op jit(solution)/shard_map/pallas_call | solution.py:226
  162.4 2.7 %shard_map.55.matrix = f32[2048,512]{1,0:T(8,128)} custom-call(s32[1]{0:T(128)} %bitcast.y_ref, f32[2048,512]{1,0:T(8,128)} %shard_map.54.matrix, f32[512,256]{1,0:T(8,128)S(1)} %bitcast.21, f32[256,256]{1,0:T(8,128)S(1)} %get-tuple-element.19.refs_0_, f32[256,256]{1,0:T(8,128)S(1)} %get-tuple-element.18.refs_1_), custom_call_target="tpu_custom_call", output_to_operand_aliasing={{}: (1, {})} | custom-call | flops 1 | bytes 1 | tf_op jit(solution)/shard_map/pallas_call | solution.py:226
  165.2 6.3 %shard_map.56 = f32[2048,512]{1,0:T(8,128)} custom-call(s32[1]{0:T(128)} %bitcast.y_ref, f32[2048,512]{1,0:T(8,128)} %shard_map.55.matrix, f32[512,256]{1,0:T(8,128)S(1)} %bitcast.22, f32[256,256]{1,0:T(8,128)S(1)} %collective-permute-done.26.refs_0_, f32[256,256]{1,0:T(8,128)S(1)} %collective-permute-done.27.refs_1_, ...), custom_call_target="tpu_custom_call", output_to_operand_aliasing={{}: (1, {})} | custom-call | flops 1 | bytes 1 | tf_op jit(solution)/shard_map/pallas_call | solution.py:226
  (31 shorter events, 0.2 us)
Async XLA Ops:
  0.6 54.3 %copy-start = (f32[256,256]{1,0:T(8,128)S(1)}, f32[256,256]{1,0:T(8,128)}, u32[]{:S(2)}) copy-start(f32[256,256]{1,0:T(8,128)} %factor.3) | copy-start | bytes 786436
  2.4 25.0 %all-to-all-start = ((f32[8,64,256]{2,1,0:T(8,128)}), f32[8,64,256]{2,1,0:T(8,128)S(1)}, u32[]{:S(2)}, u32[]{:S(2)}) async-start(f32[8,64,256]{2,1,0:T(8,128)} %broadcast_in_dim.6), calls=%async_computation | async-start | bytes 1048576 | tf_op jit(solution)/shard_map/all_to_all | solution.py:49
  10.8 13.7 %collective-permute-start = (f32[64,256]{1,0:T(8,128)}, f32[64,256]{1,0:T(8,128)S(1)}, u32[]{:S(2)}, u32[]{:S(2)}) collective-permute-start(f32[64,256]{1,0:T(8,128)} %panel.1), channel_id=1, source_target_pairs={{0,0},{1,32},{2,64},{3,96},{4,128},{5,160},{6,192},{7,224},{8,1},{... | collective-permute-start | bytes 196616 | tf_op jit(solution)/shard_map/ppermute | solution.py:254
  27.4 13.6 %collective-permute-start.5 = (f32[256,256]{1,0:T(8,128)S(1)}, f32[256,256]{1,0:T(8,128)S(1)}, u32[]{:S(2)}, u32[]{:S(2)}) collective-permute-start(f32[256,256]{1,0:T(8,128)S(1)} %get-tuple-element.21.refs_0_), channel_id=1, source_target_pairs={{0,8},{1,9},{2,10},{3,11},{4,12},{5,13},{6,14},{7,15},{8,16},{9,17... | collective-permute-start | bytes 786440 | tf_op jit(solution)/shard_map/ppermute | solution.py:54
  31.5 11.0 %collective-permute-start.8 = (f32[256,256]{1,0:T(8,128)S(1)}, f32[256,256]{1,0:T(8,128)S(1)}, u32[]{:S(2)}, u32[]{:S(2)}) collective-permute-start(f32[256,256]{1,0:T(8,128)S(1)} %get-tuple-element.20.refs_1_), channel_id=1, source_target_pairs={{0,24},{1,25},{2,26},{3,27},{4,28},{5,29},{6,30},{7,31},{8,0},{9,1... | collective-permute-start | bytes 786440 | tf_op jit(solution)/shard_map/ppermute | solution.py:54
  31.5 5.3 %collective-permute-start.1 = (f32[64,256]{1,0:T(8,128)S(1)}, f32[64,256]{1,0:T(8,128)S(1)}, u32[]{:S(2)}, u32[]{:S(2)}) collective-permute-start(f32[64,256]{1,0:T(8,128)S(1)} %collective-permute-done.refs_0_), channel_id=1, source_target_pairs={{0,192},{32,224},{64,0},{96,32},{128,64},{160,96},{192,128},{224,1... | collective-permute-start | bytes 196616 | tf_op jit(solution)/shard_map/ppermute | solution.py:79
  32.0 6.7 %collective-permute-start.2 = (f32[64,256]{1,0:T(8,128)S(1)}, f32[64,256]{1,0:T(8,128)S(1)}, u32[]{:S(2)}, u32[]{:S(2)}) collective-permute-start(f32[64,256]{1,0:T(8,128)S(1)} %collective-permute-done.refs_0_), channel_id=1, source_target_pairs={{0,128},{32,160},{64,192},{96,224},{128,0},{160,32},{192,64},{224,... | collective-permute-start | bytes 196616 | tf_op jit(solution)/shard_map/ppermute | solution.py:79
  35.0 4.3 %collective-permute-start.3 = (f32[64,256]{1,0:T(8,128)S(1)}, f32[64,256]{1,0:T(8,128)S(1)}, u32[]{:S(2)}, u32[]{:S(2)}) collective-permute-start(f32[64,256]{1,0:T(8,128)S(1)} %collective-permute-done.refs_0_), channel_id=1, source_target_pairs={{0,64},{32,96},{64,128},{96,160},{128,192},{160,224},{192,0},{224,... | collective-permute-start | bytes 196616 | tf_op jit(solution)/shard_map/ppermute | solution.py:79
  36.8 8.1 %collective-permute-start.10 = (f32[256,256]{1,0:T(8,128)S(1)}, f32[256,256]{1,0:T(8,128)S(1)}, u32[]{:S(2)}, u32[]{:S(2)}) collective-permute-start(f32[256,256]{1,0:T(8,128)S(1)} %get-tuple-element.21.refs_0_), channel_id=1, source_target_pairs={{0,24},{1,25},{2,26},{3,27},{4,28},{5,29},{6,30},{7,31},{8,0},{9,1... | collective-permute-start | bytes 786440 | tf_op jit(solution)/shard_map/ppermute | solution.py:54
  39.3 5.0 %collective-permute-start.4 = (f32[4,64,256]{2,1,0:T(8,128)S(1)}, f32[4,64,256]{2,1,0:T(8,128)S(1)}, u32[]{:S(2)}, u32[]{:S(2)}) collective-permute-start(f32[4,64,256]{2,1,0:T(8,128)S(1)} %pad_maximum_fusion), channel_id=1, source_target_pairs={{0,32},{32,0},{64,96},{96,64},{128,160},{160,128},{192,224},{224,1... | collective-permute-start | bytes 786440 | tf_op jit(solution)/shard_map/ppermute | solution.py:86
  39.4 10.4 %collective-permute-start.6 = (f32[256,256]{1,0:T(8,128)S(1)}, f32[256,256]{1,0:T(8,128)S(1)}, u32[]{:S(2)}, u32[]{:S(2)}) collective-permute-start(f32[256,256]{1,0:T(8,128)S(1)} %get-tuple-element.20.refs_1_), channel_id=1, source_target_pairs={{0,8},{1,9},{2,10},{3,11},{4,12},{5,13},{6,14},{7,15},{8,16},{9,17... | collective-permute-start | bytes 786440 | tf_op jit(solution)/shard_map/ppermute | solution.py:54
  41.0 14.0 %collective-permute-start.7 = (f32[256,256]{1,0:T(8,128)S(1)}, f32[256,256]{1,0:T(8,128)S(1)}, u32[]{:S(2)}, u32[]{:S(2)}) collective-permute-start(f32[256,256]{1,0:T(8,128)S(1)} %collective-permute-done.5.refs_2_), channel_id=1, source_target_pairs={{0,8},{1,9},{2,10},{3,11},{4,12},{5,13},{6,14},{7,15},{8,16},{9,17... | collective-permute-start | bytes 786440 | tf_op jit(solution)/shard_map/ppermute | solution.py:54
  42.5 12.4 %collective-permute-start.9 = (f32[256,256]{1,0:T(8,128)S(1)}, f32[256,256]{1,0:T(8,128)S(1)}, u32[]{:S(2)}, u32[]{:S(2)}) collective-permute-start(f32[256,256]{1,0:T(8,128)S(1)} %collective-permute-done.8.refs_7_), channel_id=1, source_target_pairs={{0,24},{1,25},{2,26},{3,27},{4,28},{5,29},{6,30},{7,31},{8,0},{9,1... | collective-permute-start | bytes 786440 | tf_op jit(solution)/shard_map/ppermute | solution.py:54
  63.3 89.0 %copy-start.1 = (f32[64,256]{1,0:T(8,128)S(1)}, f32[64,256]{1,0:T(8,128)}, u32[]{:S(2)}) copy-start(f32[64,256]{1,0:T(8,128)} %panel.1) | copy-start | bytes 196612
  82.1 9.6 %collective-permute-start.16 = (f32[32,256]{1,0:T(8,128)S(1)}, f32[32,256]{1,0:T(8,128)S(1)}, u32[]{:S(2)}, u32[]{:S(2)}) collective-permute-start(f32[32,256]{1,0:T(8,128)S(1)} %slice.25), channel_id=1, source_target_pairs={{0,1},{1,0},{2,3},{3,2},{4,5},{5,4},{6,7},{7,6},{8,9},{9,8},{10,11... | collective-permute-start | bytes 98312 | tf_op jit(solution)/shard_map/ppermute | solution.py:71
  84.5 12.2 %collective-permute-start.11 = (f32[64,256]{1,0:T(8,128)S(1)}, f32[64,256]{1,0:T(8,128)S(1)}, u32[]{:S(2)}, u32[]{:S(2)}) collective-permute-start(f32[64,256]{1,0:T(8,128)S(1)} %slice.24.refs_0_), channel_id=1, source_target_pairs={{0,0},{32,1},{64,2},{96,3},{128,4},{160,5},{192,6},{224,7},{1,8},{... | collective-permute-start | bytes 196616 | tf_op jit(solution)/shard_map/ppermute | solution.py:264
  91.7 5.1 %collective-permute-start.17 = (f32[32,256]{1,0:T(8,128)S(1)}, f32[32,256]{1,0:T(8,128)S(1)}, u32[]{:S(2)}, u32[]{:S(2)}) collective-permute-start(f32[32,256]{1,0:T(8,128)S(1)} %slice_add_fusion), channel_id=1, source_target_pairs={{0,2},{1,3},{2,0},{3,1},{4,6},{5,7},{6,4},{7,5},{8,10},{9,11},{10,... | collective-permute-start | bytes 98312 | tf_op jit(solution)/shard_map/ppermute | solution.py:71
  97.6 34.5 %all-to-all-start.2 = ((f32[8,64,256]{2,1,0:T(8,128)}), f32[8,64,256]{2,1,0:T(8,128)}, u32[]{:S(2)}, u32[]{:S(2)}) async-start(f32[8,64,256]{2,1,0:T(8,128)} %broadcast_in_dim.7), calls=%async_computation.2 | async-start | bytes 1048576 | tf_op jit(solution)/shard_map/all_to_all | solution.py:49
  101.9 18.3 %collective-permute-start.18 = (f32[32,256]{1,0:T(8,128)S(1)}, f32[32,256]{1,0:T(8,128)S(1)}, u32[]{:S(2)}, u32[]{:S(2)}) collective-permute-start(f32[32,256]{1,0:T(8,128)S(1)} %add.26), channel_id=1, source_target_pairs={{0,4},{1,5},{2,6},{3,7},{4,0},{5,1},{6,2},{7,3},{8,12},{9,13},{10,... | collective-permute-start | bytes 98312 | tf_op jit(solution)/shard_map/ppermute | solution.py:71
  120.2 7.0 %collective-permute-start.19 = (f32[32,256]{1,0:T(8,128)S(1)}, f32[32,256]{1,0:T(8,128)S(1)}, u32[]{:S(2)}, u32[]{:S(2)}) collective-permute-start(f32[32,256]{1,0:T(8,128)S(1)} %add.27), channel_id=1, source_target_pairs={{0,8},{1,9},{2,10},{3,11},{4,12},{5,13},{6,14},{7,15},{8,16},{9,17... | collective-permute-start | bytes 98312 | tf_op jit(solution)/shard_map/ppermute | solution.py:54
  120.2 9.5 %collective-permute-start.20 = (f32[32,256]{1,0:T(8,128)S(1)}, f32[32,256]{1,0:T(8,128)S(1)}, u32[]{:S(2)}, u32[]{:S(2)}) collective-permute-start(f32[32,256]{1,0:T(8,128)S(1)} %add.27), channel_id=1, source_target_pairs={{0,16},{1,17},{2,18},{3,19},{4,20},{5,21},{6,22},{7,23},{8,24},{9,... | collective-permute-start | bytes 98312 | tf_op jit(solution)/shard_map/ppermute | solution.py:54
  123.6 6.1 %collective-permute-start.21 = (f32[32,256]{1,0:T(8,128)S(1)}, f32[32,256]{1,0:T(8,128)S(1)}, u32[]{:S(2)}, u32[]{:S(2)}) collective-permute-start(f32[32,256]{1,0:T(8,128)S(1)} %add.27), channel_id=1, source_target_pairs={{0,24},{1,25},{2,26},{3,27},{4,28},{5,29},{6,30},{7,31},{8,0},{9,1... | collective-permute-start | bytes 98312 | tf_op jit(solution)/shard_map/ppermute | solution.py:54
  123.6 6.0 %collective-permute-start.12 = (f32[64,256]{1,0:T(8,128)S(1)}, f32[64,256]{1,0:T(8,128)S(1)}, u32[]{:S(2)}, u32[]{:S(2)}) collective-permute-start(f32[64,256]{1,0:T(8,128)S(1)} %slice.24.refs_0_), channel_id=1, source_target_pairs={{0,192},{32,224},{64,0},{96,32},{128,64},{160,96},{192,128},{224,1... | collective-permute-start | bytes 196616 | tf_op jit(solution)/shard_map/ppermute | solution.py:79
  126.3 5.8 %collective-permute-start.13 = (f32[64,256]{1,0:T(8,128)S(1)}, f32[64,256]{1,0:T(8,128)S(1)}, u32[]{:S(2)}, u32[]{:S(2)}) collective-permute-start(f32[64,256]{1,0:T(8,128)S(1)} %slice.24.refs_0_), channel_id=1, source_target_pairs={{0,128},{32,160},{64,192},{96,224},{128,0},{160,32},{192,64},{224,... | collective-permute-start | bytes 196616 | tf_op jit(solution)/shard_map/ppermute | solution.py:79
  127.2 5.0 %collective-permute-start.14 = (f32[64,256]{1,0:T(8,128)S(1)}, f32[64,256]{1,0:T(8,128)S(1)}, u32[]{:S(2)}, u32[]{:S(2)}) collective-permute-start(f32[64,256]{1,0:T(8,128)S(1)} %slice.24.refs_0_), channel_id=1, source_target_pairs={{0,64},{32,96},{64,128},{96,160},{128,192},{160,224},{192,0},{224,... | collective-permute-start | bytes 196616 | tf_op jit(solution)/shard_map/ppermute | solution.py:79
  133.2 14.4 %collective-permute-start.26 = (f32[256,256]{1,0:T(8,128)S(1)}, f32[256,256]{1,0:T(8,128)S(1)}, u32[]{:S(2)}, u32[]{:S(2)}) collective-permute-start(f32[256,256]{1,0:T(8,128)S(1)} %get-tuple-element.19.refs_0_), channel_id=1, source_target_pairs={{0,8},{1,9},{2,10},{3,11},{4,12},{5,13},{6,14},{7,15},{8,16},{9,17... | collective-permute-start | bytes 786440 | tf_op jit(solution)/shard_map/ppermute | solution.py:54
  133.8 13.8 %collective-permute-start.29 = (f32[256,256]{1,0:T(8,128)S(1)}, f32[256,256]{1,0:T(8,128)S(1)}, u32[]{:S(2)}, u32[]{:S(2)}) collective-permute-start(f32[256,256]{1,0:T(8,128)S(1)} %get-tuple-element.18.refs_1_), channel_id=1, source_target_pairs={{0,24},{1,25},{2,26},{3,27},{4,28},{5,29},{6,30},{7,31},{8,0},{9,1... | collective-permute-start | bytes 786440 | tf_op jit(solution)/shard_map/ppermute | solution.py:54
  136.5 14.3 %collective-permute-start.15 = (f32[4,64,256]{2,1,0:T(8,128)S(1)}, f32[4,64,256]{2,1,0:T(8,128)S(1)}, u32[]{:S(2)}, u32[]{:S(2)}) collective-permute-start(f32[4,64,256]{2,1,0:T(8,128)S(1)} %pad_maximum_fusion.1), channel_id=1, source_target_pairs={{0,32},{32,0},{64,96},{96,64},{128,160},{160,128},{192,224},{224,1... | collective-permute-start | bytes 786440 | tf_op jit(solution)/shard_map/ppermute | solution.py:86
  136.6 4.0 %collective-permute-start.22 = (f32[32,256]{1,0:T(8,128)S(1)}, f32[32,256]{1,0:T(8,128)S(1)}, u32[]{:S(2)}, u32[]{:S(2)}) collective-permute-start(f32[32,256]{1,0:T(8,128)S(1)} %add_add_fusion.refs_0_), channel_id=1, source_target_pairs={{0,192},{32,224},{64,0},{96,32},{128,64},{160,96},{192,128},{224,1... | collective-permute-start | bytes 98312 | tf_op jit(solution)/shard_map/ppermute | solution.py:79
  139.0 5.4 %collective-permute-start.23 = (f32[32,256]{1,0:T(8,128)S(1)}, f32[32,256]{1,0:T(8,128)S(1)}, u32[]{:S(2)}, u32[]{:S(2)}) collective-permute-start(f32[32,256]{1,0:T(8,128)S(1)} %add_add_fusion.refs_0_), channel_id=1, source_target_pairs={{0,128},{32,160},{64,192},{96,224},{128,0},{160,32},{192,64},{224,... | collective-permute-start | bytes 98312 | tf_op jit(solution)/shard_map/ppermute | solution.py:79
  140.6 4.3 %collective-permute-start.24 = (f32[32,256]{1,0:T(8,128)S(1)}, f32[32,256]{1,0:T(8,128)S(1)}, u32[]{:S(2)}, u32[]{:S(2)}) collective-permute-start(f32[32,256]{1,0:T(8,128)S(1)} %add_add_fusion.refs_0_), channel_id=1, source_target_pairs={{0,64},{32,96},{64,128},{96,160},{128,192},{160,224},{192,0},{224,... | collective-permute-start | bytes 98312 | tf_op jit(solution)/shard_map/ppermute | solution.py:79
  144.4 20.8 %collective-permute-start.27 = (f32[256,256]{1,0:T(8,128)S(1)}, f32[256,256]{1,0:T(8,128)S(1)}, u32[]{:S(2)}, u32[]{:S(2)}) collective-permute-start(f32[256,256]{1,0:T(8,128)S(1)} %get-tuple-element.18.refs_1_), channel_id=1, source_target_pairs={{0,8},{1,9},{2,10},{3,11},{4,12},{5,13},{6,14},{7,15},{8,16},{9,17... | collective-permute-start | bytes 786440 | tf_op jit(solution)/shard_map/ppermute | solution.py:54
  144.9 20.3 %collective-permute-start.31 = (f32[256,256]{1,0:T(8,128)S(1)}, f32[256,256]{1,0:T(8,128)S(1)}, u32[]{:S(2)}, u32[]{:S(2)}) collective-permute-start(f32[256,256]{1,0:T(8,128)S(1)} %get-tuple-element.19.refs_0_), channel_id=1, source_target_pairs={{0,24},{1,25},{2,26},{3,27},{4,28},{5,29},{6,30},{7,31},{8,0},{9,1... | collective-permute-start | bytes 786440 | tf_op jit(solution)/shard_map/ppermute | solution.py:54
  147.6 17.6 %collective-permute-start.28 = (f32[256,256]{1,0:T(8,128)S(1)}, f32[256,256]{1,0:T(8,128)S(1)}, u32[]{:S(2)}, u32[]{:S(2)}) collective-permute-start(f32[256,256]{1,0:T(8,128)S(1)} %collective-permute-done.26.refs_0_), channel_id=1, source_target_pairs={{0,8},{1,9},{2,10},{3,11},{4,12},{5,13},{6,14},{7,15},{8,16},{9,17... | collective-permute-start | bytes 786440 | tf_op jit(solution)/shard_map/ppermute | solution.py:54
  147.6 17.6 %collective-permute-start.30 = (f32[256,256]{1,0:T(8,128)S(1)}, f32[256,256]{1,0:T(8,128)S(1)}, u32[]{:S(2)}, u32[]{:S(2)}) collective-permute-start(f32[256,256]{1,0:T(8,128)S(1)} %collective-permute-done.29.refs_5_), channel_id=1, source_target_pairs={{0,24},{1,25},{2,26},{3,27},{4,28},{5,29},{6,30},{7,31},{8,0},{9,1... | collective-permute-start | bytes 786440 | tf_op jit(solution)/shard_map/ppermute | solution.py:54
  150.9 1.4 collective-permute-start.25

commit v5 on v3

v5 whole, which is shorter than its diff:
```python
import jax
import jax.numpy as jnp
from jax import lax
from jax.experimental import pallas as pl
from jax.experimental.pallas import tpu as pltpu
from jax.sharding import PartitionSpec as P

NX, NY, NZ, CORES = 4, 4, 8, 2
Z_GROUPS = [[y * NZ + z for z in range(NZ)] for y in range(NY)]
WHOLE = pl.BlockSpec(memory_space=pltpu.VMEM)
SCALARS = pl.BlockSpec(memory_space=pltpu.SMEM)
FREE = pl.CostEstimate(flops=1, bytes_accessed=1, transcendentals=0)
PARAMS = pltpu.CompilerParams(vmem_limit_bytes=20 << 20)


def after(value, *others):
    return lax.optimization_barrier((value,) + others)[0]


def exact(left, right, contract):
    return lax.dot_general(
        left,
        right,
        (contract, ((), ())),
        precision=lax.Precision.HIGHEST,
        preferred_element_type=jnp.float32,
    )


def halves(value):
    high = value.astype(jnp.bfloat16)
    return high, (value - high.astype(jnp.float32)).astype(jnp.bfloat16)


def three_pass(left, right, contract):
    def one(a, b):
        return lax.dot_general(a, b, (contract, ((), ())), preferred_element_type=jnp.float32)

    return one(left[0], right[1]) + one(left[1], right[0]) + one(left[0], right[0])


def spread(value, groups):
    copies = jnp.broadcast_to(value, (len(groups[0]),) + value.shape)
    return lax.all_to_all(copies, "col", 0, 0, axis_index_groups=groups)


def y_blocks(value):
    def shifted(step):
        perm = [(y * NZ + z, (y + step) % NY * NZ + z) for y in range(NY) for z in range(NZ)]
        return lax.ppermute(value, "col", perm)

    return [value] + [shifted(step) for step in range(1, NY)]


def y_sum(value):
    for bit in (1, 2):
        perm = [(y * NZ + z, (y ^ bit) * NZ + z) for y in range(NY) for z in range(NZ)]
        value += lax.ppermute(value, "col", perm)
    return value


def x_blocks(value):
    size = NX * CORES

    def shifted(step):
        perm = [(i, (i - CORES * step) % size) for i in range(size)]
        return lax.ppermute(value, "row", perm)

    return [value] + [shifted(step) for step in range(1, NX)]


def other_core(values):
    perm = [(i, i ^ 1) for i in range(NX * CORES)]
    return lax.ppermute(jnp.stack(values), "row", perm)


def assemble(place, mine, other, out):
    for k in range(NX):
        slot = lax.rem(place[0] + k, NX) * CORES
        out[slot + place[1]] = mine[k][...]
        out[slot + 1 - place[1]] = other[k]


def assemble_kernel(place, *refs):
    assemble(place, refs[:NX], refs[NX], refs[NX + 1])


def row_blocks(place, mine, other):
    shape = (NX * CORES,) + mine[0].shape
    return pl.pallas_call(
        assemble_kernel,
        out_shape=jax.ShapeDtypeStruct(shape, mine[0].dtype),
        in_specs=[SCALARS] + [WHOLE] * (NX + 1),
        out_specs=WHOLE,
        cost_estimate=FREE,
        compiler_params=PARAMS,
    )(place, *mine, other)


def local(kernel, shapes, operands, scratch=(), scalars=1):
    single = not isinstance(shapes, list)
    shapes = [shapes] if single else shapes
    results = pl.pallas_call(
        kernel,
        out_shape=[jax.ShapeDtypeStruct(shape, jnp.float32) for shape in shapes],
        in_specs=[SCALARS] * scalars + [WHOLE] * (len(operands) - scalars),
        out_specs=[WHOLE] * len(shapes),
        scratch_shapes=scratch,
        cost_estimate=FREE,
        compiler_params=PARAMS,
    )(*operands)
    return results[0] if single else results


def stage_kernel(matrix, out):
    pltpu.sync_copy(matrix, out)


def stage(matrix):
    return pl.pallas_call(
        stage_kernel,
        out_shape=jax.ShapeDtypeStruct(matrix.shape, matrix.dtype),
        in_specs=[pl.BlockSpec(memory_space=pl.ANY)],
        out_specs=WHOLE,
        cost_estimate=FREE,
        compiler_params=PARAMS,
    )(matrix)


def rows_of(y_ref, step, size):
    return pl.ds(pl.multiple_of(lax.rem(y_ref[0] + (NY - step), NY) * size, size), size)


def product_kernel(y_ref, matrix, factor, col_panel, *refs):
    panels, out, total = refs[:NY], refs[NY], refs[NY + 1]
    for k in range(NY):
        block = matrix[rows_of(y_ref, k, panels[k].shape[0]), :]
        piece = three_pass(halves(panels[k][...]), halves(block), ((0,), (0,)))
        if k == 0:
            total[...] = piece
        else:
            total[...] += piece
    count, rows, width = out.shape
    depth = width // count
    scaled = exact(total[...], factor[...], ((0,), (0,)))
    inner = exact(col_panel[...], scaled, ((0,), (0,)))
    out[:, : rows - depth, :] = scaled.reshape(count, rows - depth, width)
    out[:, rows - depth :, :] = inner.reshape(count, depth, width)


def reduce_kernel(parts, chunk, inner):
    total = parts[0]
    for k in range(1, parts.shape[0]):
        total += parts[k]
    chunk[...] = total[: chunk.shape[0]]
    inner[...] = total[chunk.shape[0] :]


def split_kernel(parts, block, inner):
    rows = block.shape[1]
    block[...] = parts[:, :rows, :]
    total = parts[0, rows:, :]
    for k in range(1, parts.shape[0]):
        total += parts[k, rows:, :]
    inner[...] = total


def middle_kernel(place, factor, panel, home, col_panel, *refs):
    blocks, (left, correction, scaled, small) = refs[:-4], refs[-4:]
    half = NX + 1
    assemble(place, blocks[:NX], blocks[NX], scaled)
    assemble(place, blocks[half : half + NX], blocks[half + NX], small)
    width = panel.shape[1]
    kernel = 0.5 * exact(factor[...], small[...].reshape(width, width), ((0,), (0,)))
    correction[...] = home[...] - exact(panel[...], kernel, ((1,), (0,)))
    wanted = exact(col_panel[...], kernel + kernel.T, ((1,), (0,)))
    left[...] = scaled[...].reshape(left.shape) - wanted


def first_update_kernel(y_ref, matrix, left, col_panel, own_scaled, *refs):
    panels, out = refs[:NY], refs[NY]
    right = halves(left[...])
    for k in range(NY):
        rows = rows_of(y_ref, k, panels[k].shape[0])
        value = matrix[rows, :] - three_pass(halves(panels[k][...]), right, ((1,), (1,)))
        if k == 0:
            pair = halves(own_scaled[...]), halves(col_panel[...])
            value -= three_pass(*pair, ((1,), (1,)))
        out[rows, :] = value


def last_update_kernel(y_ref, matrix, right, *refs):
    parts = refs[: NY - 1]
    out, right_high, right_low = refs[NY - 1 :]
    step = pl.program_id(0)

    @pl.when(step == 0)
    def _():
        right_high[...], right_low[...] = halves(right[...])
        out[...] = matrix[...]

    for k in range(1, NY):

        @pl.when(step == k)
        def _():
            pair = right_high[...], right_low[...]
            out[...] = matrix[...] - three_pass(halves(parts[k - 1][...]), pair, ((1,), (1,)))


def last_update(y, matrix, parts, right):
    rows, cols = matrix.shape
    block, width = parts[0].shape

    def moving(s, y_ref):
        return (lax.rem(y_ref[0] + (NY - s), NY), 0)

    def fixed(s, y_ref):
        return (0, 0)

    return pl.pallas_call(
        last_update_kernel,
        out_shape=jax.ShapeDtypeStruct((rows, cols), jnp.float32),
        grid_spec=pltpu.PrefetchScalarGridSpec(
            num_scalar_prefetch=1,
            grid=(NY,),
            in_specs=[pl.BlockSpec((block, cols), moving), pl.BlockSpec((cols, width), fixed)]
            + [pl.BlockSpec((block, width), fixed)] * (NY - 1),
            out_specs=pl.BlockSpec((block, cols), moving),
            scratch_shapes=[pltpu.VMEM((cols, width), jnp.bfloat16)] * 2,
        ),
        cost_estimate=FREE,
        compiler_params=PARAMS,
    )(y, matrix, right, *parts)


def per_device(matrix, panel, factor):
    nrows, ncols = lax.axis_size("row"), lax.axis_size("col")
    rows, width = panel.shape
    block = NZ * rows
    row = lax.axis_index("row")
    y = (lax.axis_index("col") // NZ).reshape(1)
    place = jnp.stack([row // CORES, row % CORES])
    total = nrows * ncols
    to_column = [(g, g % nrows * ncols + g // nrows) for g in range(total)]
    to_home = [(b, a) for a, b in to_column]

    moved = lax.ppermute(panel, ("row", "col"), to_column)
    mine = x_blocks(moved)
    panels = y_blocks(spread(panel, Z_GROUPS).reshape(block, width))
    col_panel = row_blocks(place, mine, other_core(mine)).reshape(nrows * rows, width)
    staged = stage(after(matrix, moved))

    depth = width // nrows
    parts = local(
        product_kernel,
        (nrows, rows + depth, width),
        (y, staged, factor, col_panel, *panels),
        [pltpu.VMEM((width, nrows * rows), jnp.float32)],
    )
    parts = lax.all_to_all(parts, "row", 0, 0)
    pair = [(rows, width), (depth, width)]
    chunk, inner = local(reduce_kernel, pair, (parts,), scalars=0)

    home = lax.ppermute(chunk, ("row", "col"), to_home)
    parts = spread(jnp.concatenate([home, y_sum(inner)]), Z_GROUPS)
    scaled = x_blocks(after(chunk, home))
    scaled += [other_core(scaled)]
    parts = after(parts, *scaled)
    pair = [(NZ, rows, width), (depth, width)]
    own_scaled, inner = local(split_kernel, pair, (parts,), scalars=0)
    scaleds = y_blocks(own_scaled.reshape(block, width))

    small = x_blocks(after(inner, own_scaled))
    small += [other_core(small)]
    left, correction = local(
        middle_kernel,
        [col_panel.shape, home.shape],
        (place, factor, panel, home, col_panel, *scaled, *small),
        [pltpu.VMEM((nrows, size, width), jnp.float32) for size in (rows, depth)],
    )
    updated = local(
        first_update_kernel, matrix.shape, (y, staged, left, col_panel, scaleds[0], *panels)
    )
    return last_update(y, updated, scaleds[1:], col_panel), correction


def solution(mesh):
    in_specs = (P("row", "col"), P(("row", "col"), None), P())
    out_specs = (P("row", "col"), P(("row", "col"), None))
    return jax.shard_map(
        per_device, mesh=mesh, in_specs=in_specs, out_specs=out_specs, check_vma=False
    )
```

time: 169 us -> 150 us (0.89)
  starting transfers between devices: 57.4 us -> 48.5 us
  waiting for transfers between devices: 63.7 us -> 56 us
  Pallas kernels: 17.4 us -> 12.7 us
  local copies, waits for them, and re-layouts: 9.54 us -> 13 us
    ppermute x4 -> x3, waiting for transfers between devices: 17.8 us -> 3.6 us  [the longest x2 3.6 us: y_sum(): value += lax.ppermute(value, 'col', perm)]
    all_to_all x2, waiting for transfers between devices: 13.1 us -> 23.4 us  [spread(): return lax.all_to_all(copies, 'col', 0, 0, axis_index_groups=groups)]
    ppermute x9 -> x6, starting transfers between devices: 15.2 us -> 9.43 us  [shifted(): return lax.ppermute(value, 'col', perm)]
    ppermute x4 -> x3, starting transfers between devices: 12.2 us -> 7.35 us  [the longest x2 3.9 us: y_sum(): value += lax.ppermute(value, 'col', perm)]
    pallas_call x4 -> x7, Pallas kernels: 16.2 us -> 12.1 us  [the longest x5 8.45 us: local(): pl.pallas_call(kernel, out_shape=[jax.ShapeDtypeStruct(shape, jnp.float32...]
    unnamed x14 -> x32, local copies, waits for them, and re-layouts: 7.01 us -> 10.4 us
    ppermute x1, waiting for transfers between devices: 5.9 us -> 4.04 us  [per_device(): home = lax.ppermute(chunk, ('row', 'col'), to_home)]
    ppermute x9 -> x6, waiting for transfers between devices: 14 us -> 13.1 us  [shifted(): return lax.ppermute(value, 'col', perm)]
  transfers between devices with their start and end apart: 28 -> 24, of which waited for: 17 -> 18; matrix products, arithmetic and copies ran while one was open for 0% -> 1% of each run, Pallas kernels for 4% -> 4%
where the time goes in v5:
time: 150 us; the launch traced here: 149 us
  waiting for transfers between devices  56 us (37%)
  starting transfers between devices  48.5 us (32%)
  blocking collectives  16.6 us (11%)
  local copies, waits for them, and re-layouts  13 us (9%)
  Pallas kernels  12.7 us (8%)
    all_to_all x2, waiting for transfers between devices, spread(): return lax.all_to_all(copies, 'col', 0, 0, axis_index_groups=groups)  23.4 us
    ppermute x9, starting transfers between devices, shifted(): return lax.ppermute(value, 'row', perm)  17.4 us
    all_to_all x1, blocking collectives, per_device(): parts = lax.all_to_all(parts, 'row', 0, 0)  16.6 us
    ppermute x6, waiting for transfers between devices, shifted(): return lax.ppermute(value, 'col', perm)  13.1 us
    all_to_all x2, starting transfers between devices, spread(): return lax.all_to_all(copies, 'col', 0, 0, axis_index_groups=groups)  12 us
    unnamed x32, local copies, waits for them, and re-layouts  10.4 us
    ppermute x6, starting transfers between devices, shifted(): return lax.ppermute(value, 'col', perm)  9.43 us
    ppermute x9, waiting for transfers between devices, shifted(): return lax.ppermute(value, 'row', perm)  9.02 us
  transfers between devices with their start and end apart: 24, of which 18 were waited for; matrix products, arithmetic and copies ran while one was open for 1% of the time, Pallas kernels for 4%

profile of v5, /device:TPU:2, one launch (start us, length us, event | category | flops | bytes accessed | tf_op | source)
XLA Modules:
  0.0 148.6 jit_solution(10686864391438779164)
XLA Ops:
  0.6 1.7 %broadcast_in_dim.6 = f32[8,64,256]{2,1,0:T(8,128)} broadcast(f32[64,256]{1,0:T(8,128)} %panel.1), dimensions={1,2} | broadcast | bytes 589824 | tf_op jit(solution)/shard_map/broadcast_in_dim | solution.py:43
  2.3 8.5 %all-to-all-start = ((f32[8,64,256]{2,1,0:T(8,128)}), f32[8,64,256]{2,1,0:T(8,128)S(1)}, u32[]{:S(2)}, u32[]{:S(2)}) async-start(f32[8,64,256]{2,1,0:T(8,128)} %broadcast_in_dim.6), calls=%async_computation | async-start | bytes 1048576 | tf_op jit(solution)/shard_map/all_to_all | solution.py:44
  10.8 3.4 %collective-permute-start = (f32[64,256]{1,0:T(8,128)}, f32[64,256]{1,0:T(8,128)S(1)}, u32[]{:S(2)}, u32[]{:S(2)}) collective-permute-start(f32[64,256]{1,0:T(8,128)} %panel.1), channel_id=1, source_target_pairs={{0,0},{1,32},{2,64},{3,96},{4,128},{5,160},{6,192},{7,224},{8,1},{... | collective-permute-start | bytes 196616 | tf_op jit(solution)/shard_map/ppermute | solution.py:247
  14.2 13.1 %all-to-all-done = f32[8,64,256]{2,1,0:T(8,128)S(1)} async-done(((f32[8,64,256]{2,1,0:T(8,128)}), f32[8,64,256]{2,1,0:T(8,128)S(1)}, u32[]{:S(2)}, u32[]{:S(2)}) %all-to-all-start) | async-done | bytes 524320 | tf_op jit(solution)/shard_map/all_to_all | solution.py:44
  27.3 3.2 %collective-permute-start.7 = (f32[512,256]{1,0:T(8,128)S(1)}, f32[512,256]{1,0:T(8,128)S(1)}, u32[]{:S(2)}, u32[]{:S(2)}) collective-permute-start(f32[512,256]{1,0:T(8,128)S(1)} %bitcast.22), channel_id=1, source_target_pairs={{0,24},{1,25},{2,26},{3,27},{4,28},{5,29},{6,30},{7,31},{8,0},{9,1... | collective-permute-start | bytes 1572872 | tf_op jit(solution)/shard_map/ppermute | solution.py:50
  30.5 2.9 %collective-permute-start.6 = (f32[512,256]{1,0:T(8,128)S(1)}, f32[512,256]{1,0:T(8,128)S(1)}, u32[]{:S(2)}, u32[]{:S(2)}) collective-permute-start(f32[512,256]{1,0:T(8,128)S(1)} %bitcast.23), channel_id=1, source_target_pairs={{0,16},{1,17},{2,18},{3,19},{4,20},{5,21},{6,22},{7,23},{8,24},{9,... | collective-permute-start | bytes 1572872 | tf_op jit(solution)/shard_map/ppermute | solution.py:50
  33.4 1.0 collective-permute-start.5
  34.4 1.5 %collective-permute-start.3 = (f32[64,256]{1,0:T(8,128)S(1)}, f32[64,256]{1,0:T(8,128)S(1)}, u32[]{:S(2)}, u32[]{:S(2)}) collective-permute-start(f32[64,256]{1,0:T(8,128)S(1)} %collective-permute-done.refs_0_), channel_id=1, source_target_pairs={{0,64},{32,96},{64,128},{96,160},{128,192},{160,224},{192,0},{224,... | collective-permute-start | bytes 196616 | tf_op jit(solution)/shard_map/ppermute | solution.py:67
  35.9 1.1 collective-permute-start.2
  37.0 2.0 %collective-permute-done.3.refs_3_ = f32[64,256]{1,0:T(8,128)S(1)} collective-permute-done((f32[64,256]{1,0:T(8,128)S(1)}, f32[64,256]{1,0:T(8,128)S(1)}, u32[]{:S(2)}, u32[]{:S(2)}) %collective-permute-start.3) | collective-permute-done | bytes 65568 | tf_op jit(solution)/shard_map/ppermute | solution.py:67
  39.0 1.8 %collective-permute-start.1 = (f32[64,256]{1,0:T(8,128)S(1)}, f32[64,256]{1,0:T(8,128)S(1)}, u32[]{:S(2)}, u32[]{:S(2)}) collective-permute-start(f32[64,256]{1,0:T(8,128)S(1)} %collective-permute-done.refs_0_), channel_id=1, source_target_pairs={{0,192},{32,224},{64,0},{96,32},{128,64},{160,96},{192,128},{224,1... | collective-permute-start | bytes 196616 | tf_op jit(solution)/shard_map/ppermute | solution.py:67
  40.8 0.9 collective-permute-done.2.refs_2_
  41.7 1.5 %collective-permute-done.1.refs_1_ = f32[64,256]{1,0:T(8,128)S(1)} collective-permute-done((f32[64,256]{1,0:T(8,128)S(1)}, f32[64,256]{1,0:T(8,128)S(1)}, u32[]{:S(2)}, u32[]{:S(2)}) %collective-permute-start.1) | collective-permute-done | bytes 65568 | tf_op jit(solution)/shard_map/ppermute | solution.py:67
  43.3 0.1 collective-permute-start.4
  43.4 0.1 pad_add_fusion.place
  43.5 2.2 %copy-done.2 = f32[2048,512]{1,0:T(8,128)S(1)} copy-done((f32[2048,512]{1,0:T(8,128)S(1)}, f32[2048,512]{1,0:T(8,128)}, u32[]{:S(2)}) %copy-start.2) | copy-done | bytes 4194328
  45.7 0.3 shard_map.50.matrix
  45.9 0.0 copy-start
  46.0 0.6 shard_map.51
  46.6 0.3 collective-permute-done.6.refs_2_
  46.9 9.8 %collective-permute-done.5.refs_1_ = f32[512,256]{1,0:T(8,128)S(1)} collective-permute-done((f32[512,256]{1,0:T(8,128)S(1)}, f32[512,256]{1,0:T(8,128)S(1)}, u32[]{:S(2)}, u32[]{:S(2)}) %collective-permute-start.5) | collective-permute-done | bytes 524320 | tf_op jit(solution)/shard_map/ppermute | solution.py:50
  56.6 3.7 %shard_map.52 = f32[8,96,256]{2,1,0:T(8,128)S(1)} custom-call(s32[1]{0:T(128)} %bitcast.y_ref, f32[2048,512]{1,0:T(8,128)S(1)} %shard_map.50.matrix, f32[256,256]{1,0:T(8,128)S(1)} %copy-done.3, f32[512,256]{1,0:T(8,128)S(1)} %bitcast.18, f32[512,256]{1,0:T(8,128)S(1)} %bitcast.25, f32[512,256]{1,0:T(8,128)S(1)} %collective-permute-done.5.refs_1_, ...), custom_call_target="tpu_custom_call" | custom-call | flops 1 | bytes 1 | tf_op jit(solution)/shard_map/pallas_call | solution.py:103
  60.3 0.0 copy-start.7
  60.3 16.6 %all_to_all.15.parts = f32[8,96,256]{2,1,0:T(8,128)S(1)} all-to-all(f32[8,96,256]{2,1,0:T(8,128)S(1)} %shard_map.52), channel_id=1, replica_groups=mesh['row'=8,'col'=32] {'row'}, dimensions={0} | all-to-all | bytes 1572864 | tf_op jit(solution)/shard_map/all_to_all | solution.py:260
  76.9 1.5 %collective-permute-start.13 = (f32[32,256]{1,0:T(8,128)S(1)}, f32[32,256]{1,0:T(8,128)S(1)}, u32[]{:S(2)}, u32[]{:S(2)}) collective-permute-start(f32[32,256]{1,0:T(8,128)S(1)} %get-tuple-element.15), channel_id=1, source_target_pairs={{0,8},{1,9},{2,10},{3,11},{4,12},{5,13},{6,14},{7,15},{8,0},{9,1},... | collective-permute-start | bytes 98312 | tf_op jit(solution)/shard_map/ppermute | solution.py:58
  78.4 1.9 %collective-permute-start.8 = (f32[64,256]{1,0:T(8,128)S(1)}, f32[64,256]{1,0:T(8,128)S(1)}, u32[]{:S(2)}, u32[]{:S(2)}) collective-permute-start(f32[64,256]{1,0:T(8,128)S(1)} %get-tuple-element.14.refs_0_), channel_id=1, source_target_pairs={{0,0},{32,1},{64,2},{96,3},{128,4},{160,5},{192,6},{224,7},{1,8},{... | collective-permute-start | bytes 196616 | tf_op jit(solution)/shard_map/ppermute | solution.py:264
  80.4 0.6 collective-permute-done.13
  80.9 2.4 %collective-permute-start.14 = (f32[32,256]{1,0:T(8,128)S(1)}, f32[32,256]{1,0:T(8,128)S(1)}, u32[]{:S(2)}, u32[]{:S(2)}) collective-permute-start(f32[32,256]{1,0:T(8,128)S(1)} %add.13), channel_id=1, source_target_pairs={{0,16},{1,17},{2,18},{3,19},{4,20},{5,21},{6,22},{7,23},{8,24},{9,... | collective-permute-start | bytes 98312 | tf_op jit(solution)/shard_map/ppermute | solution.py:58
  83.3 3.0 %collective-permute-done.14 = f32[32,256]{1,0:T(8,128)S(1)} collective-permute-done((f32[32,256]{1,0:T(8,128)S(1)}, f32[32,256]{1,0:T(8,128)S(1)}, u32[]{:S(2)}, u32[]{:S(2)}) %collective-permute-start.14) | collective-permute-done | bytes 32800 | tf_op jit(solution)/shard_map/ppermute | solution.py:58
  86.4 4.0 %collective-permute-done.8.home = f32[64,256]{1,0:T(8,128)S(1)} collective-permute-done((f32[64,256]{1,0:T(8,128)S(1)}, f32[64,256]{1,0:T(8,128)S(1)}, u32[]{:S(2)}, u32[]{:S(2)}) %collective-permute-start.8) | collective-permute-done | bytes 65568 | tf_op jit(solution)/shard_map/ppermute | solution.py:264
  90.4 1.0 broadcast_in_dim.7
  91.4 3.5 %all-to-all-start.2 = ((f32[8,96,256]{2,1,0:T(8,128)}), f32[8,96,256]{2,1,0:T(8,128)S(1)}, u32[]{:S(2)}, u32[]{:S(2)}) async-start(f32[8,96,256]{2,1,0:T(8,128)} %broadcast_in_dim.7), calls=%async_computation.2 | async-start | bytes 1572864 | tf_op jit(solution)/shard_map/all_to_all | solution.py:44
  94.9 2.7 %collective-permute-start.11 = (f32[64,256]{1,0:T(8,128)}, f32[64,256]{1,0:T(8,128)S(1)}, u32[]{:S(2)}, u32[]{:S(2)}) collective-permute-start(f32[64,256]{1,0:T(8,128)} %copy-done.8), channel_id=1, source_target_pairs={{0,64},{32,96},{64,128},{96,160},{128,192},{160,224},{192,0},{224,... | collective-permute-start | bytes 196616 | tf_op jit(solution)/shard_map/ppermute | solution.py:67
  97.6 1.1 collective-permute-start.10
  98.8 2.5 %collective-permute-start.9 = (f32[64,256]{1,0:T(8,128)}, f32[64,256]{1,0:T(8,128)S(1)}, u32[]{:S(2)}, u32[]{:S(2)}) collective-permute-start(f32[64,256]{1,0:T(8,128)} %copy-done.8), channel_id=1, source_target_pairs={{0,192},{32,224},{64,0},{96,32},{128,64},{160,96},{192,128},{224,1... | collective-permute-start | bytes 196616 | tf_op jit(solution)/shard_map/ppermute | solution.py:67
  101.3 2.4 %collective-permute-done.10.refs_2_ = f32[64,256]{1,0:T(8,128)S(1)} collective-permute-done((f32[64,256]{1,0:T(8,128)}, f32[64,256]{1,0:T(8,128)S(1)}, u32[]{:S(2)}, u32[]{:S(2)}) %collective-permute-start.10) | collective-permute-done | bytes 65568 | tf_op jit(solution)/shard_map/ppermute | solution.py:67
  103.7 0.2 collective-permute-done.9.refs_1_
  103.9 0.9 pad_maximum_fusion.1
  104.8 0.3 collective-permute-start.12
  105.1 1.5 %collective-permute-done.12.refs_4_ = f32[4,64,256]{2,1,0:T(8,128)S(1)} collective-permute-done((f32[4,64,256]{2,1,0:T(8,128)S(1)}, f32[4,64,256]{2,1,0:T(8,128)S(1)}, u32[]{:S(2)}, u32[]{:S(2)}) %collective-permute-start.12) | collective-permute-done | bytes 262176 | tf_op jit(solution)/shard_map/ppermute | solution.py:74
  106.6 0.7 copy-done.5
  107.3 10.3 %all-to-all-done.2.parts = f32[8,96,256]{2,1,0:T(8,128)S(1)} async-done(((f32[8,96,256]{2,1,0:T(8,128)}), f32[8,96,256]{2,1,0:T(8,128)S(1)}, u32[]{:S(2)}, u32[]{:S(2)}) %all-to-all-start.2) | async-done | bytes 786464 | tf_op jit(solution)/shard_map/all_to_all | solution.py:44
  117.7 0.1 shard_map.54
  117.7 1.4 collective-permute-start.21
  119.1 1.0 collective-permute-start.19
  120.1 2.3 %collective-permute-start.17 = (f32[32,256]{1,0:T(8,128)S(1)}, f32[32,256]{1,0:T(8,128)S(1)}, u32[]{:S(2)}, u32[]{:S(2)}) collective-permute-start(f32[32,256]{1,0:T(8,128)S(1)} %get-tuple-element.19.refs_5_), channel_id=1, source_target_pairs={{0,64},{32,96},{64,128},{96,160},{128,192},{160,224},{192,0},{224,... | collective-permute-start | bytes 98312 | tf_op jit(solution)/shard_map/ppermute | solution.py:67
  122.4 1.2 collective-permute-start.16
  123.6 0.4 collective-permute-done.17.refs_8_
  124.0 3.0 %collective-permute-start.15 = (f32[32,256]{1,0:T(8,128)S(1)}, f32[32,256]{1,0:T(8,128)S(1)}, u32[]{:S(2)}, u32[]{:S(2)}) collective-permute-start(f32[32,256]{1,0:T(8,128)S(1)} %get-tuple-element.19.refs_5_), channel_id=1, source_target_pairs={{0,192},{32,224},{64,0},{96,32},{128,64},{160,96},{192,128},{224,1... | collective-permute-start | bytes 98312 | tf_op jit(solution)/shard_map/ppermute | solution.py:67
  127.0 0.8 collective-permute-done.16.refs_7_
  127.8 0.8 collective-permute-done.15.refs_6_
  128.6 0.1 collective-permute-start.18
  128.8 1.3 collective-permute-done.18.refs_9_
  130.1 0.9 copy-done.4
  131.0 0.9 copy-done.6
  132.0 0.8 copy-done.9
  132.8 0.8 copy-done.11
  133.7 0.8 copy-done.13
  134.5 0.8 copy-done.15
  135.3 2.5 %shard_map.55 = (f32[512,256]{1,0:T(8,128)S(1)}, f32[64,256]{1,0:T(8,128)}) custom-call(s32[2]{0:T(128)S(1)} %pad_add_fusion.place, f32[256,256]{1,0:T(8,128)S(1)} %copy-done.4, f32[64,256]{1,0:T(8,128)S(1)} %copy-done.7, f32[64,256]{1,0:T(8,128)S(1)} %collective-permute-done.8.home, f32[512,256]{1,0:T(8,128)S(1)} %bitcast.19, f32[64,256]{1,0:T(8,128)S(1)} %copy-done.9, ...), custom_call_target="tpu_custom_call" | custom-call | flops 1 | bytes 1 | tf_op jit(solution)/shard_map/pallas_call | solution.py:103
  137.8 2.2 %copy-done.1 = f32[2048,512]{1,0:T(8,128)S(1)} copy-done((f32[2048,512]{1,0:T(8,128)S(1)}, f32[2048,512]{1,0:T(8,128)}, u32[]{:S(2)}) %copy-start.1) | copy-done | bytes 4194328
  140.0 2.2 %shard_map.56.matrix = f32[2048,512]{1,0:T(8,128)S(1)} custom-call(s32[1]{0:T(128)} %bitcast.y_ref, f32[2048,512]{1,0:T(8,128)S(1)} %copy-done.1, f32[512,256]{1,0:T(8,128)S(1)} %get-tuple-element.20.left, f32[512,256]{1,0:T(8,128)S(1)} %bitcast.20, f32[512,256]{1,0:T(8,128)S(1)} %bitcast.30, f32[512,256]{1,0:T(8,128)S(1)} %bitcast.26, ...), custom_call_target="tpu_custom_call" | custom-call | flops 1 | bytes 1 | tf_op jit(solution)/shard_map/pallas_call | solution.py:103
  142.3 3.0 %collective-permute-done.19.refs_0_ = f32[512,256]{1,0:T(8,128)S(1)} collective-permute-done((f32[512,256]{1,0:T(8,128)S(1)}, f32[512,256]{1,0:T(8,128)S(1)}, u32[]{:S(2)}, u32[]{:S(2)}) %collective-permute-start.19) | collective-permute-done | bytes 524320 | tf_op jit(solution)/shard_map/ppermute | solution.py:50
  145.3 3.4 %shard_map.57 = f32[2048,512]{1,0:T(8,128)} custom-call(s32[1]{0:T(128)} %bitcast.y_ref, f32[2048,512]{1,0:T(8,128)S(1)} %shard_map.56.matrix, f32[512,256]{1,0:T(8,128)S(1)} %bitcast.21, f32[512,256]{1,0:T(8,128)S(1)} %collective-permute-done.19.refs_0_, f32[512,256]{1,0:T(8,128)S(1)} %collective-permute-done.20.refs_1_, ...), custom_call_target="tpu_custom_call" | custom-call | flops 1 | bytes 1 | tf_op jit(solution)/shard_map/pallas_call | solution.py:220
  (34 shorter events, 0.1 us)
Async XLA Ops:
  2.3 25.0 %all-to-all-start = ((f32[8,64,256]{2,1,0:T(8,128)}), f32[8,64,256]{2,1,0:T(8,128)S(1)}, u32[]{:S(2)}, u32[]{:S(2)}) async-start(f32[8,64,256]{2,1,0:T(8,128)} %broadcast_in_dim.6), calls=%async_computation | async-start | bytes 1048576 | tf_op jit(solution)/shard_map/all_to_all | solution.py:44
  10.8 23.6 %collective-permute-start = (f32[64,256]{1,0:T(8,128)}, f32[64,256]{1,0:T(8,128)S(1)}, u32[]{:S(2)}, u32[]{:S(2)}) collective-permute-start(f32[64,256]{1,0:T(8,128)} %panel.1), channel_id=1, source_target_pairs={{0,0},{1,32},{2,64},{3,96},{4,128},{5,160},{6,192},{7,224},{8,1},{... | collective-permute-start | bytes 196616 | tf_op jit(solution)/shard_map/ppermute | solution.py:247
  27.3 19.2 %collective-permute-start.7 = (f32[512,256]{1,0:T(8,128)S(1)}, f32[512,256]{1,0:T(8,128)S(1)}, u32[]{:S(2)}, u32[]{:S(2)}) collective-permute-start(f32[512,256]{1,0:T(8,128)S(1)} %bitcast.22), channel_id=1, source_target_pairs={{0,24},{1,25},{2,26},{3,27},{4,28},{5,29},{6,30},{7,31},{8,0},{9,1... | collective-permute-start | bytes 1572872 | tf_op jit(solution)/shard_map/ppermute | solution.py:50
  30.5 16.4 %collective-permute-start.6 = (f32[512,256]{1,0:T(8,128)S(1)}, f32[512,256]{1,0:T(8,128)S(1)}, u32[]{:S(2)}, u32[]{:S(2)}) collective-permute-start(f32[512,256]{1,0:T(8,128)S(1)} %bitcast.23), channel_id=1, source_target_pairs={{0,16},{1,17},{2,18},{3,19},{4,20},{5,21},{6,22},{7,23},{8,24},{9,... | collective-permute-start | bytes 1572872 | tf_op jit(solution)/shard_map/ppermute | solution.py:50
  33.4 23.2 %collective-permute-start.5 = (f32[512,256]{1,0:T(8,128)S(1)}, f32[512,256]{1,0:T(8,128)S(1)}, u32[]{:S(2)}, u32[]{:S(2)}) collective-permute-start(f32[512,256]{1,0:T(8,128)S(1)} %bitcast.24), channel_id=1, source_target_pairs={{0,8},{1,9},{2,10},{3,11},{4,12},{5,13},{6,14},{7,15},{8,16},{9,17... | collective-permute-start | bytes 1572872 | tf_op jit(solution)/shard_map/ppermute | solution.py:50
  34.4 4.6 %collective-permute-start.3 = (f32[64,256]{1,0:T(8,128)S(1)}, f32[64,256]{1,0:T(8,128)S(1)}, u32[]{:S(2)}, u32[]{:S(2)}) collective-permute-start(f32[64,256]{1,0:T(8,128)S(1)} %collective-permute-done.refs_0_), channel_id=1, source_target_pairs={{0,64},{32,96},{64,128},{96,160},{128,192},{160,224},{192,0},{224,... | collective-permute-start | bytes 196616 | tf_op jit(solution)/shard_map/ppermute | solution.py:67
  35.9 5.8 %collective-permute-start.2 = (f32[64,256]{1,0:T(8,128)S(1)}, f32[64,256]{1,0:T(8,128)S(1)}, u32[]{:S(2)}, u32[]{:S(2)}) collective-permute-start(f32[64,256]{1,0:T(8,128)S(1)} %collective-permute-done.refs_0_), channel_id=1, source_target_pairs={{0,128},{32,160},{64,192},{96,224},{128,0},{160,32},{192,64},{224,... | collective-permute-start | bytes 196616 | tf_op jit(solution)/shard_map/ppermute | solution.py:67
  39.0 4.3 %collective-permute-start.1 = (f32[64,256]{1,0:T(8,128)S(1)}, f32[64,256]{1,0:T(8,128)S(1)}, u32[]{:S(2)}, u32[]{:S(2)}) collective-permute-start(f32[64,256]{1,0:T(8,128)S(1)} %collective-permute-done.refs_0_), channel_id=1, source_target_pairs={{0,192},{32,224},{64,0},{96,32},{128,64},{160,96},{192,128},{224,1... | collective-permute-start | bytes 196616 | tf_op jit(solution)/shard_map/ppermute | solution.py:67
  43.3 2.7 %collective-permute-start.4 = (f32[4,64,256]{2,1,0:T(8,128)S(1)}, f32[4,64,256]{2,1,0:T(8,128)S(1)}, u32[]{:S(2)}, u32[]{:S(2)}) collective-permute-start(f32[4,64,256]{2,1,0:T(8,128)S(1)} %pad_maximum_fusion), channel_id=1, source_target_pairs={{0,32},{32,0},{64,96},{96,64},{128,160},{160,128},{192,224},{224,1... | collective-permute-start | bytes 786440 | tf_op jit(solution)/shard_map/ppermute | solution.py:74
  43.5 2.2 %copy-start.2 = (f32[2048,512]{1,0:T(8,128)S(1)}, f32[2048,512]{1,0:T(8,128)}, u32[]{:S(2)}) copy-start(f32[2048,512]{1,0:T(8,128)} %matrix) | copy-start | bytes 12582916
  45.7 11.0 %copy-start.3 = (f32[256,256]{1,0:T(8,128)S(1)}, f32[256,256]{1,0:T(8,128)}, u32[]{:S(2)}) copy-start(f32[256,256]{1,0:T(8,128)} %factor.3) | copy-start | bytes 786436
  45.9 14.4 %copy-start = (f32[2048,512]{1,0:T(8,128)}, f32[2048,512]{1,0:T(8,128)S(1)}, u32[]{:S(2)}) copy-start(f32[2048,512]{1,0:T(8,128)S(1)} %shard_map.50.matrix) | copy-start | bytes 12582916
  60.3 69.8 %copy-start.7 = (f32[64,256]{1,0:T(8,128)S(1)}, f32[64,256]{1,0:T(8,128)}, u32[]{:S(2)}) copy-start(f32[64,256]{1,0:T(8,128)} %panel.1) | copy-start | bytes 196612
  76.9 13.5 %copy-start.8 = (f32[64,256]{1,0:T(8,128)}, f32[64,256]{1,0:T(8,128)S(1)}, u32[]{:S(2)}) copy-start(f32[64,256]{1,0:T(8,128)S(1)} %get-tuple-element.14.refs_0_) | copy-start | bytes 196612
  76.9 4.0 %collective-permute-start.13 = (f32[32,256]{1,0:T(8,128)S(1)}, f32[32,256]{1,0:T(8,128)S(1)}, u32[]{:S(2)}, u32[]{:S(2)}) collective-permute-start(f32[32,256]{1,0:T(8,128)S(1)} %get-tuple-element.15), channel_id=1, source_target_pairs={{0,8},{1,9},{2,10},{3,11},{4,12},{5,13},{6,14},{7,15},{8,0},{9,1},... | collective-permute-start | bytes 98312 | tf_op jit(solution)/shard_map/ppermute | solution.py:58
  78.4 12.0 %collective-permute-start.8 = (f32[64,256]{1,0:T(8,128)S(1)}, f32[64,256]{1,0:T(8,128)S(1)}, u32[]{:S(2)}, u32[]{:S(2)}) collective-permute-start(f32[64,256]{1,0:T(8,128)S(1)} %get-tuple-element.14.refs_0_), channel_id=1, source_target_pairs={{0,0},{32,1},{64,2},{96,3},{128,4},{160,5},{192,6},{224,7},{1,8},{... | collective-permute-start | bytes 196616 | tf_op jit(solution)/shard_map/ppermute | solution.py:264
  80.9 5.4 %collective-permute-start.14 = (f32[32,256]{1,0:T(8,128)S(1)}, f32[32,256]{1,0:T(8,128)S(1)}, u32[]{:S(2)}, u32[]{:S(2)}) collective-permute-start(f32[32,256]{1,0:T(8,128)S(1)} %add.13), channel_id=1, source_target_pairs={{0,16},{1,17},{2,18},{3,19},{4,20},{5,21},{6,22},{7,23},{8,24},{9,... | collective-permute-start | bytes 98312 | tf_op jit(solution)/shard_map/ppermute | solution.py:58
  91.4 26.3 %all-to-all-start.2 = ((f32[8,96,256]{2,1,0:T(8,128)}), f32[8,96,256]{2,1,0:T(8,128)S(1)}, u32[]{:S(2)}, u32[]{:S(2)}) async-start(f32[8,96,256]{2,1,0:T(8,128)} %broadcast_in_dim.7), calls=%async_computation.2 | async-start | bytes 1572864 | tf_op jit(solution)/shard_map/all_to_all | solution.py:44
  94.9 6.4 %collective-permute-start.11 = (f32[64,256]{1,0:T(8,128)}, f32[64,256]{1,0:T(8,128)S(1)}, u32[]{:S(2)}, u32[]{:S(2)}) collective-permute-start(f32[64,256]{1,0:T(8,128)} %copy-done.8), channel_id=1, source_target_pairs={{0,64},{32,96},{64,128},{96,160},{128,192},{160,224},{192,0},{224,... | collective-permute-start | bytes 196616 | tf_op jit(solution)/shard_map/ppermute | solution.py:67
  97.6 6.1 %collective-permute-start.10 = (f32[64,256]{1,0:T(8,128)}, f32[64,256]{1,0:T(8,128)S(1)}, u32[]{:S(2)}, u32[]{:S(2)}) collective-permute-start(f32[64,256]{1,0:T(8,128)} %copy-done.8), channel_id=1, source_target_pairs={{0,128},{32,160},{64,192},{96,224},{128,0},{160,32},{192,64},{224,... | collective-permute-start | bytes 196616 | tf_op jit(solution)/shard_map/ppermute | solution.py:67
  98.8 5.2 %collective-permute-start.9 = (f32[64,256]{1,0:T(8,128)}, f32[64,256]{1,0:T(8,128)S(1)}, u32[]{:S(2)}, u32[]{:S(2)}) collective-permute-start(f32[64,256]{1,0:T(8,128)} %copy-done.8), channel_id=1, source_target_pairs={{0,192},{32,224},{64,0},{96,32},{128,64},{160,96},{192,128},{224,1... | collective-permute-start | bytes 196616 | tf_op jit(solution)/shard_map/ppermute | solution.py:67
  101.3 3.8 %copy-start.10 = (f32[64,256]{1,0:T(8,128)}, f32[64,256]{1,0:T(8,128)S(1)}, u32[]{:S(2)}) copy-start(f32[64,256]{1,0:T(8,128)S(1)} %collective-permute-done.11.refs_3_) | copy-start | bytes 196612
  103.7 1.4 copy-start.12
  103.9 1.2 copy-start.14
  104.8 1.8 %collective-permute-start.12 = (f32[4,64,256]{2,1,0:T(8,128)S(1)}, f32[4,64,256]{2,1,0:T(8,128)S(1)}, u32[]{:S(2)}, u32[]{:S(2)}) collective-permute-start(f32[4,64,256]{2,1,0:T(8,128)S(1)} %pad_maximum_fusion.1), channel_id=1, source_target_pairs={{0,32},{32,0},{64,96},{96,64},{128,160},{160,128},{192,224},{224,1... | collective-permute-start | bytes 786440 | tf_op jit(solution)/shard_map/ppermute | solution.py:74
  106.6 0.7 copy-start.5
  117.7 24.5 %collective-permute-start.21 = (f32[512,256]{1,0:T(8,128)S(1)}, f32[512,256]{1,0:T(8,128)S(1)}, u32[]{:S(2)}, u32[]{:S(2)}) collective-permute-start(f32[512,256]{1,0:T(8,128)S(1)} %bitcast.27), channel_id=1, source_target_pairs={{0,24},{1,25},{2,26},{3,27},{4,28},{5,29},{6,30},{7,31},{8,0},{9,1... | collective-permute-start | bytes 1572872 | tf_op jit(solution)/shard_map/ppermute | solution.py:50
  119.1 23.1 %collective-permute-start.20 = (f32[512,256]{1,0:T(8,128)S(1)}, f32[512,256]{1,0:T(8,128)S(1)}, u32[]{:S(2)}, u32[]{:S(2)}) collective-permute-start(f32[512,256]{1,0:T(8,128)S(1)} %bitcast.28), channel_id=1, source_target_pairs={{0,16},{1,17},{2,18},{3,19},{4,20},{5,21},{6,22},{7,23},{8,24},{9,... | collective-permute-start | bytes 1572872 | tf_op jit(solution)/shard_map/ppermute | solution.py:50
  119.1 26.2 %collective-permute-start.19 = (f32[512,256]{1,0:T(8,128)S(1)}, f32[512,256]{1,0:T(8,128)S(1)}, u32[]{:S(2)}, u32[]{:S(2)}) collective-permute-start(f32[512,256]{1,0:T(8,128)S(1)} %bitcast.29), channel_id=1, source_target_pairs={{0,8},{1,9},{2,10},{3,11},{4,12},{5,13},{6,14},{7,15},{8,16},{9,17... | collective-permute-start | bytes 1572872 | tf_op jit(solution)/shard_map/ppermute | solution.py:50
  120.1 3.9 %collective-permute-start.17 = (f32[32,256]{1,0:T(8,128)S(1)}, f32[32,256]{1,0:T(8,128)S(1)}, u32[]{:S(2)}, u32[]{:S(2)}) collective-permute-start(f32[32,256]{1,0:T(8,128)S(1)} %get-tuple-element.19.refs_5_), channel_id=1, source_target_pairs={{0,64},{32,96},{64,128},{96,160},{128,192},{160,224},{192,0},{224,... | collective-permute-start | bytes 98312 | tf_op jit(solution)/shard_map/ppermute | solution.py:67
  122.4 5.4 %collective-permute-start.16 = (f32[32,256]{1,0:T(8,128)S(1)}, f32[32,256]{1,0:T(8,128)S(1)}, u32[]{:S(2)}, u32[]{:S(2)}) collective-permute-start(f32[32,256]{1,0:T(8,128)S(1)} %get-tuple-element.19.refs_5_), channel_id=1, source_target_pairs={{0,128},{32,160},{64,192},{96,224},{128,0},{160,32},{192,64},{224,... | collective-permute-start | bytes 98312 | tf_op jit(solution)/shard_map/ppermute | solution.py:67
  124.0 4.6 %collective-permute-start.15 = (f32[32,256]{1,0:T(8,128)S(1)}, f32[32,256]{1,0:T(8,128)S(1)}, u32[]{:S(2)}, u32[]{:S(2)}) collective-permute-start(f32[32,256]{1,0:T(8,128)S(1)} %get-tuple-element.19.refs_5_), channel_id=1, source_target_pairs={{0,192},{32,224},{64,0},{96,32},{128,64},{160,96},{192,128},{224,1... | collective-permute-start | bytes 98312 | tf_op jit(solution)/shard_map/ppermute | solution.py:67
  128.6 1.4 collective-permute-start.18
  130.1 1.0 copy-start.4
  131.0 0.9 copy-start.6
  132.0 0.8 copy-start.9
  132.8 0.8 copy-start.11
  133.7 0.8 copy-start.13
  134.5 0.8 copy-start.15
  137.8 2.2 %copy-start.1 = (f32[2048,512]{1,0:T(8,128)S(1)}, f32[2048,512]{1,0:T(8,128)}, u32[]{:S(2)}) copy-start(f32[2048,512]{1,0:T(8,128)} %copy-done) | copy-start | bytes 12582916

commit v6 on v5

--- a/solution.py
+++ b/solution.py
@@ -9,8 +9,9 @@
 Z_GROUPS = [[y * NZ + z for z in range(NZ)] for y in range(NY)]
 WHOLE = pl.BlockSpec(memory_space=pltpu.VMEM)
 SCALARS = pl.BlockSpec(memory_space=pltpu.SMEM)
+MIDDLE = 44
 FREE = pl.CostEstimate(flops=1, bytes_accessed=1, transcendentals=0)
-PARAMS = pltpu.CompilerParams(vmem_limit_bytes=20 << 20)
+PARAMS = pltpu.CompilerParams(vmem_limit_bytes=44 << 20)
 
 
 def after(value, *others):
@@ -52,11 +53,13 @@
     return [value] + [shifted(step) for step in range(1, NY)]
 
 
-def y_sum(value):
-    for bit in (1, 2):
-        perm = [(y * NZ + z, (y ^ bit) * NZ + z) for y in range(NY) for z in range(NZ)]
-        value += lax.ppermute(value, "col", perm)
-    return value
+def z_sum(value):
+    def partner(value, bits):
+        perm = [(y * NZ + z, y * NZ + (z ^ bits)) for y in range(NY) for z in range(NZ)]
+        return lax.ppermute(value, "col", perm)
+
+    value = sum([partner(value, bits) for bits in (1, 2, 3)], value)
+    return value + partner(value, 4)
 
 
 def x_blocks(value):
@@ -156,15 +159,6 @@
     inner[...] = total[chunk.shape[0] :]
 
 
-def split_kernel(parts, block, inner):
-    rows = block.shape[1]
-    block[...] = parts[:, :rows, :]
-    total = parts[0, rows:, :]
-    for k in range(1, parts.shape[0]):
-        total += parts[k, rows:, :]
-    inner[...] = total
-
-
 def middle_kernel(place, factor, panel, home, col_panel, *refs):
     blocks, (left, correction, scaled, small) = refs[:-4], refs[-4:]
     half = NX + 1
@@ -175,6 +169,22 @@
     correction[...] = home[...] - exact(panel[...], kernel, ((1,), (0,)))
     wanted = exact(col_panel[...], kernel + kernel.T, ((1,), (0,)))
     left[...] = scaled[...].reshape(left.shape) - wanted
+
+
+def middle(place, operands, shapes, scratch):
+    def whole(shape):
+        return pl.BlockSpec(shape, lambda step: (0,) * len(shape))
+
+    return pl.pallas_call(
+        middle_kernel,
+        out_shape=[jax.ShapeDtypeStruct(shape, jnp.float32) for shape in shapes],
+        grid=(1,),
+        in_specs=[SCALARS] + [whole(operand.shape) for operand in operands],
+        out_specs=[whole(shape) for shape in shapes],
+        scratch_shapes=scratch,
+        cost_estimate=FREE,
+        compiler_params=pltpu.CompilerParams(vmem_limit_bytes=MIDDLE << 20),
+    )(place, *operands)
 
 
 def first_update_kernel(y_ref, matrix, left, col_panel, own_scaled, *refs):
@@ -262,20 +272,20 @@
     chunk, inner = local(reduce_kernel, pair, (parts,), scalars=0)
 
     home = lax.ppermute(chunk, ("row", "col"), to_home)
-    parts = spread(jnp.concatenate([home, y_sum(inner)]), Z_GROUPS)
+    inner = z_sum(inner)
+    own_scaled = spread(after(home, inner), Z_GROUPS).reshape(block, width)
+    inner = sum(y_blocks(inner))
     scaled = x_blocks(after(chunk, home))
-    scaled += [other_core(scaled)]
-    parts = after(parts, *scaled)
-    pair = [(NZ, rows, width), (depth, width)]
-    own_scaled, inner = local(split_kernel, pair, (parts,), scalars=0)
-    scaleds = y_blocks(own_scaled.reshape(block, width))
+    own_scaled = after(own_scaled, inner, *scaled)
+    scaleds = y_blocks(own_scaled)
 
     small = x_blocks(after(inner, own_scaled))
     small += [other_core(small)]
-    left, correction = local(
-        middle_kernel,
+    scaled += [other_core(scaled)]
+    left, correction = middle(
+        place,
+        (factor, panel, home, col_panel, *scaled, *small),
         [col_panel.shape, home.shape],
-        (place, factor, panel, home, col_panel, *scaled, *small),
         [pltpu.VMEM((nrows, size, width), jnp.float32) for size in (rows, depth)],
     )
     updated = local(

time: 150 us -> 148 us (0.987)
  the two profiles are of different devices: /device:TPU:2 before, /device:TPU:1 now
where the time goes in v6:
time: 148 us; the launch traced here: 147 us
  starting transfers between devices  71.2 us (48%)
  waiting for transfers between devices  33.7 us (23%)
  blocking collectives  16.9 us (11%)
  Pallas kernels  15.8 us (11%)
  local copies, waits for them, and re-layouts  7.86 us (5%)
    all_to_all x1, blocking collectives, per_device(): parts = lax.all_to_all(parts, 'row', 0, 0)  16.9 us
    ppermute x9, starting transfers between devices, shifted(): return lax.ppermute(value, 'row', perm)  16 us
    ppermute x9, starting transfers between devices, shifted(): return lax.ppermute(value, 'col', perm)  15.4 us
    all_to_all x2, starting transfers between devices, spread(): return lax.all_to_all(copies, 'col', 0, 0, axis_index_groups=groups)  13.9 us
    all_to_all x2, waiting for transfers between devices, spread(): return lax.all_to_all(copies, 'col', 0, 0, axis_index_groups=groups)  12 us
    ppermute x9, waiting for transfers between devices, shifted(): return lax.ppermute(value, 'col', perm)  10.3 us
    pallas_call x3, Pallas kernels, local(): pl.pallas_call(kernel, out_shape=[jax.ShapeDtypeStruct(shape, jnp.float32...  8.76 us
    ppermute x1, starting transfers between devices, per_device(): moved = lax.ppermute(panel, ('row', 'col'), to_column)  8.39 us
  transfers between devices with their start and end apart: 29, of which 14 were waited for; matrix products, arithmetic and copies ran while one was open for 1% of the time, Pallas kernels for 6%

profile of v6, /device:TPU:1, one launch (start us, length us, event | category | flops | bytes accessed | tf_op | source)
XLA Modules:
  0.0 147.3 jit_solution(13350716362424182992)
XLA Ops:
  0.6 1.7 %broadcast_in_dim.6 = f32[8,64,256]{2,1,0:T(8,128)} broadcast(f32[64,256]{1,0:T(8,128)} %panel.1), dimensions={1,2} | broadcast | bytes 589824 | tf_op jit(solution)/shard_map/broadcast_in_dim | solution.py:44
  2.3 9.0 %all-to-all-start = ((f32[8,64,256]{2,1,0:T(8,128)}), f32[8,64,256]{2,1,0:T(8,128)S(1)}, u32[]{:S(2)}, u32[]{:S(2)}) async-start(f32[8,64,256]{2,1,0:T(8,128)} %broadcast_in_dim.6), calls=%async_computation | async-start | bytes 1048576 | tf_op jit(solution)/shard_map/all_to_all | solution.py:45
  11.3 8.4 %collective-permute-start = (f32[64,256]{1,0:T(8,128)}, f32[64,256]{1,0:T(8,128)S(1)}, u32[]{:S(2)}, u32[]{:S(2)}) collective-permute-start(f32[64,256]{1,0:T(8,128)} %panel.1), channel_id=1, source_target_pairs={{0,0},{1,32},{2,64},{3,96},{4,128},{5,160},{6,192},{7,224},{8,1},{... | collective-permute-start | bytes 196616 | tf_op jit(solution)/shard_map/ppermute | solution.py:257
  19.7 8.6 %all-to-all-done = f32[8,64,256]{2,1,0:T(8,128)S(1)} async-done(((f32[8,64,256]{2,1,0:T(8,128)}), f32[8,64,256]{2,1,0:T(8,128)S(1)}, u32[]{:S(2)}, u32[]{:S(2)}) %all-to-all-start) | async-done | bytes 524320 | tf_op jit(solution)/shard_map/all_to_all | solution.py:45
  28.3 2.8 %collective-permute-start.7 = (f32[512,256]{1,0:T(8,128)S(1)}, f32[512,256]{1,0:T(8,128)S(1)}, u32[]{:S(2)}, u32[]{:S(2)}) collective-permute-start(f32[512,256]{1,0:T(8,128)S(1)} %bitcast.22), channel_id=1, source_target_pairs={{0,24},{1,25},{2,26},{3,27},{4,28},{5,29},{6,30},{7,31},{8,0},{9,1... | collective-permute-start | bytes 1572872 | tf_op jit(solution)/shard_map/ppermute | solution.py:51
  31.1 2.6 %collective-permute-start.6 = (f32[512,256]{1,0:T(8,128)S(1)}, f32[512,256]{1,0:T(8,128)S(1)}, u32[]{:S(2)}, u32[]{:S(2)}) collective-permute-start(f32[512,256]{1,0:T(8,128)S(1)} %bitcast.23), channel_id=1, source_target_pairs={{0,16},{1,17},{2,18},{3,19},{4,20},{5,21},{6,22},{7,23},{8,24},{9,... | collective-permute-start | bytes 1572872 | tf_op jit(solution)/shard_map/ppermute | solution.py:51
  33.7 0.7 collective-permute-start.5
  34.4 0.0 collective-permute-done.refs_0_
  34.4 1.2 collective-permute-start.3
  35.6 2.5 %collective-permute-start.2 = (f32[64,256]{1,0:T(8,128)S(1)}, f32[64,256]{1,0:T(8,128)S(1)}, u32[]{:S(2)}, u32[]{:S(2)}) collective-permute-start(f32[64,256]{1,0:T(8,128)S(1)} %collective-permute-done.refs_0_), channel_id=1, source_target_pairs={{0,128},{32,160},{64,192},{96,224},{128,0},{160,32},{192,64},{224,... | collective-permute-start | bytes 196616 | tf_op jit(solution)/shard_map/ppermute | solution.py:70
  38.0 1.0 collective-permute-done.3.refs_3_
  39.0 1.3 collective-permute-start.1
  40.2 0.4 collective-permute-done.2.refs_2_
  40.7 1.9 %collective-permute-done.1.refs_1_ = f32[64,256]{1,0:T(8,128)S(1)} collective-permute-done((f32[64,256]{1,0:T(8,128)S(1)}, f32[64,256]{1,0:T(8,128)S(1)}, u32[]{:S(2)}, u32[]{:S(2)}) %collective-permute-start.1) | collective-permute-done | bytes 65568 | tf_op jit(solution)/shard_map/ppermute | solution.py:70
  42.6 3.6 %collective-permute-start.4 = (f32[4,64,256]{2,1,0:T(8,128)S(1)}, f32[4,64,256]{2,1,0:T(8,128)S(1)}, u32[]{:S(2)}, u32[]{:S(2)}) collective-permute-start(f32[4,64,256]{2,1,0:T(8,128)S(1)} %pad_maximum_fusion), channel_id=1, source_target_pairs={{0,32},{32,0},{64,96},{96,64},{128,160},{160,128},{192,224},{224,1... | collective-permute-start | bytes 786440 | tf_op jit(solution)/shard_map/ppermute | solution.py:77
  46.1 0.1 pad_add_fusion.place
  46.2 2.2 %copy-done.1 = f32[2048,512]{1,0:T(8,128)S(1)} copy-done((f32[2048,512]{1,0:T(8,128)S(1)}, f32[2048,512]{1,0:T(8,128)}, u32[]{:S(2)}) %copy-start.1) | copy-done | bytes 4194328
  48.4 0.3 shard_map.50.matrix
  48.7 0.0 copy-start
  48.7 0.6 shard_map.51
  49.3 0.0 collective-permute-done.7.refs_3_
  49.3 0.0 collective-permute-done.6.refs_2_
  49.3 8.3 %collective-permute-done.5.refs_1_ = f32[512,256]{1,0:T(8,128)S(1)} collective-permute-done((f32[512,256]{1,0:T(8,128)S(1)}, f32[512,256]{1,0:T(8,128)S(1)}, u32[]{:S(2)}, u32[]{:S(2)}) %collective-permute-start.5) | collective-permute-done | bytes 524320 | tf_op jit(solution)/shard_map/ppermute | solution.py:51
  57.6 3.7 %shard_map.52 = f32[8,96,256]{2,1,0:T(8,128)S(1)} custom-call(s32[1]{0:T(128)} %bitcast.y_ref, f32[2048,512]{1,0:T(8,128)S(1)} %shard_map.50.matrix, f32[256,256]{1,0:T(8,128)S(1)} %copy-done.2, f32[512,256]{1,0:T(8,128)S(1)} %bitcast.18, f32[512,256]{1,0:T(8,128)S(1)} %bitcast.25, f32[512,256]{1,0:T(8,128)S(1)} %collective-permute-done.5.refs_1_, ...), custom_call_target="tpu_custom_call" | custom-call | flops 1 | bytes 1 | tf_op jit(solution)/shard_map/pallas_call | solution.py:106
  61.3 0.0 copy-start.3
  61.3 16.9 %all_to_all.15.parts = f32[8,96,256]{2,1,0:T(8,128)S(1)} all-to-all(f32[8,96,256]{2,1,0:T(8,128)S(1)} %shard_map.52), channel_id=1, replica_groups=mesh['row'=8,'col'=32] {'row'}, dimensions={0} | all-to-all | bytes 1572864 | tf_op jit(solution)/shard_map/all_to_all | solution.py:270
  78.3 0.7 shard_map.53
  78.9 0.0 collective-permute-start.15
  78.9 0.0 collective-permute-start.14
  78.9 3.5 %collective-permute-start.13 = (f32[32,256]{1,0:T(8,128)S(1)}, f32[32,256]{1,0:T(8,128)S(1)}, u32[]{:S(2)}, u32[]{:S(2)}) collective-permute-start(f32[32,256]{1,0:T(8,128)S(1)} %get-tuple-element.14), channel_id=1, source_target_pairs={{0,1},{1,0},{2,3},{3,2},{4,5},{5,4},{6,7},{7,6},{8,9},{9,8},{10,11... | collective-permute-start | bytes 98312 | tf_op jit(solution)/shard_map/ppermute | solution.py:59
  82.5 3.4 %collective-permute-start.8 = (f32[64,256]{1,0:T(8,128)}, f32[64,256]{1,0:T(8,128)S(1)}, u32[]{:S(2)}, u32[]{:S(2)}) collective-permute-start(f32[64,256]{1,0:T(8,128)} %get-tuple-element.13.refs_0_), channel_id=1, source_target_pairs={{0,0},{32,1},{64,2},{96,3},{128,4},{160,5},{192,6},{224,7},{1,8},{... | collective-permute-start | bytes 196616 | tf_op jit(solution)/shard_map/ppermute | solution.py:274
  85.9 0.0 collective-permute-done.15
  85.9 2.8 %collective-permute-start.16 = (f32[32,256]{1,0:T(8,128)S(1)}, f32[32,256]{1,0:T(8,128)S(1)}, u32[]{:S(2)}, u32[]{:S(2)}) collective-permute-start(f32[32,256]{1,0:T(8,128)S(1)} %add_add_fusion.1), channel_id=1, source_target_pairs={{0,4},{1,5},{2,6},{3,7},{4,0},{5,1},{6,2},{7,3},{8,12},{9,13},{10,... | collective-permute-start | bytes 98312 | tf_op jit(solution)/shard_map/ppermute | solution.py:59
  88.7 4.1 %collective-permute-done.16 = f32[32,256]{1,0:T(8,128)S(1)} collective-permute-done((f32[32,256]{1,0:T(8,128)S(1)}, f32[32,256]{1,0:T(8,128)S(1)}, u32[]{:S(2)}, u32[]{:S(2)}) %collective-permute-start.16) | collective-permute-done | bytes 32800 | tf_op jit(solution)/shard_map/ppermute | solution.py:59
  92.8 0.0 copy-start.4
  92.8 0.8 broadcast_in_dim.7
  93.6 4.9 %all-to-all-start.2 = ((f32[8,64,256]{2,1,0:T(8,128)}), f32[8,64,256]{2,1,0:T(8,128)S(1)}, u32[]{:S(2)}, u32[]{:S(2)}) async-start(f32[8,64,256]{2,1,0:T(8,128)} %broadcast_in_dim.7), calls=%async_computation.2 | async-start | bytes 1048576 | tf_op jit(solution)/shard_map/all_to_all | solution.py:45
  98.5 3.3 %collective-permute-start.19 = (f32[32,256]{1,0:T(8,128)S(1)}, f32[32,256]{1,0:T(8,128)S(1)}, u32[]{:S(2)}, u32[]{:S(2)}) collective-permute-start(f32[32,256]{1,0:T(8,128)S(1)} %add.31), channel_id=1, source_target_pairs={{0,24},{1,25},{2,26},{3,27},{4,28},{5,29},{6,30},{7,31},{8,0},{9,1... | collective-permute-start | bytes 98312 | tf_op jit(solution)/shard_map/ppermute | solution.py:51
  101.9 0.3 collective-permute-start.18
  102.2 0.6 collective-permute-start.17
  102.8 3.6 %collective-permute-start.10 = (f32[64,256]{1,0:T(8,128)}, f32[64,256]{1,0:T(8,128)S(1)}, u32[]{:S(2)}, u32[]{:S(2)}) collective-permute-start(f32[64,256]{1,0:T(8,128)} %get-tuple-element.13.refs_0_), channel_id=1, source_target_pairs={{0,128},{32,160},{64,192},{96,224},{128,0},{160,32},{192,64},{224,... | collective-permute-start | bytes 196616 | tf_op jit(solution)/shard_map/ppermute | solution.py:70
  106.4 0.1 collective-permute-done.17
  106.5 1.0 collective-permute-done.11.refs_3_
  107.5 1.8 %collective-permute-done.10.refs_2_ = f32[64,256]{1,0:T(8,128)S(1)} collective-permute-done((f32[64,256]{1,0:T(8,128)}, f32[64,256]{1,0:T(8,128)S(1)}, u32[]{:S(2)}, u32[]{:S(2)}) %collective-permute-start.10) | collective-permute-done | bytes 65568 | tf_op jit(solution)/shard_map/ppermute | solution.py:70
  109.3 0.6 copy-done.8
  109.9 0.1 collective-permute-done.9.refs_1_
  110.1 3.4 %all-to-all-done.2 = f32[8,64,256]{2,1,0:T(8,128)S(1)} async-done(((f32[8,64,256]{2,1,0:T(8,128)}), f32[8,64,256]{2,1,0:T(8,128)S(1)}, u32[]{:S(2)}, u32[]{:S(2)}) %all-to-all-start.2) | async-done | bytes 524320 | tf_op jit(solution)/shard_map/all_to_all | solution.py:45
  113.5 3.9 %collective-permute-start.26 = (f32[512,256]{1,0:T(8,128)S(1)}, f32[512,256]{1,0:T(8,128)S(1)}, u32[]{:S(2)}, u32[]{:S(2)}) collective-permute-start(f32[512,256]{1,0:T(8,128)S(1)} %bitcast.27), channel_id=1, source_target_pairs={{0,24},{1,25},{2,26},{3,27},{4,28},{5,29},{6,30},{7,31},{8,0},{9,1... | collective-permute-start | bytes 1572872 | tf_op jit(solution)/shard_map/ppermute | solution.py:51
  117.4 0.3 collective-permute-start.25
  117.7 0.9 collective-permute-start.24
  118.6 5.6 %collective-permute-start.21 = (f32[32,256]{1,0:T(8,128)S(1)}, f32[32,256]{1,0:T(8,128)S(1)}, u32[]{:S(2)}, u32[]{:S(2)}) collective-permute-start(f32[32,256]{1,0:T(8,128)S(1)} %add_add_fusion.refs_5_), channel_id=1, source_target_pairs={{0,128},{32,160},{64,192},{96,224},{128,0},{160,32},{192,64},{224,... | collective-permute-start | bytes 98312 | tf_op jit(solution)/shard_map/ppermute | solution.py:70
  124.2 0.1 collective-permute-done.22.refs_8_
  124.3 1.8 %collective-permute-start.20 = (f32[32,256]{1,0:T(8,128)S(1)}, f32[32,256]{1,0:T(8,128)S(1)}, u32[]{:S(2)}, u32[]{:S(2)}) collective-permute-start(f32[32,256]{1,0:T(8,128)S(1)} %add_add_fusion.refs_5_), channel_id=1, source_target_pairs={{0,192},{32,224},{64,0},{96,32},{128,64},{160,96},{192,128},{224,1... | collective-permute-start | bytes 98312 | tf_op jit(solution)/shard_map/ppermute | solution.py:70
  126.1 1.0 pad_maximum_fusion.1
  127.1 2.3 %collective-permute-start.12 = (f32[4,64,256]{2,1,0:T(8,128)S(1)}, f32[4,64,256]{2,1,0:T(8,128)S(1)}, u32[]{:S(2)}, u32[]{:S(2)}) collective-permute-start(f32[4,64,256]{2,1,0:T(8,128)S(1)} %pad_maximum_fusion.1), channel_id=1, source_target_pairs={{0,32},{32,0},{64,96},{96,64},{128,160},{160,128},{192,224},{224,1... | collective-permute-start | bytes 786440 | tf_op jit(solution)/shard_map/ppermute | solution.py:77
  129.4 1.9 %collective-permute-start.23 = (f32[4,32,256]{2,1,0:T(8,128)S(1)}, f32[4,32,256]{2,1,0:T(8,128)S(1)}, u32[]{:S(2)}, u32[]{:S(2)}) collective-permute-start(f32[4,32,256]{2,1,0:T(8,128)S(1)} %pad_maximum_fusion.2), channel_id=1, source_target_pairs={{0,32},{32,0},{64,96},{96,64},{128,160},{160,128},{192,224},{224,1... | collective-permute-start | bytes 393224 | tf_op jit(solution)/shard_map/ppermute | solution.py:77
  131.3 1.0 collective-permute-done.23.refs_9_
  132.3 0.8 copy-done.5
  133.1 0.8 copy-done.7
  133.9 0.8 copy-done.9
  134.8 2.8 %shard_map.54 = (f32[512,256]{1,0:T(8,128)S(1)}, f32[64,256]{1,0:T(8,128)}) custom-call(s32[2]{0:T(128)S(1)} %pad_add_fusion.place, f32[256,256]{1,0:T(8,128)S(1)} %copy-done.2, f32[64,256]{1,0:T(8,128)S(1)} %copy-done.3, f32[64,256]{1,0:T(8,128)S(1)} %copy-done.5, f32[512,256]{1,0:T(8,128)S(1)} %bitcast.19, f32[64,256]{1,0:T(8,128)} %get-tuple-element.13.refs_0_, ...), custom_call_target="tpu_custom_call" | custom-call | flops 1 | bytes 1 | tf_op jit(solution)/shard_map/pallas_call | solution.py:178
  137.6 4.4 %shard_map.55.matrix = f32[2048,512]{1,0:T(8,128)S(1)} custom-call(s32[1]{0:T(128)} %bitcast.y_ref, f32[2048,512]{1,0:T(8,128)} %copy-done, f32[512,256]{1,0:T(8,128)S(1)} %get-tuple-element.18.left, f32[512,256]{1,0:T(8,128)S(1)} %bitcast.20, f32[512,256]{1,0:T(8,128)S(1)} %bitcast.30, f32[512,256]{1,0:T(8,128)S(1)} %bitcast.26, ...), custom_call_target="tpu_custom_call" | custom-call | flops 1 | bytes 1 | tf_op jit(solution)/shard_map/pallas_call | solution.py:106
  142.1 1.9 %collective-permute-done.24.refs_0_ = f32[512,256]{1,0:T(8,128)S(1)} collective-permute-done((f32[512,256]{1,0:T(8,128)S(1)}, f32[512,256]{1,0:T(8,128)S(1)}, u32[]{:S(2)}, u32[]{:S(2)}) %collective-permute-start.24) | collective-permute-done | bytes 524320 | tf_op jit(solution)/shard_map/ppermute | solution.py:51
  144.0 3.4 %shard_map.56 = f32[2048,512]{1,0:T(8,128)} custom-call(s32[1]{0:T(128)} %bitcast.y_ref, f32[2048,512]{1,0:T(8,128)S(1)} %shard_map.55.matrix, f32[512,256]{1,0:T(8,128)S(1)} %bitcast.21, f32[512,256]{1,0:T(8,128)S(1)} %collective-permute-done.24.refs_0_, f32[512,256]{1,0:T(8,128)S(1)} %collective-permute-done.25.refs_1_, ...), custom_call_target="tpu_custom_call" | custom-call | flops 1 | bytes 1 | tf_op jit(solution)/shard_map/pallas_call | solution.py:230
  (31 shorter events, 0.1 us)
Async XLA Ops:
  2.3 26.0 %all-to-all-start = ((f32[8,64,256]{2,1,0:T(8,128)}), f32[8,64,256]{2,1,0:T(8,128)S(1)}, u32[]{:S(2)}, u32[]{:S(2)}) async-start(f32[8,64,256]{2,1,0:T(8,128)} %broadcast_in_dim.6), calls=%async_computation | async-start | bytes 1048576 | tf_op jit(solution)/shard_map/all_to_all | solution.py:45
  11.3 23.0 %collective-permute-start = (f32[64,256]{1,0:T(8,128)}, f32[64,256]{1,0:T(8,128)S(1)}, u32[]{:S(2)}, u32[]{:S(2)}) collective-permute-start(f32[64,256]{1,0:T(8,128)} %panel.1), channel_id=1, source_target_pairs={{0,0},{1,32},{2,64},{3,96},{4,128},{5,160},{6,192},{7,224},{8,1},{... | collective-permute-start | bytes 196616 | tf_op jit(solution)/shard_map/ppermute | solution.py:257
  28.3 21.0 %collective-permute-start.7 = (f32[512,256]{1,0:T(8,128)S(1)}, f32[512,256]{1,0:T(8,128)S(1)}, u32[]{:S(2)}, u32[]{:S(2)}) collective-permute-start(f32[512,256]{1,0:T(8,128)S(1)} %bitcast.22), channel_id=1, source_target_pairs={{0,24},{1,25},{2,26},{3,27},{4,28},{5,29},{6,30},{7,31},{8,0},{9,1... | collective-permute-start | bytes 1572872 | tf_op jit(solution)/shard_map/ppermute | solution.py:51
  31.1 18.3 %collective-permute-start.6 = (f32[512,256]{1,0:T(8,128)S(1)}, f32[512,256]{1,0:T(8,128)S(1)}, u32[]{:S(2)}, u32[]{:S(2)}) collective-permute-start(f32[512,256]{1,0:T(8,128)S(1)} %bitcast.23), channel_id=1, source_target_pairs={{0,16},{1,17},{2,18},{3,19},{4,20},{5,21},{6,22},{7,23},{8,24},{9,... | collective-permute-start | bytes 1572872 | tf_op jit(solution)/shard_map/ppermute | solution.py:51
  33.7 24.0 %collective-permute-start.5 = (f32[512,256]{1,0:T(8,128)S(1)}, f32[512,256]{1,0:T(8,128)S(1)}, u32[]{:S(2)}, u32[]{:S(2)}) collective-permute-start(f32[512,256]{1,0:T(8,128)S(1)} %bitcast.24), channel_id=1, source_target_pairs={{0,8},{1,9},{2,10},{3,11},{4,12},{5,13},{6,14},{7,15},{8,16},{9,17... | collective-permute-start | bytes 1572872 | tf_op jit(solution)/shard_map/ppermute | solution.py:51
  34.4 4.6 %collective-permute-start.3 = (f32[64,256]{1,0:T(8,128)S(1)}, f32[64,256]{1,0:T(8,128)S(1)}, u32[]{:S(2)}, u32[]{:S(2)}) collective-permute-start(f32[64,256]{1,0:T(8,128)S(1)} %collective-permute-done.refs_0_), channel_id=1, source_target_pairs={{0,64},{32,96},{64,128},{96,160},{128,192},{160,224},{192,0},{224,... | collective-permute-start | bytes 196616 | tf_op jit(solution)/shard_map/ppermute | solution.py:70
  35.6 5.1 %collective-permute-start.2 = (f32[64,256]{1,0:T(8,128)S(1)}, f32[64,256]{1,0:T(8,128)S(1)}, u32[]{:S(2)}, u32[]{:S(2)}) collective-permute-start(f32[64,256]{1,0:T(8,128)S(1)} %collective-permute-done.refs_0_), channel_id=1, source_target_pairs={{0,128},{32,160},{64,192},{96,224},{128,0},{160,32},{192,64},{224,... | collective-permute-start | bytes 196616 | tf_op jit(solution)/shard_map/ppermute | solution.py:70
  39.0 3.6 %collective-permute-start.1 = (f32[64,256]{1,0:T(8,128)S(1)}, f32[64,256]{1,0:T(8,128)S(1)}, u32[]{:S(2)}, u32[]{:S(2)}) collective-permute-start(f32[64,256]{1,0:T(8,128)S(1)} %collective-permute-done.refs_0_), channel_id=1, source_target_pairs={{0,192},{32,224},{64,0},{96,32},{128,64},{160,96},{192,128},{224,1... | collective-permute-start | bytes 196616 | tf_op jit(solution)/shard_map/ppermute | solution.py:70
  42.6 6.2 %collective-permute-start.4 = (f32[4,64,256]{2,1,0:T(8,128)S(1)}, f32[4,64,256]{2,1,0:T(8,128)S(1)}, u32[]{:S(2)}, u32[]{:S(2)}) collective-permute-start(f32[4,64,256]{2,1,0:T(8,128)S(1)} %pad_maximum_fusion), channel_id=1, source_target_pairs={{0,32},{32,0},{64,96},{96,64},{128,160},{160,128},{192,224},{224,1... | collective-permute-start | bytes 786440 | tf_op jit(solution)/shard_map/ppermute | solution.py:77
  46.2 2.2 %copy-start.1 = (f32[2048,512]{1,0:T(8,128)S(1)}, f32[2048,512]{1,0:T(8,128)}, u32[]{:S(2)}) copy-start(f32[2048,512]{1,0:T(8,128)} %matrix) | copy-start | bytes 12582916
  48.4 9.2 %copy-start.2 = (f32[256,256]{1,0:T(8,128)S(1)}, f32[256,256]{1,0:T(8,128)}, u32[]{:S(2)}) copy-start(f32[256,256]{1,0:T(8,128)} %factor.3) | copy-start | bytes 786436
  48.7 12.6 %copy-start = (f32[2048,512]{1,0:T(8,128)}, f32[2048,512]{1,0:T(8,128)S(1)}, u32[]{:S(2)}) copy-start(f32[2048,512]{1,0:T(8,128)S(1)} %shard_map.50.matrix) | copy-start | bytes 12582916
  61.3 70.9 %copy-start.3 = (f32[64,256]{1,0:T(8,128)S(1)}, f32[64,256]{1,0:T(8,128)}, u32[]{:S(2)}) copy-start(f32[64,256]{1,0:T(8,128)} %panel.1) | copy-start | bytes 196612
  78.9 6.9 %collective-permute-start.15 = (f32[32,256]{1,0:T(8,128)S(1)}, f32[32,256]{1,0:T(8,128)S(1)}, u32[]{:S(2)}, u32[]{:S(2)}) collective-permute-start(f32[32,256]{1,0:T(8,128)S(1)} %get-tuple-element.14), channel_id=1, source_target_pairs={{0,3},{1,2},{2,1},{3,0},{4,7},{5,6},{6,5},{7,4},{8,11},{9,10},{10,... | collective-permute-start | bytes 98312 | tf_op jit(solution)/shard_map/ppermute | solution.py:59
  78.9 7.0 %collective-permute-start.14 = (f32[32,256]{1,0:T(8,128)S(1)}, f32[32,256]{1,0:T(8,128)S(1)}, u32[]{:S(2)}, u32[]{:S(2)}) collective-permute-start(f32[32,256]{1,0:T(8,128)S(1)} %get-tuple-element.14), channel_id=1, source_target_pairs={{0,2},{1,3},{2,0},{3,1},{4,6},{5,7},{6,4},{7,5},{8,10},{9,11},{10,... | collective-permute-start | bytes 98312 | tf_op jit(solution)/shard_map/ppermute | solution.py:59
  78.9 7.0 %collective-permute-start.13 = (f32[32,256]{1,0:T(8,128)S(1)}, f32[32,256]{1,0:T(8,128)S(1)}, u32[]{:S(2)}, u32[]{:S(2)}) collective-permute-start(f32[32,256]{1,0:T(8,128)S(1)} %get-tuple-element.14), channel_id=1, source_target_pairs={{0,1},{1,0},{2,3},{3,2},{4,5},{5,4},{6,7},{7,6},{8,9},{9,8},{10,11... | collective-permute-start | bytes 98312 | tf_op jit(solution)/shard_map/ppermute | solution.py:59
  82.5 10.3 %collective-permute-start.8 = (f32[64,256]{1,0:T(8,128)}, f32[64,256]{1,0:T(8,128)S(1)}, u32[]{:S(2)}, u32[]{:S(2)}) collective-permute-start(f32[64,256]{1,0:T(8,128)} %get-tuple-element.13.refs_0_), channel_id=1, source_target_pairs={{0,0},{32,1},{64,2},{96,3},{128,4},{160,5},{192,6},{224,7},{1,8},{... | collective-permute-start | bytes 196616 | tf_op jit(solution)/shard_map/ppermute | solution.py:274
  85.9 6.9 %collective-permute-start.16 = (f32[32,256]{1,0:T(8,128)S(1)}, f32[32,256]{1,0:T(8,128)S(1)}, u32[]{:S(2)}, u32[]{:S(2)}) collective-permute-start(f32[32,256]{1,0:T(8,128)S(1)} %add_add_fusion.1), channel_id=1, source_target_pairs={{0,4},{1,5},{2,6},{3,7},{4,0},{5,1},{6,2},{7,3},{8,12},{9,13},{10,... | collective-permute-start | bytes 98312 | tf_op jit(solution)/shard_map/ppermute | solution.py:59
  92.8 0.8 copy-start.4
  93.6 19.8 %all-to-all-start.2 = ((f32[8,64,256]{2,1,0:T(8,128)}), f32[8,64,256]{2,1,0:T(8,128)S(1)}, u32[]{:S(2)}, u32[]{:S(2)}) async-start(f32[8,64,256]{2,1,0:T(8,128)} %broadcast_in_dim.7), calls=%async_computation.2 | async-start | bytes 1048576 | tf_op jit(solution)/shard_map/all_to_all | solution.py:45
  98.5 7.9 %collective-permute-start.19 = (f32[32,256]{1,0:T(8,128)S(1)}, f32[32,256]{1,0:T(8,128)S(1)}, u32[]{:S(2)}, u32[]{:S(2)}) collective-permute-start(f32[32,256]{1,0:T(8,128)S(1)} %add.31), channel_id=1, source_target_pairs={{0,24},{1,25},{2,26},{3,27},{4,28},{5,29},{6,30},{7,31},{8,0},{9,1... | collective-permute-start | bytes 98312 | tf_op jit(solution)/shard_map/ppermute | solution.py:51
  101.9 4.6 %collective-permute-start.18 = (f32[32,256]{1,0:T(8,128)S(1)}, f32[32,256]{1,0:T(8,128)S(1)}, u32[]{:S(2)}, u32[]{:S(2)}) collective-permute-start(f32[32,256]{1,0:T(8,128)S(1)} %add.31), channel_id=1, source_target_pairs={{0,16},{1,17},{2,18},{3,19},{4,20},{5,21},{6,22},{7,23},{8,24},{9,... | collective-permute-start | bytes 98312 | tf_op jit(solution)/shard_map/ppermute | solution.py:51
  102.2 4.3 %collective-permute-start.17 = (f32[32,256]{1,0:T(8,128)S(1)}, f32[32,256]{1,0:T(8,128)S(1)}, u32[]{:S(2)}, u32[]{:S(2)}) collective-permute-start(f32[32,256]{1,0:T(8,128)S(1)} %add.31), channel_id=1, source_target_pairs={{0,8},{1,9},{2,10},{3,11},{4,12},{5,13},{6,14},{7,15},{8,16},{9,17... | collective-permute-start | bytes 98312 | tf_op jit(solution)/shard_map/ppermute | solution.py:51
  102.8 4.7 %collective-permute-start.11 = (f32[64,256]{1,0:T(8,128)}, f32[64,256]{1,0:T(8,128)S(1)}, u32[]{:S(2)}, u32[]{:S(2)}) collective-permute-start(f32[64,256]{1,0:T(8,128)} %get-tuple-element.13.refs_0_), channel_id=1, source_target_pairs={{0,64},{32,96},{64,128},{96,160},{128,192},{160,224},{192,0},{224,... | collective-permute-start | bytes 196616 | tf_op jit(solution)/shard_map/ppermute | solution.py:70
  102.8 6.5 %collective-permute-start.10 = (f32[64,256]{1,0:T(8,128)}, f32[64,256]{1,0:T(8,128)S(1)}, u32[]{:S(2)}, u32[]{:S(2)}) collective-permute-start(f32[64,256]{1,0:T(8,128)} %get-tuple-element.13.refs_0_), channel_id=1, source_target_pairs={{0,128},{32,160},{64,192},{96,224},{128,0},{160,32},{192,64},{224,... | collective-permute-start | bytes 196616 | tf_op jit(solution)/shard_map/ppermute | solution.py:70
  106.4 3.6 %collective-permute-start.9 = (f32[64,256]{1,0:T(8,128)}, f32[64,256]{1,0:T(8,128)}, u32[]{:S(2)}, u32[]{:S(2)}) collective-permute-start(f32[64,256]{1,0:T(8,128)} %get-tuple-element.13.refs_0_), channel_id=1, source_target_pairs={{0,192},{32,224},{64,0},{96,32},{128,64},{160,96},{192,128},{224,1... | collective-permute-start | bytes 196616 | tf_op jit(solution)/shard_map/ppermute | solution.py:70
  107.5 1.8 %copy-start.6 = (f32[64,256]{1,0:T(8,128)}, f32[64,256]{1,0:T(8,128)S(1)}, u32[]{:S(2)}) copy-start(f32[64,256]{1,0:T(8,128)S(1)} %collective-permute-done.11.refs_3_) | copy-start | bytes 196612
  109.3 0.6 copy-start.8
  113.5 28.6 %collective-permute-start.26 = (f32[512,256]{1,0:T(8,128)S(1)}, f32[512,256]{1,0:T(8,128)S(1)}, u32[]{:S(2)}, u32[]{:S(2)}) collective-permute-start(f32[512,256]{1,0:T(8,128)S(1)} %bitcast.27), channel_id=1, source_target_pairs={{0,24},{1,25},{2,26},{3,27},{4,28},{5,29},{6,30},{7,31},{8,0},{9,1... | collective-permute-start | bytes 1572872 | tf_op jit(solution)/shard_map/ppermute | solution.py:51
  117.4 24.7 %collective-permute-start.25 = (f32[512,256]{1,0:T(8,128)S(1)}, f32[512,256]{1,0:T(8,128)S(1)}, u32[]{:S(2)}, u32[]{:S(2)}) collective-permute-start(f32[512,256]{1,0:T(8,128)S(1)} %bitcast.28), channel_id=1, source_target_pairs={{0,16},{1,17},{2,18},{3,19},{4,20},{5,21},{6,22},{7,23},{8,24},{9,... | collective-permute-start | bytes 1572872 | tf_op jit(solution)/shard_map/ppermute | solution.py:51
  117.7 26.3 %collective-permute-start.24 = (f32[512,256]{1,0:T(8,128)S(1)}, f32[512,256]{1,0:T(8,128)S(1)}, u32[]{:S(2)}, u32[]{:S(2)}) collective-permute-start(f32[512,256]{1,0:T(8,128)S(1)} %bitcast.29), channel_id=1, source_target_pairs={{0,8},{1,9},{2,10},{3,11},{4,12},{5,13},{6,14},{7,15},{8,16},{9,17... | collective-permute-start | bytes 1572872 | tf_op jit(solution)/shard_map/ppermute | solution.py:51
  118.6 5.8 %collective-permute-start.22 = (f32[32,256]{1,0:T(8,128)S(1)}, f32[32,256]{1,0:T(8,128)S(1)}, u32[]{:S(2)}, u32[]{:S(2)}) collective-permute-start(f32[32,256]{1,0:T(8,128)S(1)} %add_add_fusion.refs_5_), channel_id=1, source_target_pairs={{0,64},{32,96},{64,128},{96,160},{128,192},{160,224},{192,0},{224,... | collective-permute-start | bytes 98312 | tf_op jit(solution)/shard_map/ppermute | solution.py:70
  118.6 8.5 %collective-permute-start.21 = (f32[32,256]{1,0:T(8,128)S(1)}, f32[32,256]{1,0:T(8,128)S(1)}, u32[]{:S(2)}, u32[]{:S(2)}) collective-permute-start(f32[32,256]{1,0:T(8,128)S(1)} %add_add_fusion.refs_5_), channel_id=1, source_target_pairs={{0,128},{32,160},{64,192},{96,224},{128,0},{160,32},{192,64},{224,... | collective-permute-start | bytes 98312 | tf_op jit(solution)/shard_map/ppermute | solution.py:70
  124.3 5.0 %collective-permute-start.20 = (f32[32,256]{1,0:T(8,128)S(1)}, f32[32,256]{1,0:T(8,128)S(1)}, u32[]{:S(2)}, u32[]{:S(2)}) collective-permute-start(f32[32,256]{1,0:T(8,128)S(1)} %add_add_fusion.refs_5_), channel_id=1, source_target_pairs={{0,192},{32,224},{64,0},{96,32},{128,64},{160,96},{192,128},{224,1... | collective-permute-start | bytes 98312 | tf_op jit(solution)/shard_map/ppermute | solution.py:70
  127.1 4.2 %collective-permute-start.12 = (f32[4,64,256]{2,1,0:T(8,128)S(1)}, f32[4,64,256]{2,1,0:T(8,128)S(1)}, u32[]{:S(2)}, u32[]{:S(2)}) collective-permute-start(f32[4,64,256]{2,1,0:T(8,128)S(1)} %pad_maximum_fusion.1), channel_id=1, source_target_pairs={{0,32},{32,0},{64,96},{96,64},{128,160},{160,128},{192,224},{224,1... | collective-permute-start | bytes 786440 | tf_op jit(solution)/shard_map/ppermute | solution.py:77
  129.4 2.9 %collective-permute-start.23 = (f32[4,32,256]{2,1,0:T(8,128)S(1)}, f32[4,32,256]{2,1,0:T(8,128)S(1)}, u32[]{:S(2)}, u32[]{:S(2)}) collective-permute-start(f32[4,32,256]{2,1,0:T(8,128)S(1)} %pad_maximum_fusion.2), channel_id=1, source_target_pairs={{0,32},{32,0},{64,96},{96,64},{128,160},{160,128},{192,224},{224,1... | collective-permute-start | bytes 393224 | tf_op jit(solution)/shard_map/ppermute | solution.py:77
  132.3 0.8 copy-start.5
  133.1 0.8 copy-start.7
  133.9 0.8 copy-start.9

commit v7 on v6

--- a/solution.py
+++ b/solution.py
@@ -53,13 +53,37 @@
     return [value] + [shifted(step) for step in range(1, NY)]
 
 
-def z_sum(value):
-    def partner(value, bits):
-        perm = [(y * NZ + z, y * NZ + (z ^ bits)) for y in range(NY) for z in range(NZ)]
-        return lax.ppermute(value, "col", perm)
-
-    value = sum([partner(value, bits) for bits in (1, 2, 3)], value)
-    return value + partner(value, 4)
+def z_partner(value, bit):
+    perm = [(y * NZ + z, y * NZ + (z ^ bit)) for y in range(NY) for z in range(NZ)]
+    return lax.ppermute(value, "col", perm)
+
+
+def z_scatter(value, z):
+    for bit in (4, 2, 1):
+        half = value.shape[0] // 2
+        upper = z // bit % 2
+        mine = lax.dynamic_slice_in_dim(value, upper * half, half, 0)
+        theirs = lax.dynamic_slice_in_dim(value, (1 - upper) * half, half, 0)
+        value = mine + z_partner(theirs, bit)
+    return value
+
+
+def z_gather(value):
+    for bit in (1, 2, 4):
+        value = jnp.concatenate([value, z_partner(value, bit)])
+    return value
+
+
+def y_sum_step(value, bit):
+    perm = [(y * NZ + z, (y ^ bit) * NZ + z) for y in range(NY) for z in range(NZ)]
+    return value + lax.ppermute(value, "col", perm)
+
+
+def row_sum(value):
+    for bit in (1, 2, 4):
+        perm = [(i, i ^ bit) for i in range(NX * CORES)]
+        value += lax.ppermute(value, "row", perm)
+    return value
 
 
 def x_blocks(value):
@@ -135,7 +159,7 @@
 
 
 def product_kernel(y_ref, matrix, factor, col_panel, *refs):
-    panels, out, total = refs[:NY], refs[NY], refs[NY + 1]
+    panels, (out, inner, total) = refs[:NY], refs[NY:]
     for k in range(NY):
         block = matrix[rows_of(y_ref, k, panels[k].shape[0]), :]
         piece = three_pass(halves(panels[k][...]), halves(block), ((0,), (0,)))
@@ -143,27 +167,23 @@
             total[...] = piece
         else:
             total[...] += piece
-    count, rows, width = out.shape
-    depth = width // count
     scaled = exact(total[...], factor[...], ((0,), (0,)))
-    inner = exact(col_panel[...], scaled, ((0,), (0,)))
-    out[:, : rows - depth, :] = scaled.reshape(count, rows - depth, width)
-    out[:, rows - depth :, :] = inner.reshape(count, depth, width)
-
-
-def reduce_kernel(parts, chunk, inner):
+    out[...] = scaled.reshape(out.shape)
+    inner[...] = exact(col_panel[...], scaled, ((0,), (0,)))
+
+
+def reduce_kernel(parts, chunk):
     total = parts[0]
     for k in range(1, parts.shape[0]):
         total += parts[k]
-    chunk[...] = total[: chunk.shape[0]]
-    inner[...] = total[chunk.shape[0] :]
+    chunk[...] = total
 
 
 def middle_kernel(place, factor, panel, home, col_panel, *refs):
-    blocks, (left, correction, scaled, small) = refs[:-4], refs[-4:]
-    half = NX + 1
+    blocks, gathered, (left, correction, scaled, small) = refs[:-5], refs[-5], refs[-4:]
     assemble(place, blocks[:NX], blocks[NX], scaled)
-    assemble(place, blocks[half : half + NX], blocks[half + NX], small)
+    for k in range(NZ):
+        small[place[2 + k]] = gathered[k]
     width = panel.shape[1]
     kernel = 0.5 * exact(factor[...], small[...].reshape(width, width), ((0,), (0,)))
     correction[...] = home[...] - exact(panel[...], kernel, ((1,), (0,)))
@@ -249,7 +269,8 @@
     block = NZ * rows
     row = lax.axis_index("row")
     y = (lax.axis_index("col") // NZ).reshape(1)
-    place = jnp.stack([row // CORES, row % CORES])
+    z = lax.axis_index("col") % NZ
+    place = jnp.stack([row // CORES, row % CORES] + [z ^ k for k in range(NZ)])
     total = nrows * ncols
     to_column = [(g, g % nrows * ncols + g // nrows) for g in range(total)]
     to_home = [(b, a) for a, b in to_column]
@@ -260,33 +281,32 @@
     col_panel = row_blocks(place, mine, other_core(mine)).reshape(nrows * rows, width)
     staged = stage(after(matrix, moved))
 
-    depth = width // nrows
-    parts = local(
+    shares, inner = local(
         product_kernel,
-        (nrows, rows + depth, width),
+        [(nrows, rows, width), (width, width)],
         (y, staged, factor, col_panel, *panels),
         [pltpu.VMEM((width, nrows * rows), jnp.float32)],
     )
-    parts = lax.all_to_all(parts, "row", 0, 0)
-    pair = [(rows, width), (depth, width)]
-    chunk, inner = local(reduce_kernel, pair, (parts,), scalars=0)
+    parts = lax.all_to_all(shares, "row", 0, 0)
+    inner = z_scatter(inner, z)
+    chunk = local(reduce_kernel, (rows, width), (parts,), scalars=0)
 
     home = lax.ppermute(chunk, ("row", "col"), to_home)
-    inner = z_sum(inner)
+    inner = y_sum_step(inner, 1)
     own_scaled = spread(after(home, inner), Z_GROUPS).reshape(block, width)
-    inner = sum(y_blocks(inner))
+    inner = row_sum(y_sum_step(inner, 2))
     scaled = x_blocks(after(chunk, home))
     own_scaled = after(own_scaled, inner, *scaled)
     scaleds = y_blocks(own_scaled)
 
-    small = x_blocks(after(inner, own_scaled))
-    small += [other_core(small)]
+    depth = width // NZ
+    small = z_gather(after(inner, own_scaled)).reshape(NZ, depth, width)
     scaled += [other_core(scaled)]
     left, correction = middle(
         place,
-        (factor, panel, home, col_panel, *scaled, *small),
+        (factor, panel, home, col_panel, *scaled, small),
         [col_panel.shape, home.shape],
-        [pltpu.VMEM((nrows, size, width), jnp.float32) for size in (rows, depth)],
+        [pltpu.VMEM(shape, jnp.float32) for shape in ((nrows, rows, width), small.shape)],
     )
     updated = local(
         first_update_kernel, matrix.shape, (y, staged, left, col_panel, scaleds[0], *panels)

time: 148 us -> 160 us (1.081)
  the two profiles are of different devices: /device:TPU:1 before, /device:TPU:2 now
where the time goes in v7:
time: 160 us; the launch traced here: 159 us
  waiting for transfers between devices  65.9 us (41%)
  starting transfers between devices  56.5 us (35%)
  Pallas kernels  15.2 us (10%)
  local copies, waits for them, and re-layouts  12 us (8%)
  other arithmetic  7.89 us (5%)
    ppermute x6, waiting for transfers between devices, z_partner(): return lax.ppermute(value, 'col', perm)  24.7 us
    all_to_all x2, waiting for transfers between devices, spread(): return lax.all_to_all(copies, 'col', 0, 0, axis_index_groups=groups)  13.1 us
    all_to_all x2, starting transfers between devices, spread(): return lax.all_to_all(copies, 'col', 0, 0, axis_index_groups=groups)  12 us
    ppermute x6, starting transfers between devices, shifted(): return lax.ppermute(value, 'col', perm)  10.1 us
    ppermute x6, waiting for transfers between devices, shifted(): return lax.ppermute(value, 'col', perm)  10 us
    ppermute x6, starting transfers between devices, shifted(): return lax.ppermute(value, 'row', perm)  9.89 us
    ppermute x6, starting transfers between devices, z_partner(): return lax.ppermute(value, 'col', perm)  8.64 us
    unnamed x28, local copies, waits for them, and re-layouts  8.13 us
  transfers between devices with their start and end apart: 30, of which 15 were waited for; matrix products, arithmetic and copies ran while one was open for 5% of the time, Pallas kernels for 5%

profile of v7, /device:TPU:2, one launch (start us, length us, event | category | flops | bytes accessed | tf_op | source)
XLA Modules:
  0.0 158.5 jit_solution(14082978362507897158)
XLA Ops:
  0.6 1.7 %broadcast_in_dim.6 = f32[8,64,256]{2,1,0:T(8,128)} broadcast(f32[64,256]{1,0:T(8,128)} %panel.1), dimensions={1,2} | broadcast | bytes 589824 | tf_op jit(solution)/shard_map/broadcast_in_dim | solution.py:44
  2.3 8.5 %all-to-all-start = ((f32[8,64,256]{2,1,0:T(8,128)}), f32[8,64,256]{2,1,0:T(8,128)S(1)}, u32[]{:S(2)}, u32[]{:S(2)}) async-start(f32[8,64,256]{2,1,0:T(8,128)} %broadcast_in_dim.6), calls=%async_computation | async-start | bytes 1048576 | tf_op jit(solution)/shard_map/all_to_all | solution.py:45
  10.8 3.4 %collective-permute-start = (f32[64,256]{1,0:T(8,128)}, f32[64,256]{1,0:T(8,128)S(1)}, u32[]{:S(2)}, u32[]{:S(2)}) collective-permute-start(f32[64,256]{1,0:T(8,128)} %panel.1), channel_id=1, source_target_pairs={{0,0},{1,32},{2,64},{3,96},{4,128},{5,160},{6,192},{7,224},{8,1},{... | collective-permute-start | bytes 196616 | tf_op jit(solution)/shard_map/ppermute | solution.py:278
  14.2 13.1 %all-to-all-done = f32[8,64,256]{2,1,0:T(8,128)S(1)} async-done(((f32[8,64,256]{2,1,0:T(8,128)}), f32[8,64,256]{2,1,0:T(8,128)S(1)}, u32[]{:S(2)}, u32[]{:S(2)}) %all-to-all-start) | async-done | bytes 524320 | tf_op jit(solution)/shard_map/all_to_all | solution.py:45
  27.3 3.2 %collective-permute-start.7 = (f32[512,256]{1,0:T(8,128)S(1)}, f32[512,256]{1,0:T(8,128)S(1)}, u32[]{:S(2)}, u32[]{:S(2)}) collective-permute-start(f32[512,256]{1,0:T(8,128)S(1)} %bitcast.27), channel_id=1, source_target_pairs={{0,24},{1,25},{2,26},{3,27},{4,28},{5,29},{6,30},{7,31},{8,0},{9,1... | collective-permute-start | bytes 1572872 | tf_op jit(solution)/shard_map/ppermute | solution.py:51
  30.5 2.9 %collective-permute-start.6 = (f32[512,256]{1,0:T(8,128)S(1)}, f32[512,256]{1,0:T(8,128)S(1)}, u32[]{:S(2)}, u32[]{:S(2)}) collective-permute-start(f32[512,256]{1,0:T(8,128)S(1)} %bitcast.28), channel_id=1, source_target_pairs={{0,16},{1,17},{2,18},{3,19},{4,20},{5,21},{6,22},{7,23},{8,24},{9,... | collective-permute-start | bytes 1572872 | tf_op jit(solution)/shard_map/ppermute | solution.py:51
  33.4 1.0 collective-permute-start.5
  34.4 1.5 collective-permute-start.3
  35.9 1.1 collective-permute-start.2
  37.0 2.0 %collective-permute-done.3.refs_3_ = f32[64,256]{1,0:T(8,128)S(1)} collective-permute-done((f32[64,256]{1,0:T(8,128)S(1)}, f32[64,256]{1,0:T(8,128)S(1)}, u32[]{:S(2)}, u32[]{:S(2)}) %collective-permute-start.3) | collective-permute-done | bytes 65568 | tf_op jit(solution)/shard_map/ppermute | solution.py:94
  39.0 1.8 %collective-permute-start.1 = (f32[64,256]{1,0:T(8,128)S(1)}, f32[64,256]{1,0:T(8,128)S(1)}, u32[]{:S(2)}, u32[]{:S(2)}) collective-permute-start(f32[64,256]{1,0:T(8,128)S(1)} %collective-permute-done.refs_0_), channel_id=1, source_target_pairs={{0,192},{32,224},{64,0},{96,32},{128,64},{160,96},{192,128},{224,1... | collective-permute-start | bytes 196616 | tf_op jit(solution)/shard_map/ppermute | solution.py:94
  40.8 0.9 collective-permute-done.2.refs_2_
  41.7 1.5 collective-permute-done.1.refs_1_
  43.5 2.2 %copy-done.1 = f32[2048,512]{1,0:T(8,128)S(1)} copy-done((f32[2048,512]{1,0:T(8,128)S(1)}, f32[2048,512]{1,0:T(8,128)}, u32[]{:S(2)}) %copy-start.1) | copy-done | bytes 4194328
  45.7 0.3 shard_map.50.matrix
  46.0 0.6 shard_map.51
  46.9 9.8 %collective-permute-done.5.refs_1_ = f32[512,256]{1,0:T(8,128)S(1)} collective-permute-done((f32[512,256]{1,0:T(8,128)S(1)}, f32[512,256]{1,0:T(8,128)S(1)}, u32[]{:S(2)}, u32[]{:S(2)}) %collective-permute-start.5) | collective-permute-done | bytes 524320 | tf_op jit(solution)/shard_map/ppermute | solution.py:51
  56.6 3.7 %shard_map.52 = (f32[8,64,256]{2,1,0:T(8,128)S(1)}, f32[256,256]{1,0:T(8,128)S(1)}) custom-call(s32[1]{0:T(128)} %bitcast.y_ref, f32[2048,512]{1,0:T(8,128)S(1)} %shard_map.50.matrix, f32[256,256]{1,0:T(8,128)S(1)} %copy-done.2, f32[512,256]{1,0:T(8,128)S(1)} %bitcast.23, f32[512,256]{1,0:T(8,128)S(1)} %bitcast.30, ...), custom_call_target="tpu_custom_call" | custom-call | flops 1 | bytes 1 | tf_op jit(solution)/shard_map/pallas_call | solution.py:130
  60.3 0.8 copy-done.3
  61.1 0.7 copy-done.7
  61.8 0.7 constant_dynamic-slice_fusion.2
  62.5 4.8 %all-to-all-start.1 = ((f32[8,64,256]{2,1,0:T(8,128)}), f32[8,64,256]{2,1,0:T(8,128)S(1)}, u32[]{:S(2)}, u32[]{:S(2)}) async-start(f32[8,64,256]{2,1,0:T(8,128)} %copy-done.3), calls=%async_computation.1 | async-start | bytes 1048576 | tf_op jit(solution)/shard_map/all_to_all | solution.py:290
  67.3 7.6 %collective-permute-done.13 = f32[128,256]{1,0:T(8,128)} collective-permute-done((f32[128,256]{1,0:T(8,128)}, f32[128,256]{1,0:T(8,128)}, u32[]{:S(2)}, u32[]{:S(2)}) %collective-permute-start.13) | collective-permute-done | bytes 131104 | tf_op jit(solution)/shard_map/ppermute | solution.py:58
  75.0 1.0 dynamic-slice_add_fusion
  75.9 0.6 copy-done.12
  76.6 5.2 %collective-permute-done.14 = f32[64,256]{1,0:T(8,128)} collective-permute-done((f32[64,256]{1,0:T(8,128)S(1)}, f32[64,256]{1,0:T(8,128)}, u32[]{:S(2)}, u32[]{:S(2)}) %collective-permute-start.14) | collective-permute-done | bytes 65568 | tf_op jit(solution)/shard_map/ppermute | solution.py:58
  81.9 0.9 dynamic-slice_add_fusion.1
  82.8 0.6 constant_dynamic-slice_fusion
  83.4 2.3 %collective-permute-start.8 = (f32[64,256]{1,0:T(8,128)S(1)}, f32[64,256]{1,0:T(8,128)S(1)}, u32[]{:S(2)}, u32[]{:S(2)}) collective-permute-start(f32[64,256]{1,0:T(8,128)S(1)} %shard_map.53.refs_0_), channel_id=1, source_target_pairs={{0,0},{32,1},{64,2},{96,3},{128,4},{160,5},{192,6},{224,7},{1,8},{... | collective-permute-start | bytes 196616 | tf_op jit(solution)/shard_map/ppermute | solution.py:294
  85.7 1.9 %collective-permute-done.15 = f32[32,256]{1,0:T(8,128)} collective-permute-done((f32[32,256]{1,0:T(8,128)}, f32[32,256]{1,0:T(8,128)}, u32[]{:S(2)}, u32[]{:S(2)}) %collective-permute-start.15) | collective-permute-done | bytes 32800 | tf_op jit(solution)/shard_map/ppermute | solution.py:58
  87.6 0.8 dynamic-slice_add_fusion.2
  88.4 4.9 %collective-permute-done.16 = f32[32,256]{1,0:T(8,128)S(1)} collective-permute-done((f32[32,256]{1,0:T(8,128)S(1)}, f32[32,256]{1,0:T(8,128)S(1)}, u32[]{:S(2)}, u32[]{:S(2)}) %collective-permute-start.16) | collective-permute-done | bytes 32800 | tf_op jit(solution)/shard_map/ppermute | solution.py:79
  93.3 0.6 add.77
  93.9 0.8 broadcast_in_dim.7
  94.8 3.5 %all-to-all-start.2 = ((f32[8,64,256]{2,1,0:T(8,128)}), f32[8,64,256]{2,1,0:T(8,128)S(1)}, u32[]{:S(2)}, u32[]{:S(2)}) async-start(f32[8,64,256]{2,1,0:T(8,128)} %broadcast_in_dim.7), calls=%async_computation.2 | async-start | bytes 1048576 | tf_op jit(solution)/shard_map/all_to_all | solution.py:45
  98.3 2.8 %collective-permute-start.17 = (f32[32,256]{1,0:T(8,128)}, f32[32,256]{1,0:T(8,128)S(1)}, u32[]{:S(2)}, u32[]{:S(2)}) collective-permute-start(f32[32,256]{1,0:T(8,128)} %add.77), channel_id=1, source_target_pairs={{0,16},{1,17},{2,18},{3,19},{4,20},{5,21},{6,22},{7,23},{8,24},{9,... | collective-permute-start | bytes 98312 | tf_op jit(solution)/shard_map/ppermute | solution.py:79
  101.1 2.9 %collective-permute-done.17 = f32[32,256]{1,0:T(8,128)S(1)} collective-permute-done((f32[32,256]{1,0:T(8,128)}, f32[32,256]{1,0:T(8,128)S(1)}, u32[]{:S(2)}, u32[]{:S(2)}) %collective-permute-start.17) | collective-permute-done | bytes 32800 | tf_op jit(solution)/shard_map/ppermute | solution.py:79
  104.0 0.8 add.78
  104.8 1.2 collective-permute-done.18
  106.0 1.5 collective-permute-start.19
  107.5 2.6 %collective-permute-start.11 = (f32[64,256]{1,0:T(8,128)S(1)}, f32[64,256]{1,0:T(8,128)S(1)}, u32[]{:S(2)}, u32[]{:S(2)}) collective-permute-start(f32[64,256]{1,0:T(8,128)S(1)} %shard_map.53.refs_0_), channel_id=1, source_target_pairs={{0,64},{32,96},{64,128},{96,160},{128,192},{160,224},{192,0},{224,... | collective-permute-start | bytes 196616 | tf_op jit(solution)/shard_map/ppermute | solution.py:94
  110.3 2.6 %collective-permute-start.9 = (f32[64,256]{1,0:T(8,128)S(1)}, f32[64,256]{1,0:T(8,128)}, u32[]{:S(2)}, u32[]{:S(2)}) collective-permute-start(f32[64,256]{1,0:T(8,128)S(1)} %shard_map.53.refs_0_), channel_id=1, source_target_pairs={{0,192},{32,224},{64,0},{96,32},{128,64},{160,96},{192,128},{224,1... | collective-permute-start | bytes 196616 | tf_op jit(solution)/shard_map/ppermute | solution.py:94
  113.0 0.9 collective-permute-start.20
  113.8 4.6 %collective-permute-done.20 = f32[32,256]{1,0:T(8,128)S(1)} collective-permute-done((f32[32,256]{1,0:T(8,128)S(1)}, f32[32,256]{1,0:T(8,128)S(1)}, u32[]{:S(2)}, u32[]{:S(2)}) %collective-permute-start.20) | collective-permute-done | bytes 32800 | tf_op jit(solution)/shard_map/ppermute | solution.py:85
  118.5 0.6 add.81
  119.1 0.6 copy-done.8
  119.7 0.6 copy-done.10
  120.3 2.1 %collective-permute-start.21 = (f32[32,256]{1,0:T(8,128)}, f32[32,256]{1,0:T(8,128)S(1)}, u32[]{:S(2)}, u32[]{:S(2)}) collective-permute-start(f32[32,256]{1,0:T(8,128)} %add.81), channel_id=1, source_target_pairs={{0,1},{1,0},{2,3},{3,2},{4,5},{5,4},{6,7},{7,6},{8,9},{9,8},{10,11... | collective-permute-start | bytes 98312 | tf_op jit(solution)/shard_map/ppermute | solution.py:58
  122.5 1.6 %collective-permute-start.25 = (f32[512,256]{1,0:T(8,128)S(1)}, f32[512,256]{1,0:T(8,128)S(1)}, u32[]{:S(2)}, u32[]{:S(2)}) collective-permute-start(f32[512,256]{1,0:T(8,128)S(1)} %bitcast.33), channel_id=1, source_target_pairs={{0,16},{1,17},{2,18},{3,19},{4,20},{5,21},{6,22},{7,23},{8,24},{9,... | collective-permute-start | bytes 1572872 | tf_op jit(solution)/shard_map/ppermute | solution.py:51
  124.1 1.4 collective-permute-start.24
  125.5 0.8 pad_maximum_fusion.4
  126.3 2.4 %collective-permute-start.22 = (f32[64,256]{1,0:T(8,128)S(1)}, f32[64,256]{1,0:T(8,128)S(1)}, u32[]{:S(2)}, u32[]{:S(2)}) collective-permute-start(f32[64,256]{1,0:T(8,128)S(1)} %pad_maximum_fusion.4), channel_id=1, source_target_pairs={{0,2},{1,3},{2,0},{3,1},{4,6},{5,7},{6,4},{7,5},{8,10},{9,11},{10,... | collective-permute-start | bytes 196616 | tf_op jit(solution)/shard_map/ppermute | solution.py:58
  128.7 0.9 pad_maximum_fusion.1
  129.7 2.5 %collective-permute-done.22 = f32[64,256]{1,0:T(8,128)S(1)} collective-permute-done((f32[64,256]{1,0:T(8,128)S(1)}, f32[64,256]{1,0:T(8,128)S(1)}, u32[]{:S(2)}, u32[]{:S(2)}) %collective-permute-start.22) | collective-permute-done | bytes 65568 | tf_op jit(solution)/shard_map/ppermute | solution.py:58
  132.2 0.8 pad_maximum_fusion.3
  132.9 4.1 %collective-permute-start.23 = (f32[128,256]{1,0:T(8,128)S(1)}, f32[128,256]{1,0:T(8,128)S(1)}, u32[]{:S(2)}, u32[]{:S(2)}) collective-permute-start(f32[128,256]{1,0:T(8,128)S(1)} %pad_maximum_fusion.3), channel_id=1, source_target_pairs={{0,4},{1,5},{2,6},{3,7},{4,0},{5,1},{6,2},{7,3},{8,12},{9,13},{10,... | collective-permute-start | bytes 393224 | tf_op jit(solution)/shard_map/ppermute | solution.py:58
  137.1 7.5 %collective-permute-done.23 = f32[128,256]{1,0:T(8,128)S(1)} collective-permute-done((f32[128,256]{1,0:T(8,128)S(1)}, f32[128,256]{1,0:T(8,128)S(1)}, u32[]{:S(2)}, u32[]{:S(2)}) %collective-permute-start.23) | collective-permute-done | bytes 131104 | tf_op jit(solution)/shard_map/ppermute | solution.py:58
  144.5 0.8 pad_maximum_fusion.2
  145.4 0.8 copy-done.6
  146.2 0.8 copy-done.9
  147.0 0.8 copy-done.11
  147.9 2.8 %shard_map.54 = (f32[512,256]{1,0:T(8,128)S(1)}, f32[64,256]{1,0:T(8,128)}) custom-call(s32[10]{0:T(128)S(1)} %stack.73.place, f32[256,256]{1,0:T(8,128)S(1)} %copy-done.2, f32[64,256]{1,0:T(8,128)S(1)} %copy-done.4, f32[64,256]{1,0:T(8,128)S(1)} %copy-done.6, f32[512,256]{1,0:T(8,128)S(1)} %bitcast.24, f32[64,256]{1,0:T(8,128)S(1)} %shard_map.53.refs_0_, ...), custom_call_target="tpu_custom_call" | custom-call | flops 1 | bytes 1 | tf_op jit(solution)/shard_map/pallas_call | solution.py:198
  150.6 4.4 %shard_map.55.matrix = f32[2048,512]{1,0:T(8,128)S(1)} custom-call(s32[1]{0:T(128)} %bitcast.y_ref, f32[2048,512]{1,0:T(8,128)} %copy-done, f32[512,256]{1,0:T(8,128)S(1)} %get-tuple-element.18.left, f32[512,256]{1,0:T(8,128)S(1)} %bitcast.25, f32[512,256]{1,0:T(8,128)S(1)} %bitcast.35, f32[512,256]{1,0:T(8,128)S(1)} %bitcast.31, ...), custom_call_target="tpu_custom_call" | custom-call | flops 1 | bytes 1 | tf_op jit(solution)/shard_map/pallas_call | solution.py:130
  155.1 3.4 %shard_map.56 = f32[2048,512]{1,0:T(8,128)} custom-call(s32[1]{0:T(128)} %bitcast.y_ref, f32[2048,512]{1,0:T(8,128)S(1)} %shard_map.55.matrix, f32[512,256]{1,0:T(8,128)S(1)} %bitcast.26, f32[512,256]{1,0:T(8,128)S(1)} %collective-permute-done.24.refs_0_, f32[512,256]{1,0:T(8,128)S(1)} %collective-permute-done.25.refs_1_, ...), custom_call_target="tpu_custom_call" | custom-call | flops 1 | bytes 1 | tf_op jit(solution)/shard_map/pallas_call | solution.py:250
  (50 shorter events, 0.9 us)
Async XLA Ops:
  2.3 25.0 %all-to-all-start = ((f32[8,64,256]{2,1,0:T(8,128)}), f32[8,64,256]{2,1,0:T(8,128)S(1)}, u32[]{:S(2)}, u32[]{:S(2)}) async-start(f32[8,64,256]{2,1,0:T(8,128)} %broadcast_in_dim.6), calls=%async_computation | async-start | bytes 1048576 | tf_op jit(solution)/shard_map/all_to_all | solution.py:45
  10.8 23.6 %collective-permute-start = (f32[64,256]{1,0:T(8,128)}, f32[64,256]{1,0:T(8,128)S(1)}, u32[]{:S(2)}, u32[]{:S(2)}) collective-permute-start(f32[64,256]{1,0:T(8,128)} %panel.1), channel_id=1, source_target_pairs={{0,0},{1,32},{2,64},{3,96},{4,128},{5,160},{6,192},{7,224},{8,1},{... | collective-permute-start | bytes 196616 | tf_op jit(solution)/shard_map/ppermute | solution.py:278
  27.3 19.3 %collective-permute-start.7 = (f32[512,256]{1,0:T(8,128)S(1)}, f32[512,256]{1,0:T(8,128)S(1)}, u32[]{:S(2)}, u32[]{:S(2)}) collective-permute-start(f32[512,256]{1,0:T(8,128)S(1)} %bitcast.27), channel_id=1, source_target_pairs={{0,24},{1,25},{2,26},{3,27},{4,28},{5,29},{6,30},{7,31},{8,0},{9,1... | collective-permute-start | bytes 1572872 | tf_op jit(solution)/shard_map/ppermute | solution.py:51
  30.5 16.4 %collective-permute-start.6 = (f32[512,256]{1,0:T(8,128)S(1)}, f32[512,256]{1,0:T(8,128)S(1)}, u32[]{:S(2)}, u32[]{:S(2)}) collective-permute-start(f32[512,256]{1,0:T(8,128)S(1)} %bitcast.28), channel_id=1, source_target_pairs={{0,16},{1,17},{2,18},{3,19},{4,20},{5,21},{6,22},{7,23},{8,24},{9,... | collective-permute-start | bytes 1572872 | tf_op jit(solution)/shard_map/ppermute | solution.py:51
  33.4 23.2 %collective-permute-start.5 = (f32[512,256]{1,0:T(8,128)S(1)}, f32[512,256]{1,0:T(8,128)S(1)}, u32[]{:S(2)}, u32[]{:S(2)}) collective-permute-start(f32[512,256]{1,0:T(8,128)S(1)} %bitcast.29), channel_id=1, source_target_pairs={{0,8},{1,9},{2,10},{3,11},{4,12},{5,13},{6,14},{7,15},{8,16},{9,17... | collective-permute-start | bytes 1572872 | tf_op jit(solution)/shard_map/ppermute | solution.py:51
  34.4 4.6 %collective-permute-start.3 = (f32[64,256]{1,0:T(8,128)S(1)}, f32[64,256]{1,0:T(8,128)S(1)}, u32[]{:S(2)}, u32[]{:S(2)}) collective-permute-start(f32[64,256]{1,0:T(8,128)S(1)} %collective-permute-done.refs_0_), channel_id=1, source_target_pairs={{0,64},{32,96},{64,128},{96,160},{128,192},{160,224},{192,0},{224,... | collective-permute-start | bytes 196616 | tf_op jit(solution)/shard_map/ppermute | solution.py:94
  35.9 5.8 %collective-permute-start.2 = (f32[64,256]{1,0:T(8,128)S(1)}, f32[64,256]{1,0:T(8,128)S(1)}, u32[]{:S(2)}, u32[]{:S(2)}) collective-permute-start(f32[64,256]{1,0:T(8,128)S(1)} %collective-permute-done.refs_0_), channel_id=1, source_target_pairs={{0,128},{32,160},{64,192},{96,224},{128,0},{160,32},{192,64},{224,... | collective-permute-start | bytes 196616 | tf_op jit(solution)/shard_map/ppermute | solution.py:94
  39.0 4.3 %collective-permute-start.1 = (f32[64,256]{1,0:T(8,128)S(1)}, f32[64,256]{1,0:T(8,128)S(1)}, u32[]{:S(2)}, u32[]{:S(2)}) collective-permute-start(f32[64,256]{1,0:T(8,128)S(1)} %collective-permute-done.refs_0_), channel_id=1, source_target_pairs={{0,192},{32,224},{64,0},{96,32},{128,64},{160,96},{192,128},{224,1... | collective-permute-start | bytes 196616 | tf_op jit(solution)/shard_map/ppermute | solution.py:94
  43.3 2.8 %collective-permute-start.4 = (f32[4,64,256]{2,1,0:T(8,128)S(1)}, f32[4,64,256]{2,1,0:T(8,128)S(1)}, u32[]{:S(2)}, u32[]{:S(2)}) collective-permute-start(f32[4,64,256]{2,1,0:T(8,128)S(1)} %pad_maximum_fusion), channel_id=1, source_target_pairs={{0,32},{32,0},{64,96},{96,64},{128,160},{160,128},{192,224},{224,1... | collective-permute-start | bytes 786440 | tf_op jit(solution)/shard_map/ppermute | solution.py:101
  43.5 2.2 %copy-start.1 = (f32[2048,512]{1,0:T(8,128)S(1)}, f32[2048,512]{1,0:T(8,128)}, u32[]{:S(2)}) copy-start(f32[2048,512]{1,0:T(8,128)} %matrix) | copy-start | bytes 12582916
  45.7 10.9 %copy-start.2 = (f32[256,256]{1,0:T(8,128)S(1)}, f32[256,256]{1,0:T(8,128)}, u32[]{:S(2)}) copy-start(f32[256,256]{1,0:T(8,128)} %factor.3) | copy-start | bytes 786436
  46.0 16.5 %copy-start = (f32[2048,512]{1,0:T(8,128)}, f32[2048,512]{1,0:T(8,128)S(1)}, u32[]{:S(2)}) copy-start(f32[2048,512]{1,0:T(8,128)S(1)} %shard_map.50.matrix) | copy-start | bytes 12582916
  60.3 0.8 copy-start.3
  61.1 0.7 copy-start.7
  61.1 84.2 %copy-start.4 = (f32[64,256]{1,0:T(8,128)S(1)}, f32[64,256]{1,0:T(8,128)}, u32[]{:S(2)}) copy-start(f32[64,256]{1,0:T(8,128)} %panel.1) | copy-start | bytes 196612
  62.5 12.5 %collective-permute-start.13 = (f32[128,256]{1,0:T(8,128)}, f32[128,256]{1,0:T(8,128)}, u32[]{:S(2)}, u32[]{:S(2)}) collective-permute-start(f32[128,256]{1,0:T(8,128)} %constant_dynamic-slice_fusion.2), channel_id=1, source_target_pairs={{0,4},{1,5},{2,6},{3,7},{4,0},{5,1},{6,2},{7,3},{8,12},{9,13},{10,... | collective-permute-start | bytes 393224 | tf_op jit(solution)/shard_map/ppermute | solution.py:58
  62.5 20.9 %all-to-all-start.1 = ((f32[8,64,256]{2,1,0:T(8,128)}), f32[8,64,256]{2,1,0:T(8,128)S(1)}, u32[]{:S(2)}, u32[]{:S(2)}) async-start(f32[8,64,256]{2,1,0:T(8,128)} %copy-done.3), calls=%async_computation.1 | async-start | bytes 1048576 | tf_op jit(solution)/shard_map/all_to_all | solution.py:290
  75.9 0.7 copy-start.12
  76.6 5.3 %collective-permute-start.14 = (f32[64,256]{1,0:T(8,128)S(1)}, f32[64,256]{1,0:T(8,128)}, u32[]{:S(2)}, u32[]{:S(2)}) collective-permute-start(f32[64,256]{1,0:T(8,128)S(1)} %constant_dynamic-slice_fusion.1), channel_id=1, source_target_pairs={{0,2},{1,3},{2,0},{3,1},{4,6},{5,7},{6,4},{7,5},{8,10},{9,11},{10,... | collective-permute-start | bytes 196616 | tf_op jit(solution)/shard_map/ppermute | solution.py:58
  82.8 0.6 copy-start.13
  83.4 4.2 %collective-permute-start.15 = (f32[32,256]{1,0:T(8,128)}, f32[32,256]{1,0:T(8,128)}, u32[]{:S(2)}, u32[]{:S(2)}) collective-permute-start(f32[32,256]{1,0:T(8,128)} %constant_dynamic-slice_fusion), channel_id=1, source_target_pairs={{0,1},{1,0},{2,3},{3,2},{4,5},{5,4},{6,7},{7,6},{8,9},{9,8},{10,11... | collective-permute-start | bytes 98312 | tf_op jit(solution)/shard_map/ppermute | solution.py:58
  83.4 10.5 %collective-permute-start.8 = (f32[64,256]{1,0:T(8,128)S(1)}, f32[64,256]{1,0:T(8,128)S(1)}, u32[]{:S(2)}, u32[]{:S(2)}) collective-permute-start(f32[64,256]{1,0:T(8,128)S(1)} %shard_map.53.refs_0_), channel_id=1, source_target_pairs={{0,0},{32,1},{64,2},{96,3},{128,4},{160,5},{192,6},{224,7},{1,8},{... | collective-permute-start | bytes 196616 | tf_op jit(solution)/shard_map/ppermute | solution.py:294
  88.4 4.9 %collective-permute-start.16 = (f32[32,256]{1,0:T(8,128)S(1)}, f32[32,256]{1,0:T(8,128)S(1)}, u32[]{:S(2)}, u32[]{:S(2)}) collective-permute-start(f32[32,256]{1,0:T(8,128)S(1)} %dynamic-slice_add_fusion.2), channel_id=1, source_target_pairs={{0,8},{1,9},{2,10},{3,11},{4,12},{5,13},{6,14},{7,15},{8,0},{9,1},... | collective-permute-start | bytes 98312 | tf_op jit(solution)/shard_map/ppermute | solution.py:79
  93.9 0.8 copy-start.5
  94.8 25.6 %all-to-all-start.2 = ((f32[8,64,256]{2,1,0:T(8,128)}), f32[8,64,256]{2,1,0:T(8,128)S(1)}, u32[]{:S(2)}, u32[]{:S(2)}) async-start(f32[8,64,256]{2,1,0:T(8,128)} %broadcast_in_dim.7), calls=%async_computation.2 | async-start | bytes 1048576 | tf_op jit(solution)/shard_map/all_to_all | solution.py:45
  98.3 5.7 %collective-permute-start.17 = (f32[32,256]{1,0:T(8,128)}, f32[32,256]{1,0:T(8,128)S(1)}, u32[]{:S(2)}, u32[]{:S(2)}) collective-permute-start(f32[32,256]{1,0:T(8,128)} %add.77), channel_id=1, source_target_pairs={{0,16},{1,17},{2,18},{3,19},{4,20},{5,21},{6,22},{7,23},{8,24},{9,... | collective-permute-start | bytes 98312 | tf_op jit(solution)/shard_map/ppermute | solution.py:79
  104.8 1.2 collective-permute-start.18
  106.0 7.0 %collective-permute-start.19 = (f32[32,256]{1,0:T(8,128)S(1)}, f32[32,256]{1,0:T(8,128)S(1)}, u32[]{:S(2)}, u32[]{:S(2)}) collective-permute-start(f32[32,256]{1,0:T(8,128)S(1)} %add.79), channel_id=1, source_target_pairs={{0,64},{32,96},{64,0},{96,32},{128,192},{160,224},{192,128},{224,1... | collective-permute-start | bytes 98312 | tf_op jit(solution)/shard_map/ppermute | solution.py:85
  107.5 11.6 %collective-permute-start.11 = (f32[64,256]{1,0:T(8,128)S(1)}, f32[64,256]{1,0:T(8,128)S(1)}, u32[]{:S(2)}, u32[]{:S(2)}) collective-permute-start(f32[64,256]{1,0:T(8,128)S(1)} %shard_map.53.refs_0_), channel_id=1, source_target_pairs={{0,64},{32,96},{64,128},{96,160},{128,192},{160,224},{192,0},{224,... | collective-permute-start | bytes 196616 | tf_op jit(solution)/shard_map/ppermute | solution.py:94
  110.1 9.0 %collective-permute-start.10 = (f32[64,256]{1,0:T(8,128)S(1)}, f32[64,256]{1,0:T(8,128)S(1)}, u32[]{:S(2)}, u32[]{:S(2)}) collective-permute-start(f32[64,256]{1,0:T(8,128)S(1)} %shard_map.53.refs_0_), channel_id=1, source_target_pairs={{0,128},{32,160},{64,192},{96,224},{128,0},{160,32},{192,64},{224,... | collective-permute-start | bytes 196616 | tf_op jit(solution)/shard_map/ppermute | solution.py:94
  110.3 10.0 %collective-permute-start.9 = (f32[64,256]{1,0:T(8,128)S(1)}, f32[64,256]{1,0:T(8,128)}, u32[]{:S(2)}, u32[]{:S(2)}) collective-permute-start(f32[64,256]{1,0:T(8,128)S(1)} %shard_map.53.refs_0_), channel_id=1, source_target_pairs={{0,192},{32,224},{64,0},{96,32},{128,64},{160,96},{192,128},{224,1... | collective-permute-start | bytes 196616 | tf_op jit(solution)/shard_map/ppermute | solution.py:94
  113.0 5.5 %collective-permute-start.20 = (f32[32,256]{1,0:T(8,128)S(1)}, f32[32,256]{1,0:T(8,128)S(1)}, u32[]{:S(2)}, u32[]{:S(2)}) collective-permute-start(f32[32,256]{1,0:T(8,128)S(1)} %add.80), channel_id=1, source_target_pairs={{0,128},{32,160},{64,192},{96,224},{128,0},{160,32},{192,64},{224,... | collective-permute-start | bytes 98312 | tf_op jit(solution)/shard_map/ppermute | solution.py:85
  119.1 0.6 copy-start.8
  119.7 0.6 copy-start.10
  120.3 5.2 %collective-permute-start.21 = (f32[32,256]{1,0:T(8,128)}, f32[32,256]{1,0:T(8,128)S(1)}, u32[]{:S(2)}, u32[]{:S(2)}) collective-permute-start(f32[32,256]{1,0:T(8,128)} %add.81), channel_id=1, source_target_pairs={{0,1},{1,0},{2,3},{3,2},{4,5},{5,4},{6,7},{7,6},{8,9},{9,8},{10,11... | collective-permute-start | bytes 98312 | tf_op jit(solution)/shard_map/ppermute | solution.py:58
  122.5 32.6 %collective-permute-start.26 = (f32[512,256]{1,0:T(8,128)S(1)}, f32[512,256]{1,0:T(8,128)S(1)}, u32[]{:S(2)}, u32[]{:S(2)}) collective-permute-start(f32[512,256]{1,0:T(8,128)S(1)} %bitcast.32), channel_id=1, source_target_pairs={{0,24},{1,25},{2,26},{3,27},{4,28},{5,29},{6,30},{7,31},{8,0},{9,1... | collective-permute-start | bytes 1572872 | tf_op jit(solution)/shard_map/ppermute | solution.py:51
  122.5 32.6 %collective-permute-start.25 = (f32[512,256]{1,0:T(8,128)S(1)}, f32[512,256]{1,0:T(8,128)S(1)}, u32[]{:S(2)}, u32[]{:S(2)}) collective-permute-start(f32[512,256]{1,0:T(8,128)S(1)} %bitcast.33), channel_id=1, source_target_pairs={{0,16},{1,17},{2,18},{3,19},{4,20},{5,21},{6,22},{7,23},{8,24},{9,... | collective-permute-start | bytes 1572872 | tf_op jit(solution)/shard_map/ppermute | solution.py:51
  124.1 31.0 %collective-permute-start.24 = (f32[512,256]{1,0:T(8,128)S(1)}, f32[512,256]{1,0:T(8,128)S(1)}, u32[]{:S(2)}, u32[]{:S(2)}) collective-permute-start(f32[512,256]{1,0:T(8,128)S(1)} %bitcast.34), channel_id=1, source_target_pairs={{0,8},{1,9},{2,10},{3,11},{4,12},{5,13},{6,14},{7,15},{8,16},{9,17... | collective-permute-start | bytes 1572872 | tf_op jit(solution)/shard_map/ppermute | solution.py:51
  126.3 5.9 %collective-permute-start.22 = (f32[64,256]{1,0:T(8,128)S(1)}, f32[64,256]{1,0:T(8,128)S(1)}, u32[]{:S(2)}, u32[]{:S(2)}) collective-permute-start(f32[64,256]{1,0:T(8,128)S(1)} %pad_maximum_fusion.4), channel_id=1, source_target_pairs={{0,2},{1,3},{2,0},{3,1},{4,6},{5,7},{6,4},{7,5},{8,10},{9,11},{10,... | collective-permute-start | bytes 196616 | tf_op jit(solution)/shard_map/ppermute | solution.py:58
  129.6 15.7 %collective-permute-start.12 = (f32[4,64,256]{2,1,0:T(8,128)S(1)}, f32[4,64,256]{2,1,0:T(8,128)S(1)}, u32[]{:S(2)}, u32[]{:S(2)}) collective-permute-start(f32[4,64,256]{2,1,0:T(8,128)S(1)} %pad_maximum_fusion.1), channel_id=1, source_target_pairs={{0,32},{32,0},{64,96},{96,64},{128,160},{160,128},{192,224},{224,1... | collective-permute-start | bytes 786440 | tf_op jit(solution)/shard_map/ppermute | solution.py:101
  132.9 11.6 %collective-permute-start.23 = (f32[128,256]{1,0:T(8,128)S(1)}, f32[128,256]{1,0:T(8,128)S(1)}, u32[]{:S(2)}, u32[]{:S(2)}) collective-permute-start(f32[128,256]{1,0:T(8,128)S(1)} %pad_maximum_fusion.3), channel_id=1, source_target_pairs={{0,4},{1,5},{2,6},{3,7},{4,0},{5,1},{6,2},{7,3},{8,12},{9,13},{10,... | collective-permute-start | bytes 393224 | tf_op jit(solution)/shard_map/ppermute | solution.py:58
  145.3 0.8 copy-start.6
  146.2 0.8 copy-start.9
  147.0 0.8 copy-start.11

commit v8 on v6

--- a/solution.py
+++ b/solution.py
@@ -10,6 +10,8 @@
 WHOLE = pl.BlockSpec(memory_space=pltpu.VMEM)
 SCALARS = pl.BlockSpec(memory_space=pltpu.SMEM)
 MIDDLE = 44
+HALF = 256
+PIECES = [(0, 0), (1, 0), (2, 0), (2, HALF), (3, 0)]
 FREE = pl.CostEstimate(flops=1, bytes_accessed=1, transcendentals=0)
 PARAMS = pltpu.CompilerParams(vmem_limit_bytes=44 << 20)
 
@@ -45,12 +47,18 @@
     return lax.all_to_all(copies, "col", 0, 0, axis_index_groups=groups)
 
 
+def y_shift(value, step):
+    perm = [(y * NZ + z, (y + step) % NY * NZ + z) for y in range(NY) for z in range(NZ)]
+    return lax.ppermute(value, "col", perm)
+
+
 def y_blocks(value):
-    def shifted(step):
-        perm = [(y * NZ + z, (y + step) % NY * NZ + z) for y in range(NY) for z in range(NZ)]
-        return lax.ppermute(value, "col", perm)
-
-    return [value] + [shifted(step) for step in range(1, NY)]
+    return [value] + [y_shift(value, step) for step in range(1, NY)]
+
+
+def y_pieces(value):
+    up, down = y_shift(value, 1), y_shift(value, -1)
+    return [value, up, y_shift(up[:HALF], 1), y_shift(down[HALF:], -1), down]
 
 
 def z_sum(value):
@@ -130,19 +138,21 @@
     )(matrix)
 
 
-def rows_of(y_ref, step, size):
-    return pl.ds(pl.multiple_of(lax.rem(y_ref[0] + (NY - step), NY) * size, size), size)
+def rows_of(y_ref, k, piece, block):
+    below, first = PIECES[k]
+    start = lax.rem(y_ref[0] + (NY - below), NY) * block + first
+    return pl.ds(pl.multiple_of(start, HALF), piece.shape[0])
 
 
 def product_kernel(y_ref, matrix, factor, col_panel, *refs):
-    panels, out, total = refs[:NY], refs[NY], refs[NY + 1]
-    for k in range(NY):
-        block = matrix[rows_of(y_ref, k, panels[k].shape[0]), :]
-        piece = three_pass(halves(panels[k][...]), halves(block), ((0,), (0,)))
+    pieces, (out, total) = refs[:-2], refs[-2:]
+    for k, piece in enumerate(pieces):
+        block = matrix[rows_of(y_ref, k, piece, pieces[0].shape[0]), :]
+        part = three_pass(halves(piece[...]), halves(block), ((0,), (0,)))
         if k == 0:
-            total[...] = piece
+            total[...] = part
         else:
-            total[...] += piece
+            total[...] += part
     count, rows, width = out.shape
     depth = width // count
     scaled = exact(total[...], factor[...], ((0,), (0,)))
@@ -188,11 +198,11 @@
 
 
 def first_update_kernel(y_ref, matrix, left, col_panel, own_scaled, *refs):
-    panels, out = refs[:NY], refs[NY]
+    pieces, out = refs[:-1], refs[-1]
     right = halves(left[...])
-    for k in range(NY):
-        rows = rows_of(y_ref, k, panels[k].shape[0])
-        value = matrix[rows, :] - three_pass(halves(panels[k][...]), right, ((1,), (1,)))
+    for k, piece in enumerate(pieces):
+        rows = rows_of(y_ref, k, piece, pieces[0].shape[0])
+        value = matrix[rows, :] - three_pass(halves(piece[...]), right, ((1,), (1,)))
         if k == 0:
             pair = halves(own_scaled[...]), halves(col_panel[...])
             value -= three_pass(*pair, ((1,), (1,)))
@@ -255,8 +265,9 @@
     to_home = [(b, a) for a, b in to_column]
 
     moved = lax.ppermute(panel, ("row", "col"), to_column)
-    mine = x_blocks(moved)
-    panels = y_blocks(spread(panel, Z_GROUPS).reshape(block, width))
+    own_panel = after(spread(panel, Z_GROUPS).reshape(block, width), moved)
+    panels = y_pieces(own_panel)
+    mine = x_blocks(after(moved, own_panel))
     col_panel = row_blocks(place, mine, other_core(mine)).reshape(nrows * rows, width)
     staged = stage(after(matrix, moved))
 

time: 148 us -> 149 us (level)
  the two profiles are of different devices: /device:TPU:1 before, /device:TPU:2 now
where the time goes in v8:
time: 149 us; the launch traced here: 148 us
  starting transfers between devices  53.7 us (36%)
  waiting for transfers between devices  50.3 us (34%)
  blocking collectives  16.9 us (11%)
  Pallas kernels  15.8 us (11%)
  local copies, waits for them, and re-layouts  9.29 us (6%)
    all_to_all x1, blocking collectives, per_device(): parts = lax.all_to_all(parts, 'row', 0, 0)  16.9 us
    ppermute x10, waiting for transfers between devices, y_shift(): return lax.ppermute(value, 'col', perm)  15.3 us
    all_to_all x2, starting transfers between devices, spread(): return lax.all_to_all(copies, 'col', 0, 0, axis_index_groups=groups)  13.8 us
    ppermute x9, starting transfers between devices, shifted(): return lax.ppermute(value, 'row', perm)  13.7 us
    ppermute x10, starting transfers between devices, y_shift(): return lax.ppermute(value, 'col', perm)  11.2 us
    ppermute x1, waiting for transfers between devices, per_device(): moved = lax.ppermute(panel, ('row', 'col'), to_column)  10.2 us
    ppermute x9, waiting for transfers between devices, shifted(): return lax.ppermute(value, 'row', perm)  9.81 us
    pallas_call x3, Pallas kernels, local(): pl.pallas_call(kernel, out_shape=[jax.ShapeDtypeStruct(shape, jnp.float32...  8.75 us
  transfers between devices with their start and end apart: 30, of which 14 were waited for; matrix products, arithmetic and copies ran while one was open for 2% of the time, Pallas kernels for 5%

profile of v8, /device:TPU:2, one launch (start us, length us, event | category | flops | bytes accessed | tf_op | source)
XLA Modules:
  0.0 148.0 jit_solution(6804684197252828120)
XLA Ops:
  0.6 1.7 %broadcast_in_dim.6 = f32[8,64,256]{2,1,0:T(8,128)} broadcast(f32[64,256]{1,0:T(8,128)} %panel.1), dimensions={1,2} | broadcast | bytes 589824 | tf_op jit(solution)/shard_map/broadcast_in_dim | solution.py:46
  2.3 8.5 %all-to-all-start = ((f32[8,64,256]{2,1,0:T(8,128)}), f32[8,64,256]{2,1,0:T(8,128)S(1)}, u32[]{:S(2)}, u32[]{:S(2)}) async-start(f32[8,64,256]{2,1,0:T(8,128)} %broadcast_in_dim.6), calls=%async_computation | async-start | bytes 1048576 | tf_op jit(solution)/shard_map/all_to_all | solution.py:47
  10.8 3.4 %collective-permute-start = (f32[64,256]{1,0:T(8,128)}, f32[64,256]{1,0:T(8,128)S(1)}, u32[]{:S(2)}, u32[]{:S(2)}) collective-permute-start(f32[64,256]{1,0:T(8,128)} %panel.1), channel_id=1, source_target_pairs={{0,0},{1,32},{2,64},{3,96},{4,128},{5,160},{6,192},{7,224},{8,1},{... | collective-permute-start | bytes 196616 | tf_op jit(solution)/shard_map/ppermute | solution.py:267
  14.2 10.2 %collective-permute-done.refs_0_ = f32[64,256]{1,0:T(8,128)S(1)} collective-permute-done((f32[64,256]{1,0:T(8,128)}, f32[64,256]{1,0:T(8,128)S(1)}, u32[]{:S(2)}, u32[]{:S(2)}) %collective-permute-start) | collective-permute-done | bytes 65568 | tf_op jit(solution)/shard_map/ppermute | solution.py:267
  24.4 2.9 %all-to-all-done = f32[8,64,256]{2,1,0:T(8,128)S(1)} async-done(((f32[8,64,256]{2,1,0:T(8,128)}), f32[8,64,256]{2,1,0:T(8,128)S(1)}, u32[]{:S(2)}, u32[]{:S(2)}) %all-to-all-start) | async-done | bytes 524320 | tf_op jit(solution)/shard_map/all_to_all | solution.py:47
  27.3 3.2 %collective-permute-start.7 = (f32[512,256]{1,0:T(8,128)S(1)}, f32[512,256]{1,0:T(8,128)S(1)}, u32[]{:S(2)}, u32[]{:S(2)}) collective-permute-start(f32[512,256]{1,0:T(8,128)S(1)} %bitcast.22), channel_id=1, source_target_pairs={{0,24},{1,25},{2,26},{3,27},{4,28},{5,29},{6,30},{7,31},{8,0},{9,1... | collective-permute-start | bytes 1572872 | tf_op jit(solution)/shard_map/ppermute | solution.py:52
  30.5 0.9 collective-permute-start.5
  31.3 1.7 %collective-permute-start.3 = (f32[64,256]{1,0:T(8,128)S(1)}, f32[64,256]{1,0:T(8,128)S(1)}, u32[]{:S(2)}, u32[]{:S(2)}) collective-permute-start(f32[64,256]{1,0:T(8,128)S(1)} %collective-permute-done.refs_0_), channel_id=1, source_target_pairs={{0,64},{32,96},{64,128},{96,160},{128,192},{160,224},{192,0},{224,... | collective-permute-start | bytes 196616 | tf_op jit(solution)/shard_map/ppermute | solution.py:78
  33.0 0.9 collective-permute-start.2
  33.9 2.2 %collective-permute-start.1 = (f32[64,256]{1,0:T(8,128)S(1)}, f32[64,256]{1,0:T(8,128)S(1)}, u32[]{:S(2)}, u32[]{:S(2)}) collective-permute-start(f32[64,256]{1,0:T(8,128)S(1)} %collective-permute-done.refs_0_), channel_id=1, source_target_pairs={{0,192},{32,224},{64,0},{96,32},{128,64},{160,96},{192,128},{224,1... | collective-permute-start | bytes 196616 | tf_op jit(solution)/shard_map/ppermute | solution.py:78
  36.1 2.8 %collective-permute-done.2.refs_2_ = f32[64,256]{1,0:T(8,128)S(1)} collective-permute-done((f32[64,256]{1,0:T(8,128)S(1)}, f32[64,256]{1,0:T(8,128)S(1)}, u32[]{:S(2)}, u32[]{:S(2)}) %collective-permute-start.2) | collective-permute-done | bytes 65568 | tf_op jit(solution)/shard_map/ppermute | solution.py:78
  38.9 0.1 collective-permute-start.4
  39.0 4.2 %collective-permute-done.7.refs_4_ = f32[512,256]{1,0:T(8,128)S(1)} collective-permute-done((f32[512,256]{1,0:T(8,128)S(1)}, f32[512,256]{1,0:T(8,128)S(1)}, u32[]{:S(2)}, u32[]{:S(2)}) %collective-permute-start.7) | collective-permute-done | bytes 524320 | tf_op jit(solution)/shard_map/ppermute | solution.py:52
  43.2 0.7 slice.9
  44.0 2.1 %collective-permute-start.8 = (f32[256,256]{1,0:T(8,128)}, f32[256,256]{1,0:T(8,128)S(1)}, u32[]{:S(2)}, u32[]{:S(2)}) collective-permute-start(f32[256,256]{1,0:T(8,128)} %slice.9), channel_id=1, source_target_pairs={{0,24},{1,25},{2,26},{3,27},{4,28},{5,29},{6,30},{7,31},{8,0},{9,1... | collective-permute-start | bytes 786440 | tf_op jit(solution)/shard_map/ppermute | solution.py:52
  46.1 0.7 slice.8
  46.8 0.1 pad_add_fusion.place
  46.9 2.2 %copy-done.1 = f32[2048,512]{1,0:T(8,128)S(1)} copy-done((f32[2048,512]{1,0:T(8,128)S(1)}, f32[2048,512]{1,0:T(8,128)}, u32[]{:S(2)}) %copy-start.1) | copy-done | bytes 4194328
  49.1 0.3 shard_map.50.matrix
  49.4 0.6 shard_map.51
  50.0 1.7 %collective-permute-done.8.refs_3_ = f32[256,256]{1,0:T(8,128)S(1)} collective-permute-done((f32[256,256]{1,0:T(8,128)}, f32[256,256]{1,0:T(8,128)S(1)}, u32[]{:S(2)}, u32[]{:S(2)}) %collective-permute-start.8) | collective-permute-done | bytes 262176 | tf_op jit(solution)/shard_map/ppermute | solution.py:52
  51.7 3.5 %collective-permute-done.6.refs_2_ = f32[256,256]{1,0:T(8,128)S(1)} collective-permute-done((f32[256,256]{1,0:T(8,128)}, f32[256,256]{1,0:T(8,128)S(1)}, u32[]{:S(2)}, u32[]{:S(2)}) %collective-permute-start.6) | collective-permute-done | bytes 262176 | tf_op jit(solution)/shard_map/ppermute | solution.py:52
  55.2 3.7 %shard_map.52 = f32[8,96,256]{2,1,0:T(8,128)S(1)} custom-call(s32[1]{0:T(128)} %bitcast.y_ref, f32[2048,512]{1,0:T(8,128)S(1)} %shard_map.50.matrix, f32[256,256]{1,0:T(8,128)S(1)} %copy-done.2, f32[512,256]{1,0:T(8,128)S(1)} %bitcast.18, f32[512,256]{1,0:T(8,128)S(1)} %bitcast.24, f32[512,256]{1,0:T(8,128)S(1)} %collective-permute-done.5.refs_1_, ...), custom_call_target="tpu_custom_call" | custom-call | flops 1 | bytes 1 | tf_op jit(solution)/shard_map/pallas_call | solution.py:114
  58.9 0.0 copy-start.3
  58.9 16.9 %all_to_all.15.parts = f32[8,96,256]{2,1,0:T(8,128)S(1)} all-to-all(f32[8,96,256]{2,1,0:T(8,128)S(1)} %shard_map.52), channel_id=1, replica_groups=mesh['row'=8,'col'=32] {'row'}, dimensions={0} | all-to-all | bytes 1572864 | tf_op jit(solution)/shard_map/all_to_all | solution.py:281
  75.8 0.6 shard_map.53
  76.5 3.1 %collective-permute-start.16 = (f32[32,256]{1,0:T(8,128)S(1)}, f32[32,256]{1,0:T(8,128)S(1)}, u32[]{:S(2)}, u32[]{:S(2)}) collective-permute-start(f32[32,256]{1,0:T(8,128)S(1)} %get-tuple-element.18), channel_id=1, source_target_pairs={{0,3},{1,2},{2,1},{3,0},{4,7},{5,6},{6,5},{7,4},{8,11},{9,10},{10,... | collective-permute-start | bytes 98312 | tf_op jit(solution)/shard_map/ppermute | solution.py:67
  79.6 0.3 collective-permute-start.15
  79.9 1.0 collective-permute-start.14
  80.9 4.4 %collective-permute-start.9 = (f32[64,256]{1,0:T(8,128)}, f32[64,256]{1,0:T(8,128)S(1)}, u32[]{:S(2)}, u32[]{:S(2)}) collective-permute-start(f32[64,256]{1,0:T(8,128)} %get-tuple-element.17.refs_0_), channel_id=1, source_target_pairs={{0,0},{32,1},{64,2},{96,3},{128,4},{160,5},{192,6},{224,7},{1,8},{... | collective-permute-start | bytes 196616 | tf_op jit(solution)/shard_map/ppermute | solution.py:285
  85.4 2.2 %collective-permute-start.17 = (f32[32,256]{1,0:T(8,128)S(1)}, f32[32,256]{1,0:T(8,128)S(1)}, u32[]{:S(2)}, u32[]{:S(2)}) collective-permute-start(f32[32,256]{1,0:T(8,128)S(1)} %add_add_fusion.1), channel_id=1, source_target_pairs={{0,4},{1,5},{2,6},{3,7},{4,0},{5,1},{6,2},{7,3},{8,12},{9,13},{10,... | collective-permute-start | bytes 98312 | tf_op jit(solution)/shard_map/ppermute | solution.py:67
  87.5 5.7 %collective-permute-done.17 = f32[32,256]{1,0:T(8,128)S(1)} collective-permute-done((f32[32,256]{1,0:T(8,128)S(1)}, f32[32,256]{1,0:T(8,128)S(1)}, u32[]{:S(2)}, u32[]{:S(2)}) %collective-permute-start.17) | collective-permute-done | bytes 32800 | tf_op jit(solution)/shard_map/ppermute | solution.py:67
  93.3 0.0 copy-start.4
  93.3 0.8 broadcast_in_dim.7
  94.1 5.3 %all-to-all-start.2 = ((f32[8,64,256]{2,1,0:T(8,128)}), f32[8,64,256]{2,1,0:T(8,128)S(1)}, u32[]{:S(2)}, u32[]{:S(2)}) async-start(f32[8,64,256]{2,1,0:T(8,128)} %broadcast_in_dim.7), calls=%async_computation.2 | async-start | bytes 1048576 | tf_op jit(solution)/shard_map/all_to_all | solution.py:47
  99.4 1.3 collective-permute-start.20
  100.7 0.4 collective-permute-start.19
  101.1 0.6 collective-permute-start.18
  101.7 3.2 %collective-permute-start.12 = (f32[64,256]{1,0:T(8,128)}, f32[64,256]{1,0:T(8,128)S(1)}, u32[]{:S(2)}, u32[]{:S(2)}) collective-permute-start(f32[64,256]{1,0:T(8,128)} %get-tuple-element.17.refs_0_), channel_id=1, source_target_pairs={{0,64},{32,96},{64,128},{96,160},{128,192},{160,224},{192,0},{224,... | collective-permute-start | bytes 196616 | tf_op jit(solution)/shard_map/ppermute | solution.py:78
  104.8 1.1 collective-permute-start.11
  105.9 1.2 collective-permute-start.10
  107.2 3.7 %collective-permute-done.11.refs_2_ = f32[64,256]{1,0:T(8,128)S(1)} collective-permute-done((f32[64,256]{1,0:T(8,128)}, f32[64,256]{1,0:T(8,128)S(1)}, u32[]{:S(2)}, u32[]{:S(2)}) %collective-permute-start.11) | collective-permute-done | bytes 65568 | tf_op jit(solution)/shard_map/ppermute | solution.py:78
  110.9 0.6 copy-done.8
  111.5 5.1 %all-to-all-done.2 = f32[8,64,256]{2,1,0:T(8,128)S(1)} async-done(((f32[8,64,256]{2,1,0:T(8,128)}), f32[8,64,256]{2,1,0:T(8,128)S(1)}, u32[]{:S(2)}, u32[]{:S(2)}) %all-to-all-start.2) | async-done | bytes 524320 | tf_op jit(solution)/shard_map/all_to_all | solution.py:47
  116.6 2.0 %collective-permute-start.27 = (f32[512,256]{1,0:T(8,128)S(1)}, f32[512,256]{1,0:T(8,128)S(1)}, u32[]{:S(2)}, u32[]{:S(2)}) collective-permute-start(f32[512,256]{1,0:T(8,128)S(1)} %bitcast.26), channel_id=1, source_target_pairs={{0,24},{1,25},{2,26},{3,27},{4,28},{5,29},{6,30},{7,31},{8,0},{9,1... | collective-permute-start | bytes 1572872 | tf_op jit(solution)/shard_map/ppermute | solution.py:52
  118.6 0.1 collective-permute-start.26
  118.7 0.8 collective-permute-start.25
  119.4 0.5 collective-permute-start.23
  120.0 1.6 %collective-permute-start.22 = (f32[32,256]{1,0:T(8,128)S(1)}, f32[32,256]{1,0:T(8,128)S(1)}, u32[]{:S(2)}, u32[]{:S(2)}) collective-permute-start(f32[32,256]{1,0:T(8,128)S(1)} %add_add_fusion.refs_5_), channel_id=1, source_target_pairs={{0,128},{32,160},{64,192},{96,224},{128,0},{160,32},{192,64},{224,... | collective-permute-start | bytes 98312 | tf_op jit(solution)/shard_map/ppermute | solution.py:78
  121.6 1.7 %collective-permute-done.23.refs_8_ = f32[32,256]{1,0:T(8,128)S(1)} collective-permute-done((f32[32,256]{1,0:T(8,128)S(1)}, f32[32,256]{1,0:T(8,128)S(1)}, u32[]{:S(2)}, u32[]{:S(2)}) %collective-permute-start.23) | collective-permute-done | bytes 32800 | tf_op jit(solution)/shard_map/ppermute | solution.py:78
  123.4 1.3 collective-permute-start.21
  124.7 1.0 pad_maximum_fusion.1
  125.6 0.1 collective-permute-start.13
  125.7 1.5 %collective-permute-done.21.refs_6_ = f32[32,256]{1,0:T(8,128)S(1)} collective-permute-done((f32[32,256]{1,0:T(8,128)S(1)}, f32[32,256]{1,0:T(8,128)S(1)}, u32[]{:S(2)}, u32[]{:S(2)}) %collective-permute-start.21) | collective-permute-done | bytes 32800 | tf_op jit(solution)/shard_map/ppermute | solution.py:78
  127.3 0.3 collective-permute-start.24
  127.6 1.3 collective-permute-done.24.refs_9_
  128.9 0.8 copy-done.5
  129.8 0.8 copy-done.7
  130.6 0.8 copy-done.9
  131.5 2.8 %shard_map.54 = (f32[512,256]{1,0:T(8,128)S(1)}, f32[64,256]{1,0:T(8,128)}) custom-call(s32[2]{0:T(128)S(1)} %pad_add_fusion.place, f32[256,256]{1,0:T(8,128)S(1)} %copy-done.2, f32[64,256]{1,0:T(8,128)S(1)} %copy-done.3, f32[64,256]{1,0:T(8,128)S(1)} %copy-done.5, f32[512,256]{1,0:T(8,128)S(1)} %bitcast.19, f32[64,256]{1,0:T(8,128)} %get-tuple-element.17.refs_0_, ...), custom_call_target="tpu_custom_call" | custom-call | flops 1 | bytes 1 | tf_op jit(solution)/shard_map/pallas_call | solution.py:188
  134.3 4.4 %shard_map.55.matrix = f32[2048,512]{1,0:T(8,128)S(1)} custom-call(s32[1]{0:T(128)} %bitcast.y_ref, f32[2048,512]{1,0:T(8,128)} %copy-done, f32[512,256]{1,0:T(8,128)S(1)} %get-tuple-element.22.left, f32[512,256]{1,0:T(8,128)S(1)} %bitcast.20, f32[512,256]{1,0:T(8,128)S(1)} %bitcast.29, f32[512,256]{1,0:T(8,128)S(1)} %bitcast.25, ...), custom_call_target="tpu_custom_call" | custom-call | flops 1 | bytes 1 | tf_op jit(solution)/shard_map/pallas_call | solution.py:114
  138.7 2.5 %collective-permute-done.27.refs_2_ = f32[512,256]{1,0:T(8,128)S(1)} collective-permute-done((f32[512,256]{1,0:T(8,128)S(1)}, f32[512,256]{1,0:T(8,128)S(1)}, u32[]{:S(2)}, u32[]{:S(2)}) %collective-permute-start.27) | collective-permute-done | bytes 524320 | tf_op jit(solution)/shard_map/ppermute | solution.py:52
  141.2 3.4 %collective-permute-done.25.refs_0_ = f32[512,256]{1,0:T(8,128)S(1)} collective-permute-done((f32[512,256]{1,0:T(8,128)S(1)}, f32[512,256]{1,0:T(8,128)S(1)}, u32[]{:S(2)}, u32[]{:S(2)}) %collective-permute-start.25) | collective-permute-done | bytes 524320 | tf_op jit(solution)/shard_map/ppermute | solution.py:52
  144.6 3.4 %shard_map.56 = f32[2048,512]{1,0:T(8,128)} custom-call(s32[1]{0:T(128)} %bitcast.y_ref, f32[2048,512]{1,0:T(8,128)S(1)} %shard_map.55.matrix, f32[512,256]{1,0:T(8,128)S(1)} %bitcast.21, f32[512,256]{1,0:T(8,128)S(1)} %collective-permute-done.25.refs_0_, f32[512,256]{1,0:T(8,128)S(1)} %collective-permute-done.26.refs_1_, ...), custom_call_target="tpu_custom_call" | custom-call | flops 1 | bytes 1 | tf_op jit(solution)/shard_map/pallas_call | solution.py:240
  (35 shorter events, 0.1 us)
Async XLA Ops:
  2.3 25.0 %all-to-all-start = ((f32[8,64,256]{2,1,0:T(8,128)}), f32[8,64,256]{2,1,0:T(8,128)S(1)}, u32[]{:S(2)}, u32[]{:S(2)}) async-start(f32[8,64,256]{2,1,0:T(8,128)} %broadcast_in_dim.6), calls=%async_computation | async-start | bytes 1048576 | tf_op jit(solution)/shard_map/all_to_all | solution.py:47
  10.8 13.7 %collective-permute-start = (f32[64,256]{1,0:T(8,128)}, f32[64,256]{1,0:T(8,128)S(1)}, u32[]{:S(2)}, u32[]{:S(2)}) collective-permute-start(f32[64,256]{1,0:T(8,128)} %panel.1), channel_id=1, source_target_pairs={{0,0},{1,32},{2,64},{3,96},{4,128},{5,160},{6,192},{7,224},{8,1},{... | collective-permute-start | bytes 196616 | tf_op jit(solution)/shard_map/ppermute | solution.py:267
  27.3 15.9 %collective-permute-start.7 = (f32[512,256]{1,0:T(8,128)S(1)}, f32[512,256]{1,0:T(8,128)S(1)}, u32[]{:S(2)}, u32[]{:S(2)}) collective-permute-start(f32[512,256]{1,0:T(8,128)S(1)} %bitcast.22), channel_id=1, source_target_pairs={{0,24},{1,25},{2,26},{3,27},{4,28},{5,29},{6,30},{7,31},{8,0},{9,1... | collective-permute-start | bytes 1572872 | tf_op jit(solution)/shard_map/ppermute | solution.py:52
  30.5 15.6 %collective-permute-start.5 = (f32[512,256]{1,0:T(8,128)S(1)}, f32[512,256]{1,0:T(8,128)S(1)}, u32[]{:S(2)}, u32[]{:S(2)}) collective-permute-start(f32[512,256]{1,0:T(8,128)S(1)} %bitcast.23), channel_id=1, source_target_pairs={{0,8},{1,9},{2,10},{3,11},{4,12},{5,13},{6,14},{7,15},{8,16},{9,17... | collective-permute-start | bytes 1572872 | tf_op jit(solution)/shard_map/ppermute | solution.py:52
  31.3 4.8 %collective-permute-start.3 = (f32[64,256]{1,0:T(8,128)S(1)}, f32[64,256]{1,0:T(8,128)S(1)}, u32[]{:S(2)}, u32[]{:S(2)}) collective-permute-start(f32[64,256]{1,0:T(8,128)S(1)} %collective-permute-done.refs_0_), channel_id=1, source_target_pairs={{0,64},{32,96},{64,128},{96,160},{128,192},{160,224},{192,0},{224,... | collective-permute-start | bytes 196616 | tf_op jit(solution)/shard_map/ppermute | solution.py:78
  33.0 5.9 %collective-permute-start.2 = (f32[64,256]{1,0:T(8,128)S(1)}, f32[64,256]{1,0:T(8,128)S(1)}, u32[]{:S(2)}, u32[]{:S(2)}) collective-permute-start(f32[64,256]{1,0:T(8,128)S(1)} %collective-permute-done.refs_0_), channel_id=1, source_target_pairs={{0,128},{32,160},{64,192},{96,224},{128,0},{160,32},{192,64},{224,... | collective-permute-start | bytes 196616 | tf_op jit(solution)/shard_map/ppermute | solution.py:78
  33.9 5.0 %collective-permute-start.1 = (f32[64,256]{1,0:T(8,128)S(1)}, f32[64,256]{1,0:T(8,128)S(1)}, u32[]{:S(2)}, u32[]{:S(2)}) collective-permute-start(f32[64,256]{1,0:T(8,128)S(1)} %collective-permute-done.refs_0_), channel_id=1, source_target_pairs={{0,192},{32,224},{64,0},{96,32},{128,64},{160,96},{192,128},{224,1... | collective-permute-start | bytes 196616 | tf_op jit(solution)/shard_map/ppermute | solution.py:78
  38.9 10.4 %collective-permute-start.4 = (f32[4,64,256]{2,1,0:T(8,128)S(1)}, f32[4,64,256]{2,1,0:T(8,128)S(1)}, u32[]{:S(2)}, u32[]{:S(2)}) collective-permute-start(f32[4,64,256]{2,1,0:T(8,128)S(1)} %pad_maximum_fusion), channel_id=1, source_target_pairs={{0,32},{32,0},{64,96},{96,64},{128,160},{160,128},{192,224},{224,1... | collective-permute-start | bytes 786440 | tf_op jit(solution)/shard_map/ppermute | solution.py:85
  44.0 7.7 %collective-permute-start.8 = (f32[256,256]{1,0:T(8,128)}, f32[256,256]{1,0:T(8,128)S(1)}, u32[]{:S(2)}, u32[]{:S(2)}) collective-permute-start(f32[256,256]{1,0:T(8,128)} %slice.9), channel_id=1, source_target_pairs={{0,24},{1,25},{2,26},{3,27},{4,28},{5,29},{6,30},{7,31},{8,0},{9,1... | collective-permute-start | bytes 786440 | tf_op jit(solution)/shard_map/ppermute | solution.py:52
  46.8 8.4 %collective-permute-start.6 = (f32[256,256]{1,0:T(8,128)}, f32[256,256]{1,0:T(8,128)S(1)}, u32[]{:S(2)}, u32[]{:S(2)}) collective-permute-start(f32[256,256]{1,0:T(8,128)} %slice.8), channel_id=1, source_target_pairs={{0,8},{1,9},{2,10},{3,11},{4,12},{5,13},{6,14},{7,15},{8,16},{9,17... | collective-permute-start | bytes 786440 | tf_op jit(solution)/shard_map/ppermute | solution.py:52
  46.9 2.2 %copy-start.1 = (f32[2048,512]{1,0:T(8,128)S(1)}, f32[2048,512]{1,0:T(8,128)}, u32[]{:S(2)}) copy-start(f32[2048,512]{1,0:T(8,128)} %matrix) | copy-start | bytes 12582916
  49.1 6.1 %copy-start.2 = (f32[256,256]{1,0:T(8,128)S(1)}, f32[256,256]{1,0:T(8,128)}, u32[]{:S(2)}) copy-start(f32[256,256]{1,0:T(8,128)} %factor.3) | copy-start | bytes 786436
  49.4 9.5 %copy-start = (f32[2048,512]{1,0:T(8,128)}, f32[2048,512]{1,0:T(8,128)S(1)}, u32[]{:S(2)}) copy-start(f32[2048,512]{1,0:T(8,128)S(1)} %shard_map.50.matrix) | copy-start | bytes 12582916
  58.9 70.1 %copy-start.3 = (f32[64,256]{1,0:T(8,128)S(1)}, f32[64,256]{1,0:T(8,128)}, u32[]{:S(2)}) copy-start(f32[64,256]{1,0:T(8,128)} %panel.1) | copy-start | bytes 196612
  76.5 8.8 %collective-permute-start.16 = (f32[32,256]{1,0:T(8,128)S(1)}, f32[32,256]{1,0:T(8,128)S(1)}, u32[]{:S(2)}, u32[]{:S(2)}) collective-permute-start(f32[32,256]{1,0:T(8,128)S(1)} %get-tuple-element.18), channel_id=1, source_target_pairs={{0,3},{1,2},{2,1},{3,0},{4,7},{5,6},{6,5},{7,4},{8,11},{9,10},{10,... | collective-permute-start | bytes 98312 | tf_op jit(solution)/shard_map/ppermute | solution.py:67
  79.6 5.7 %collective-permute-start.15 = (f32[32,256]{1,0:T(8,128)S(1)}, f32[32,256]{1,0:T(8,128)S(1)}, u32[]{:S(2)}, u32[]{:S(2)}) collective-permute-start(f32[32,256]{1,0:T(8,128)S(1)} %get-tuple-element.18), channel_id=1, source_target_pairs={{0,2},{1,3},{2,0},{3,1},{4,6},{5,7},{6,4},{7,5},{8,10},{9,11},{10,... | collective-permute-start | bytes 98312 | tf_op jit(solution)/shard_map/ppermute | solution.py:67
  79.9 5.4 %collective-permute-start.14 = (f32[32,256]{1,0:T(8,128)S(1)}, f32[32,256]{1,0:T(8,128)S(1)}, u32[]{:S(2)}, u32[]{:S(2)}) collective-permute-start(f32[32,256]{1,0:T(8,128)S(1)} %get-tuple-element.18), channel_id=1, source_target_pairs={{0,1},{1,0},{2,3},{3,2},{4,5},{5,4},{6,7},{7,6},{8,9},{9,8},{10,11... | collective-permute-start | bytes 98312 | tf_op jit(solution)/shard_map/ppermute | solution.py:67
  80.9 12.4 %collective-permute-start.9 = (f32[64,256]{1,0:T(8,128)}, f32[64,256]{1,0:T(8,128)S(1)}, u32[]{:S(2)}, u32[]{:S(2)}) collective-permute-start(f32[64,256]{1,0:T(8,128)} %get-tuple-element.17.refs_0_), channel_id=1, source_target_pairs={{0,0},{32,1},{64,2},{96,3},{128,4},{160,5},{192,6},{224,7},{1,8},{... | collective-permute-start | bytes 196616 | tf_op jit(solution)/shard_map/ppermute | solution.py:285
  85.4 7.9 %collective-permute-start.17 = (f32[32,256]{1,0:T(8,128)S(1)}, f32[32,256]{1,0:T(8,128)S(1)}, u32[]{:S(2)}, u32[]{:S(2)}) collective-permute-start(f32[32,256]{1,0:T(8,128)S(1)} %add_add_fusion.1), channel_id=1, source_target_pairs={{0,4},{1,5},{2,6},{3,7},{4,0},{5,1},{6,2},{7,3},{8,12},{9,13},{10,... | collective-permute-start | bytes 98312 | tf_op jit(solution)/shard_map/ppermute | solution.py:67
  93.3 0.8 copy-start.4
  94.1 22.5 %all-to-all-start.2 = ((f32[8,64,256]{2,1,0:T(8,128)}), f32[8,64,256]{2,1,0:T(8,128)S(1)}, u32[]{:S(2)}, u32[]{:S(2)}) async-start(f32[8,64,256]{2,1,0:T(8,128)} %broadcast_in_dim.7), calls=%async_computation.2 | async-start | bytes 1048576 | tf_op jit(solution)/shard_map/all_to_all | solution.py:47
  99.4 6.5 %collective-permute-start.20 = (f32[32,256]{1,0:T(8,128)S(1)}, f32[32,256]{1,0:T(8,128)S(1)}, u32[]{:S(2)}, u32[]{:S(2)}) collective-permute-start(f32[32,256]{1,0:T(8,128)S(1)} %add.31), channel_id=1, source_target_pairs={{0,24},{1,25},{2,26},{3,27},{4,28},{5,29},{6,30},{7,31},{8,0},{9,1... | collective-permute-start | bytes 98312 | tf_op jit(solution)/shard_map/ppermute | solution.py:52
  100.7 6.4 %collective-permute-start.19 = (f32[32,256]{1,0:T(8,128)S(1)}, f32[32,256]{1,0:T(8,128)S(1)}, u32[]{:S(2)}, u32[]{:S(2)}) collective-permute-start(f32[32,256]{1,0:T(8,128)S(1)} %add.31), channel_id=1, source_target_pairs={{0,16},{1,17},{2,18},{3,19},{4,20},{5,21},{6,22},{7,23},{8,24},{9,... | collective-permute-start | bytes 98312 | tf_op jit(solution)/shard_map/ppermute | solution.py:52
  101.1 6.1 %collective-permute-start.18 = (f32[32,256]{1,0:T(8,128)S(1)}, f32[32,256]{1,0:T(8,128)S(1)}, u32[]{:S(2)}, u32[]{:S(2)}) collective-permute-start(f32[32,256]{1,0:T(8,128)S(1)} %add.31), channel_id=1, source_target_pairs={{0,8},{1,9},{2,10},{3,11},{4,12},{5,13},{6,14},{7,15},{8,16},{9,17... | collective-permute-start | bytes 98312 | tf_op jit(solution)/shard_map/ppermute | solution.py:52
  101.7 5.5 %collective-permute-start.12 = (f32[64,256]{1,0:T(8,128)}, f32[64,256]{1,0:T(8,128)S(1)}, u32[]{:S(2)}, u32[]{:S(2)}) collective-permute-start(f32[64,256]{1,0:T(8,128)} %get-tuple-element.17.refs_0_), channel_id=1, source_target_pairs={{0,64},{32,96},{64,128},{96,160},{128,192},{160,224},{192,0},{224,... | collective-permute-start | bytes 196616 | tf_op jit(solution)/shard_map/ppermute | solution.py:78
  104.8 6.1 %collective-permute-start.11 = (f32[64,256]{1,0:T(8,128)}, f32[64,256]{1,0:T(8,128)S(1)}, u32[]{:S(2)}, u32[]{:S(2)}) collective-permute-start(f32[64,256]{1,0:T(8,128)} %get-tuple-element.17.refs_0_), channel_id=1, source_target_pairs={{0,128},{32,160},{64,192},{96,224},{128,0},{160,32},{192,64},{224,... | collective-permute-start | bytes 196616 | tf_op jit(solution)/shard_map/ppermute | solution.py:78
  105.9 5.6 %collective-permute-start.10 = (f32[64,256]{1,0:T(8,128)}, f32[64,256]{1,0:T(8,128)}, u32[]{:S(2)}, u32[]{:S(2)}) collective-permute-start(f32[64,256]{1,0:T(8,128)} %get-tuple-element.17.refs_0_), channel_id=1, source_target_pairs={{0,192},{32,224},{64,0},{96,32},{128,64},{160,96},{192,128},{224,1... | collective-permute-start | bytes 196616 | tf_op jit(solution)/shard_map/ppermute | solution.py:78
  107.2 3.7 %copy-start.6 = (f32[64,256]{1,0:T(8,128)}, f32[64,256]{1,0:T(8,128)S(1)}, u32[]{:S(2)}) copy-start(f32[64,256]{1,0:T(8,128)S(1)} %collective-permute-done.12.refs_3_) | copy-start | bytes 196612
  110.9 0.6 copy-start.8
  116.6 24.6 %collective-permute-start.27 = (f32[512,256]{1,0:T(8,128)S(1)}, f32[512,256]{1,0:T(8,128)S(1)}, u32[]{:S(2)}, u32[]{:S(2)}) collective-permute-start(f32[512,256]{1,0:T(8,128)S(1)} %bitcast.26), channel_id=1, source_target_pairs={{0,24},{1,25},{2,26},{3,27},{4,28},{5,29},{6,30},{7,31},{8,0},{9,1... | collective-permute-start | bytes 1572872 | tf_op jit(solution)/shard_map/ppermute | solution.py:52
  118.6 22.6 %collective-permute-start.26 = (f32[512,256]{1,0:T(8,128)S(1)}, f32[512,256]{1,0:T(8,128)S(1)}, u32[]{:S(2)}, u32[]{:S(2)}) collective-permute-start(f32[512,256]{1,0:T(8,128)S(1)} %bitcast.27), channel_id=1, source_target_pairs={{0,16},{1,17},{2,18},{3,19},{4,20},{5,21},{6,22},{7,23},{8,24},{9,... | collective-permute-start | bytes 1572872 | tf_op jit(solution)/shard_map/ppermute | solution.py:52
  118.7 25.9 %collective-permute-start.25 = (f32[512,256]{1,0:T(8,128)S(1)}, f32[512,256]{1,0:T(8,128)S(1)}, u32[]{:S(2)}, u32[]{:S(2)}) collective-permute-start(f32[512,256]{1,0:T(8,128)S(1)} %bitcast.28), channel_id=1, source_target_pairs={{0,8},{1,9},{2,10},{3,11},{4,12},{5,13},{6,14},{7,15},{8,16},{9,17... | collective-permute-start | bytes 1572872 | tf_op jit(solution)/shard_map/ppermute | solution.py:52
  119.4 3.9 %collective-permute-start.23 = (f32[32,256]{1,0:T(8,128)S(1)}, f32[32,256]{1,0:T(8,128)S(1)}, u32[]{:S(2)}, u32[]{:S(2)}) collective-permute-start(f32[32,256]{1,0:T(8,128)S(1)} %add_add_fusion.refs_5_), channel_id=1, source_target_pairs={{0,64},{32,96},{64,128},{96,160},{128,192},{160,224},{192,0},{224,... | collective-permute-start | bytes 98312 | tf_op jit(solution)/shard_map/ppermute | solution.py:78
  120.0 5.7 %collective-permute-start.22 = (f32[32,256]{1,0:T(8,128)S(1)}, f32[32,256]{1,0:T(8,128)S(1)}, u32[]{:S(2)}, u32[]{:S(2)}) collective-permute-start(f32[32,256]{1,0:T(8,128)S(1)} %add_add_fusion.refs_5_), channel_id=1, source_target_pairs={{0,128},{32,160},{64,192},{96,224},{128,0},{160,32},{192,64},{224,... | collective-permute-start | bytes 98312 | tf_op jit(solution)/shard_map/ppermute | solution.py:78
  123.4 3.9 %collective-permute-start.21 = (f32[32,256]{1,0:T(8,128)S(1)}, f32[32,256]{1,0:T(8,128)S(1)}, u32[]{:S(2)}, u32[]{:S(2)}) collective-permute-start(f32[32,256]{1,0:T(8,128)S(1)} %add_add_fusion.refs_5_), channel_id=1, source_target_pairs={{0,192},{32,224},{64,0},{96,32},{128,64},{160,96},{192,128},{224,1... | collective-permute-start | bytes 98312 | tf_op jit(solution)/shard_map/ppermute | solution.py:78
  125.6 2.0 %collective-permute-start.13 = (f32[4,64,256]{2,1,0:T(8,128)S(1)}, f32[4,64,256]{2,1,0:T(8,128)S(1)}, u32[]{:S(2)}, u32[]{:S(2)}) collective-permute-start(f32[4,64,256]{2,1,0:T(8,128)S(1)} %pad_maximum_fusion.1), channel_id=1, source_target_pairs={{0,32},{32,0},{64,96},{96,64},{128,160},{160,128},{192,224},{224,1... | collective-permute-start | bytes 786440 | tf_op jit(solution)/shard_map/ppermute | solution.py:85
  127.3 1.7 %collective-permute-start.24 = (f32[4,32,256]{2,1,0:T(8,128)S(1)}, f32[4,32,256]{2,1,0:T(8,128)S(1)}, u32[]{:S(2)}, u32[]{:S(2)}) collective-permute-start(f32[4,32,256]{2,1,0:T(8,128)S(1)} %pad_maximum_fusion.2), channel_id=1, source_target_pairs={{0,32},{32,0},{64,96},{96,64},{128,160},{160,128},{192,224},{224,1... | collective-permute-start | bytes 393224 | tf_op jit(solution)/shard_map/ppermute | solution.py:85
  128.9 0.8 copy-start.5
  129.8 0.8 copy-start.7
  130.6 0.8 copy-start.9

commit v9 on v6

--- a/solution.py
+++ b/solution.py
@@ -58,8 +58,8 @@
         perm = [(y * NZ + z, y * NZ + (z ^ bits)) for y in range(NY) for z in range(NZ)]
         return lax.ppermute(value, "col", perm)
 
-    value = sum([partner(value, bits) for bits in (1, 2, 3)], value)
-    return value + partner(value, 4)
+    value = sum([partner(value, bits) for bits in (2, 4, 6)], value)
+    return value + partner(value, 1)
 
 
 def x_blocks(value):

time: 148 us -> 150 us (1.014)
  the two profiles are of different devices: /device:TPU:1 before, /device:TPU:2 now
where the time goes in v9:
time: 150 us; the launch traced here: 148 us
  starting transfers between devices  56.8 us (38%)
  waiting for transfers between devices  48.7 us (32%)
  blocking collectives  16.6 us (11%)
  Pallas kernels  15.8 us (11%)
  local copies, waits for them, and re-layouts  7.86 us (5%)
    all_to_all x2, waiting for transfers between devices, spread(): return lax.all_to_all(copies, 'col', 0, 0, axis_index_groups=groups)  17.9 us
    all_to_all x1, blocking collectives, per_device(): parts = lax.all_to_all(parts, 'row', 0, 0)  16.6 us
    ppermute x9, starting transfers between devices, shifted(): return lax.ppermute(value, 'row', perm)  16.4 us
    ppermute x9, waiting for transfers between devices, shifted(): return lax.ppermute(value, 'col', perm)  13.8 us
    ppermute x9, starting transfers between devices, shifted(): return lax.ppermute(value, 'col', perm)  13.7 us
    all_to_all x2, starting transfers between devices, spread(): return lax.all_to_all(copies, 'col', 0, 0, axis_index_groups=groups)  12 us
    pallas_call x3, Pallas kernels, local(): pl.pallas_call(kernel, out_shape=[jax.ShapeDtypeStruct(shape, jnp.float32...  8.76 us
    ppermute x9, waiting for transfers between devices, shifted(): return lax.ppermute(value, 'row', perm)  8.12 us
  transfers between devices with their start and end apart: 29, of which 17 were waited for; matrix products, arithmetic and copies ran while one was open for 1% of the time, Pallas kernels for 5%

profile of v9, /device:TPU:2, one launch (start us, length us, event | category | flops | bytes accessed | tf_op | source)
XLA Modules:
  0.0 147.6 jit_solution(13874543748385158971)
XLA Ops:
  0.6 1.7 %broadcast_in_dim.6 = f32[8,64,256]{2,1,0:T(8,128)} broadcast(f32[64,256]{1,0:T(8,128)} %panel.1), dimensions={1,2} | broadcast | bytes 589824 | tf_op jit(solution)/shard_map/broadcast_in_dim | solution.py:44
  2.3 8.5 %all-to-all-start = ((f32[8,64,256]{2,1,0:T(8,128)}), f32[8,64,256]{2,1,0:T(8,128)S(1)}, u32[]{:S(2)}, u32[]{:S(2)}) async-start(f32[8,64,256]{2,1,0:T(8,128)} %broadcast_in_dim.6), calls=%async_computation | async-start | bytes 1048576 | tf_op jit(solution)/shard_map/all_to_all | solution.py:45
  10.8 3.4 %collective-permute-start = (f32[64,256]{1,0:T(8,128)}, f32[64,256]{1,0:T(8,128)S(1)}, u32[]{:S(2)}, u32[]{:S(2)}) collective-permute-start(f32[64,256]{1,0:T(8,128)} %panel.1), channel_id=1, source_target_pairs={{0,0},{1,32},{2,64},{3,96},{4,128},{5,160},{6,192},{7,224},{8,1},{... | collective-permute-start | bytes 196616 | tf_op jit(solution)/shard_map/ppermute | solution.py:257
  14.2 13.1 %all-to-all-done = f32[8,64,256]{2,1,0:T(8,128)S(1)} async-done(((f32[8,64,256]{2,1,0:T(8,128)}), f32[8,64,256]{2,1,0:T(8,128)S(1)}, u32[]{:S(2)}, u32[]{:S(2)}) %all-to-all-start) | async-done | bytes 524320 | tf_op jit(solution)/shard_map/all_to_all | solution.py:45
  27.3 3.2 %collective-permute-start.7 = (f32[512,256]{1,0:T(8,128)S(1)}, f32[512,256]{1,0:T(8,128)S(1)}, u32[]{:S(2)}, u32[]{:S(2)}) collective-permute-start(f32[512,256]{1,0:T(8,128)S(1)} %bitcast.22), channel_id=1, source_target_pairs={{0,24},{1,25},{2,26},{3,27},{4,28},{5,29},{6,30},{7,31},{8,0},{9,1... | collective-permute-start | bytes 1572872 | tf_op jit(solution)/shard_map/ppermute | solution.py:51
  30.5 2.9 %collective-permute-start.6 = (f32[512,256]{1,0:T(8,128)S(1)}, f32[512,256]{1,0:T(8,128)S(1)}, u32[]{:S(2)}, u32[]{:S(2)}) collective-permute-start(f32[512,256]{1,0:T(8,128)S(1)} %bitcast.23), channel_id=1, source_target_pairs={{0,16},{1,17},{2,18},{3,19},{4,20},{5,21},{6,22},{7,23},{8,24},{9,... | collective-permute-start | bytes 1572872 | tf_op jit(solution)/shard_map/ppermute | solution.py:51
  33.4 1.0 collective-permute-start.5
  34.4 0.0 collective-permute-done.refs_0_
  34.4 1.5 %collective-permute-start.3 = (f32[64,256]{1,0:T(8,128)S(1)}, f32[64,256]{1,0:T(8,128)S(1)}, u32[]{:S(2)}, u32[]{:S(2)}) collective-permute-start(f32[64,256]{1,0:T(8,128)S(1)} %collective-permute-done.refs_0_), channel_id=1, source_target_pairs={{0,64},{32,96},{64,128},{96,160},{128,192},{160,224},{192,0},{224,... | collective-permute-start | bytes 196616 | tf_op jit(solution)/shard_map/ppermute | solution.py:70
  35.9 1.1 collective-permute-start.2
  37.0 2.0 %collective-permute-done.3.refs_3_ = f32[64,256]{1,0:T(8,128)S(1)} collective-permute-done((f32[64,256]{1,0:T(8,128)S(1)}, f32[64,256]{1,0:T(8,128)S(1)}, u32[]{:S(2)}, u32[]{:S(2)}) %collective-permute-start.3) | collective-permute-done | bytes 65568 | tf_op jit(solution)/shard_map/ppermute | solution.py:70
  39.0 1.8 %collective-permute-start.1 = (f32[64,256]{1,0:T(8,128)S(1)}, f32[64,256]{1,0:T(8,128)S(1)}, u32[]{:S(2)}, u32[]{:S(2)}) collective-permute-start(f32[64,256]{1,0:T(8,128)S(1)} %collective-permute-done.refs_0_), channel_id=1, source_target_pairs={{0,192},{32,224},{64,0},{96,32},{128,64},{160,96},{192,128},{224,1... | collective-permute-start | bytes 196616 | tf_op jit(solution)/shard_map/ppermute | solution.py:70
  40.8 0.9 collective-permute-done.2.refs_2_
  41.7 1.5 %collective-permute-done.1.refs_1_ = f32[64,256]{1,0:T(8,128)S(1)} collective-permute-done((f32[64,256]{1,0:T(8,128)S(1)}, f32[64,256]{1,0:T(8,128)S(1)}, u32[]{:S(2)}, u32[]{:S(2)}) %collective-permute-start.1) | collective-permute-done | bytes 65568 | tf_op jit(solution)/shard_map/ppermute | solution.py:70
  43.3 0.1 collective-permute-start.4
  43.4 0.1 pad_add_fusion.place
  43.5 2.2 %copy-done.1 = f32[2048,512]{1,0:T(8,128)S(1)} copy-done((f32[2048,512]{1,0:T(8,128)S(1)}, f32[2048,512]{1,0:T(8,128)}, u32[]{:S(2)}) %copy-start.1) | copy-done | bytes 4194328
  45.7 0.3 shard_map.50.matrix
  45.9 0.0 copy-start
  46.0 0.6 shard_map.51
  46.6 0.3 collective-permute-done.6.refs_2_
  46.9 9.8 %collective-permute-done.5.refs_1_ = f32[512,256]{1,0:T(8,128)S(1)} collective-permute-done((f32[512,256]{1,0:T(8,128)S(1)}, f32[512,256]{1,0:T(8,128)S(1)}, u32[]{:S(2)}, u32[]{:S(2)}) %collective-permute-start.5) | collective-permute-done | bytes 524320 | tf_op jit(solution)/shard_map/ppermute | solution.py:51
  56.6 3.7 %shard_map.52 = f32[8,96,256]{2,1,0:T(8,128)S(1)} custom-call(s32[1]{0:T(128)} %bitcast.y_ref, f32[2048,512]{1,0:T(8,128)S(1)} %shard_map.50.matrix, f32[256,256]{1,0:T(8,128)S(1)} %copy-done.2, f32[512,256]{1,0:T(8,128)S(1)} %bitcast.18, f32[512,256]{1,0:T(8,128)S(1)} %bitcast.25, f32[512,256]{1,0:T(8,128)S(1)} %collective-permute-done.5.refs_1_, ...), custom_call_target="tpu_custom_call" | custom-call | flops 1 | bytes 1 | tf_op jit(solution)/shard_map/pallas_call | solution.py:106
  60.3 0.0 copy-start.3
  60.3 16.6 %all_to_all.15.parts = f32[8,96,256]{2,1,0:T(8,128)S(1)} all-to-all(f32[8,96,256]{2,1,0:T(8,128)S(1)} %shard_map.52), channel_id=1, replica_groups=mesh['row'=8,'col'=32] {'row'}, dimensions={0} | all-to-all | bytes 1572864 | tf_op jit(solution)/shard_map/all_to_all | solution.py:270
  76.9 0.7 shard_map.53
  77.5 1.4 collective-permute-start.15
  79.0 1.6 %collective-permute-start.14 = (f32[32,256]{1,0:T(8,128)S(1)}, f32[32,256]{1,0:T(8,128)S(1)}, u32[]{:S(2)}, u32[]{:S(2)}) collective-permute-start(f32[32,256]{1,0:T(8,128)S(1)} %get-tuple-element.14), channel_id=1, source_target_pairs={{0,4},{1,5},{2,6},{3,7},{4,0},{5,1},{6,2},{7,3},{8,12},{9,13},{10,... | collective-permute-start | bytes 98312 | tf_op jit(solution)/shard_map/ppermute | solution.py:59
  80.6 3.4 %collective-permute-start.13 = (f32[32,256]{1,0:T(8,128)S(1)}, f32[32,256]{1,0:T(8,128)S(1)}, u32[]{:S(2)}, u32[]{:S(2)}) collective-permute-start(f32[32,256]{1,0:T(8,128)S(1)} %get-tuple-element.14), channel_id=1, source_target_pairs={{0,2},{1,3},{2,0},{3,1},{4,6},{5,7},{6,4},{7,5},{8,10},{9,11},{10,... | collective-permute-start | bytes 98312 | tf_op jit(solution)/shard_map/ppermute | solution.py:59
  84.0 2.8 %collective-permute-start.8 = (f32[64,256]{1,0:T(8,128)}, f32[64,256]{1,0:T(8,128)S(1)}, u32[]{:S(2)}, u32[]{:S(2)}) collective-permute-start(f32[64,256]{1,0:T(8,128)} %get-tuple-element.13.refs_0_), channel_id=1, source_target_pairs={{0,0},{32,1},{64,2},{96,3},{128,4},{160,5},{192,6},{224,7},{1,8},{... | collective-permute-start | bytes 196616 | tf_op jit(solution)/shard_map/ppermute | solution.py:274
  86.9 1.5 %collective-permute-start.16 = (f32[32,256]{1,0:T(8,128)S(1)}, f32[32,256]{1,0:T(8,128)S(1)}, u32[]{:S(2)}, u32[]{:S(2)}) collective-permute-start(f32[32,256]{1,0:T(8,128)S(1)} %add_add_fusion.1), channel_id=1, source_target_pairs={{0,1},{1,0},{2,3},{3,2},{4,5},{5,4},{6,7},{7,6},{8,9},{9,8},{10,11... | collective-permute-start | bytes 98312 | tf_op jit(solution)/shard_map/ppermute | solution.py:59
  88.4 2.5 %collective-permute-done.16 = f32[32,256]{1,0:T(8,128)S(1)} collective-permute-done((f32[32,256]{1,0:T(8,128)S(1)}, f32[32,256]{1,0:T(8,128)S(1)}, u32[]{:S(2)}, u32[]{:S(2)}) %collective-permute-start.16) | collective-permute-done | bytes 32800 | tf_op jit(solution)/shard_map/ppermute | solution.py:59
  90.9 5.1 %collective-permute-done.8.home = f32[64,256]{1,0:T(8,128)S(1)} collective-permute-done((f32[64,256]{1,0:T(8,128)}, f32[64,256]{1,0:T(8,128)S(1)}, u32[]{:S(2)}, u32[]{:S(2)}) %collective-permute-start.8) | collective-permute-done | bytes 65568 | tf_op jit(solution)/shard_map/ppermute | solution.py:274
  96.0 0.8 broadcast_in_dim.7
  96.8 3.5 %all-to-all-start.2 = ((f32[8,64,256]{2,1,0:T(8,128)}), f32[8,64,256]{2,1,0:T(8,128)S(1)}, u32[]{:S(2)}, u32[]{:S(2)}) async-start(f32[8,64,256]{2,1,0:T(8,128)} %broadcast_in_dim.7), calls=%async_computation.2 | async-start | bytes 1048576 | tf_op jit(solution)/shard_map/all_to_all | solution.py:45
  100.3 3.2 %collective-permute-start.19 = (f32[32,256]{1,0:T(8,128)S(1)}, f32[32,256]{1,0:T(8,128)S(1)}, u32[]{:S(2)}, u32[]{:S(2)}) collective-permute-start(f32[32,256]{1,0:T(8,128)S(1)} %add.31), channel_id=1, source_target_pairs={{0,24},{1,25},{2,26},{3,27},{4,28},{5,29},{6,30},{7,31},{8,0},{9,1... | collective-permute-start | bytes 98312 | tf_op jit(solution)/shard_map/ppermute | solution.py:51
  103.6 0.0 collective-permute-start.18
  103.6 1.1 collective-permute-start.17
  104.7 3.6 %collective-permute-start.10 = (f32[64,256]{1,0:T(8,128)}, f32[64,256]{1,0:T(8,128)S(1)}, u32[]{:S(2)}, u32[]{:S(2)}) collective-permute-start(f32[64,256]{1,0:T(8,128)} %get-tuple-element.13.refs_0_), channel_id=1, source_target_pairs={{0,128},{32,160},{64,192},{96,224},{128,0},{160,32},{192,64},{224,... | collective-permute-start | bytes 196616 | tf_op jit(solution)/shard_map/ppermute | solution.py:70
  108.3 0.6 collective-permute-start.9
  108.9 0.1 collective-permute-done.18
  109.1 0.1 collective-permute-done.11.refs_3_
  109.2 1.6 %collective-permute-done.10.refs_2_ = f32[64,256]{1,0:T(8,128)S(1)} collective-permute-done((f32[64,256]{1,0:T(8,128)}, f32[64,256]{1,0:T(8,128)S(1)}, u32[]{:S(2)}, u32[]{:S(2)}) %collective-permute-start.10) | collective-permute-done | bytes 65568 | tf_op jit(solution)/shard_map/ppermute | solution.py:70
  110.8 0.6 copy-done.8
  111.4 1.5 collective-permute-done.9.refs_1_
  112.9 4.8 %all-to-all-done.2 = f32[8,64,256]{2,1,0:T(8,128)S(1)} async-done(((f32[8,64,256]{2,1,0:T(8,128)}), f32[8,64,256]{2,1,0:T(8,128)S(1)}, u32[]{:S(2)}, u32[]{:S(2)}) %all-to-all-start.2) | async-done | bytes 524320 | tf_op jit(solution)/shard_map/all_to_all | solution.py:45
  117.7 1.2 collective-permute-start.25
  118.9 1.0 collective-permute-start.24
  119.9 1.6 %collective-permute-start.22 = (f32[32,256]{1,0:T(8,128)S(1)}, f32[32,256]{1,0:T(8,128)S(1)}, u32[]{:S(2)}, u32[]{:S(2)}) collective-permute-start(f32[32,256]{1,0:T(8,128)S(1)} %add_add_fusion.refs_5_), channel_id=1, source_target_pairs={{0,64},{32,96},{64,128},{96,160},{128,192},{160,224},{192,0},{224,... | collective-permute-start | bytes 98312 | tf_op jit(solution)/shard_map/ppermute | solution.py:70
  121.5 3.1 %collective-permute-start.21 = (f32[32,256]{1,0:T(8,128)S(1)}, f32[32,256]{1,0:T(8,128)S(1)}, u32[]{:S(2)}, u32[]{:S(2)}) collective-permute-start(f32[32,256]{1,0:T(8,128)S(1)} %add_add_fusion.refs_5_), channel_id=1, source_target_pairs={{0,128},{32,160},{64,192},{96,224},{128,0},{160,32},{192,64},{224,... | collective-permute-start | bytes 98312 | tf_op jit(solution)/shard_map/ppermute | solution.py:70
  124.6 3.1 %collective-permute-start.20 = (f32[32,256]{1,0:T(8,128)S(1)}, f32[32,256]{1,0:T(8,128)S(1)}, u32[]{:S(2)}, u32[]{:S(2)}) collective-permute-start(f32[32,256]{1,0:T(8,128)S(1)} %add_add_fusion.refs_5_), channel_id=1, source_target_pairs={{0,192},{32,224},{64,0},{96,32},{128,64},{160,96},{192,128},{224,1... | collective-permute-start | bytes 98312 | tf_op jit(solution)/shard_map/ppermute | solution.py:70
  127.7 1.0 pad_maximum_fusion.1
  128.6 0.1 collective-permute-start.12
  128.7 0.5 collective-permute-done.20.refs_6_
  129.3 0.3 collective-permute-start.23
  129.6 0.7 collective-permute-done.12.refs_4_
  130.2 0.7 collective-permute-done.23.refs_9_
  130.9 0.8 copy-done.5
  131.8 0.8 copy-done.7
  132.6 0.8 copy-done.9
  133.4 2.8 %shard_map.54 = (f32[512,256]{1,0:T(8,128)S(1)}, f32[64,256]{1,0:T(8,128)}) custom-call(s32[2]{0:T(128)S(1)} %pad_add_fusion.place, f32[256,256]{1,0:T(8,128)S(1)} %copy-done.2, f32[64,256]{1,0:T(8,128)S(1)} %copy-done.3, f32[64,256]{1,0:T(8,128)S(1)} %copy-done.5, f32[512,256]{1,0:T(8,128)S(1)} %bitcast.19, f32[64,256]{1,0:T(8,128)} %get-tuple-element.13.refs_0_, ...), custom_call_target="tpu_custom_call" | custom-call | flops 1 | bytes 1 | tf_op jit(solution)/shard_map/pallas_call | solution.py:178
  136.3 4.4 %shard_map.55.matrix = f32[2048,512]{1,0:T(8,128)S(1)} custom-call(s32[1]{0:T(128)} %bitcast.y_ref, f32[2048,512]{1,0:T(8,128)} %copy-done, f32[512,256]{1,0:T(8,128)S(1)} %get-tuple-element.18.left, f32[512,256]{1,0:T(8,128)S(1)} %bitcast.20, f32[512,256]{1,0:T(8,128)S(1)} %bitcast.30, f32[512,256]{1,0:T(8,128)S(1)} %bitcast.26, ...), custom_call_target="tpu_custom_call" | custom-call | flops 1 | bytes 1 | tf_op jit(solution)/shard_map/pallas_call | solution.py:106
  140.7 3.5 %collective-permute-done.24.refs_0_ = f32[512,256]{1,0:T(8,128)S(1)} collective-permute-done((f32[512,256]{1,0:T(8,128)S(1)}, f32[512,256]{1,0:T(8,128)S(1)}, u32[]{:S(2)}, u32[]{:S(2)}) %collective-permute-start.24) | collective-permute-done | bytes 524320 | tf_op jit(solution)/shard_map/ppermute | solution.py:51
  144.3 3.4 %shard_map.56 = f32[2048,512]{1,0:T(8,128)} custom-call(s32[1]{0:T(128)} %bitcast.y_ref, f32[2048,512]{1,0:T(8,128)S(1)} %shard_map.55.matrix, f32[512,256]{1,0:T(8,128)S(1)} %bitcast.21, f32[512,256]{1,0:T(8,128)S(1)} %collective-permute-done.24.refs_0_, f32[512,256]{1,0:T(8,128)S(1)} %collective-permute-done.25.refs_1_, ...), custom_call_target="tpu_custom_call" | custom-call | flops 1 | bytes 1 | tf_op jit(solution)/shard_map/pallas_call | solution.py:230
  (31 shorter events, 0.1 us)
Async XLA Ops:
  2.3 25.0 %all-to-all-start = ((f32[8,64,256]{2,1,0:T(8,128)}), f32[8,64,256]{2,1,0:T(8,128)S(1)}, u32[]{:S(2)}, u32[]{:S(2)}) async-start(f32[8,64,256]{2,1,0:T(8,128)} %broadcast_in_dim.6), calls=%async_computation | async-start | bytes 1048576 | tf_op jit(solution)/shard_map/all_to_all | solution.py:45
  10.8 23.6 %collective-permute-start = (f32[64,256]{1,0:T(8,128)}, f32[64,256]{1,0:T(8,128)S(1)}, u32[]{:S(2)}, u32[]{:S(2)}) collective-permute-start(f32[64,256]{1,0:T(8,128)} %panel.1), channel_id=1, source_target_pairs={{0,0},{1,32},{2,64},{3,96},{4,128},{5,160},{6,192},{7,224},{8,1},{... | collective-permute-start | bytes 196616 | tf_op jit(solution)/shard_map/ppermute | solution.py:257
  27.3 19.2 %collective-permute-start.7 = (f32[512,256]{1,0:T(8,128)S(1)}, f32[512,256]{1,0:T(8,128)S(1)}, u32[]{:S(2)}, u32[]{:S(2)}) collective-permute-start(f32[512,256]{1,0:T(8,128)S(1)} %bitcast.22), channel_id=1, source_target_pairs={{0,24},{1,25},{2,26},{3,27},{4,28},{5,29},{6,30},{7,31},{8,0},{9,1... | collective-permute-start | bytes 1572872 | tf_op jit(solution)/shard_map/ppermute | solution.py:51
  30.5 16.4 %collective-permute-start.6 = (f32[512,256]{1,0:T(8,128)S(1)}, f32[512,256]{1,0:T(8,128)S(1)}, u32[]{:S(2)}, u32[]{:S(2)}) collective-permute-start(f32[512,256]{1,0:T(8,128)S(1)} %bitcast.23), channel_id=1, source_target_pairs={{0,16},{1,17},{2,18},{3,19},{4,20},{5,21},{6,22},{7,23},{8,24},{9,... | collective-permute-start | bytes 1572872 | tf_op jit(solution)/shard_map/ppermute | solution.py:51
  33.4 23.2 %collective-permute-start.5 = (f32[512,256]{1,0:T(8,128)S(1)}, f32[512,256]{1,0:T(8,128)S(1)}, u32[]{:S(2)}, u32[]{:S(2)}) collective-permute-start(f32[512,256]{1,0:T(8,128)S(1)} %bitcast.24), channel_id=1, source_target_pairs={{0,8},{1,9},{2,10},{3,11},{4,12},{5,13},{6,14},{7,15},{8,16},{9,17... | collective-permute-start | bytes 1572872 | tf_op jit(solution)/shard_map/ppermute | solution.py:51
  34.4 4.6 %collective-permute-start.3 = (f32[64,256]{1,0:T(8,128)S(1)}, f32[64,256]{1,0:T(8,128)S(1)}, u32[]{:S(2)}, u32[]{:S(2)}) collective-permute-start(f32[64,256]{1,0:T(8,128)S(1)} %collective-permute-done.refs_0_), channel_id=1, source_target_pairs={{0,64},{32,96},{64,128},{96,160},{128,192},{160,224},{192,0},{224,... | collective-permute-start | bytes 196616 | tf_op jit(solution)/shard_map/ppermute | solution.py:70
  35.9 5.8 %collective-permute-start.2 = (f32[64,256]{1,0:T(8,128)S(1)}, f32[64,256]{1,0:T(8,128)S(1)}, u32[]{:S(2)}, u32[]{:S(2)}) collective-permute-start(f32[64,256]{1,0:T(8,128)S(1)} %collective-permute-done.refs_0_), channel_id=1, source_target_pairs={{0,128},{32,160},{64,192},{96,224},{128,0},{160,32},{192,64},{224,... | collective-permute-start | bytes 196616 | tf_op jit(solution)/shard_map/ppermute | solution.py:70
  39.0 4.3 %collective-permute-start.1 = (f32[64,256]{1,0:T(8,128)S(1)}, f32[64,256]{1,0:T(8,128)S(1)}, u32[]{:S(2)}, u32[]{:S(2)}) collective-permute-start(f32[64,256]{1,0:T(8,128)S(1)} %collective-permute-done.refs_0_), channel_id=1, source_target_pairs={{0,192},{32,224},{64,0},{96,32},{128,64},{160,96},{192,128},{224,1... | collective-permute-start | bytes 196616 | tf_op jit(solution)/shard_map/ppermute | solution.py:70
  43.3 2.7 %collective-permute-start.4 = (f32[4,64,256]{2,1,0:T(8,128)S(1)}, f32[4,64,256]{2,1,0:T(8,128)S(1)}, u32[]{:S(2)}, u32[]{:S(2)}) collective-permute-start(f32[4,64,256]{2,1,0:T(8,128)S(1)} %pad_maximum_fusion), channel_id=1, source_target_pairs={{0,32},{32,0},{64,96},{96,64},{128,160},{160,128},{192,224},{224,1... | collective-permute-start | bytes 786440 | tf_op jit(solution)/shard_map/ppermute | solution.py:77
  43.5 2.2 %copy-start.1 = (f32[2048,512]{1,0:T(8,128)S(1)}, f32[2048,512]{1,0:T(8,128)}, u32[]{:S(2)}) copy-start(f32[2048,512]{1,0:T(8,128)} %matrix) | copy-start | bytes 12582916
  45.7 11.0 %copy-start.2 = (f32[256,256]{1,0:T(8,128)S(1)}, f32[256,256]{1,0:T(8,128)}, u32[]{:S(2)}) copy-start(f32[256,256]{1,0:T(8,128)} %factor.3) | copy-start | bytes 786436
  45.9 14.4 %copy-start = (f32[2048,512]{1,0:T(8,128)}, f32[2048,512]{1,0:T(8,128)S(1)}, u32[]{:S(2)}) copy-start(f32[2048,512]{1,0:T(8,128)S(1)} %shard_map.50.matrix) | copy-start | bytes 12582916
  60.3 70.6 %copy-start.3 = (f32[64,256]{1,0:T(8,128)S(1)}, f32[64,256]{1,0:T(8,128)}, u32[]{:S(2)}) copy-start(f32[64,256]{1,0:T(8,128)} %panel.1) | copy-start | bytes 196612
  77.5 9.3 %collective-permute-start.15 = (f32[32,256]{1,0:T(8,128)S(1)}, f32[32,256]{1,0:T(8,128)S(1)}, u32[]{:S(2)}, u32[]{:S(2)}) collective-permute-start(f32[32,256]{1,0:T(8,128)S(1)} %get-tuple-element.14), channel_id=1, source_target_pairs={{0,6},{1,7},{2,4},{3,5},{4,2},{5,3},{6,0},{7,1},{8,14},{9,15},{10,... | collective-permute-start | bytes 98312 | tf_op jit(solution)/shard_map/ppermute | solution.py:59
  79.0 7.9 %collective-permute-start.14 = (f32[32,256]{1,0:T(8,128)S(1)}, f32[32,256]{1,0:T(8,128)S(1)}, u32[]{:S(2)}, u32[]{:S(2)}) collective-permute-start(f32[32,256]{1,0:T(8,128)S(1)} %get-tuple-element.14), channel_id=1, source_target_pairs={{0,4},{1,5},{2,6},{3,7},{4,0},{5,1},{6,2},{7,3},{8,12},{9,13},{10,... | collective-permute-start | bytes 98312 | tf_op jit(solution)/shard_map/ppermute | solution.py:59
  80.6 6.3 %collective-permute-start.13 = (f32[32,256]{1,0:T(8,128)S(1)}, f32[32,256]{1,0:T(8,128)S(1)}, u32[]{:S(2)}, u32[]{:S(2)}) collective-permute-start(f32[32,256]{1,0:T(8,128)S(1)} %get-tuple-element.14), channel_id=1, source_target_pairs={{0,2},{1,3},{2,0},{3,1},{4,6},{5,7},{6,4},{7,5},{8,10},{9,11},{10,... | collective-permute-start | bytes 98312 | tf_op jit(solution)/shard_map/ppermute | solution.py:59
  84.0 11.9 %collective-permute-start.8 = (f32[64,256]{1,0:T(8,128)}, f32[64,256]{1,0:T(8,128)S(1)}, u32[]{:S(2)}, u32[]{:S(2)}) collective-permute-start(f32[64,256]{1,0:T(8,128)} %get-tuple-element.13.refs_0_), channel_id=1, source_target_pairs={{0,0},{32,1},{64,2},{96,3},{128,4},{160,5},{192,6},{224,7},{1,8},{... | collective-permute-start | bytes 196616 | tf_op jit(solution)/shard_map/ppermute | solution.py:274
  86.9 4.0 %collective-permute-start.16 = (f32[32,256]{1,0:T(8,128)S(1)}, f32[32,256]{1,0:T(8,128)S(1)}, u32[]{:S(2)}, u32[]{:S(2)}) collective-permute-start(f32[32,256]{1,0:T(8,128)S(1)} %add_add_fusion.1), channel_id=1, source_target_pairs={{0,1},{1,0},{2,3},{3,2},{4,5},{5,4},{6,7},{7,6},{8,9},{9,8},{10,11... | collective-permute-start | bytes 98312 | tf_op jit(solution)/shard_map/ppermute | solution.py:59
  96.0 0.8 copy-start.4
  96.8 20.9 %all-to-all-start.2 = ((f32[8,64,256]{2,1,0:T(8,128)}), f32[8,64,256]{2,1,0:T(8,128)S(1)}, u32[]{:S(2)}, u32[]{:S(2)}) async-start(f32[8,64,256]{2,1,0:T(8,128)} %broadcast_in_dim.7), calls=%async_computation.2 | async-start | bytes 1048576 | tf_op jit(solution)/shard_map/all_to_all | solution.py:45
  100.3 8.0 %collective-permute-start.19 = (f32[32,256]{1,0:T(8,128)S(1)}, f32[32,256]{1,0:T(8,128)S(1)}, u32[]{:S(2)}, u32[]{:S(2)}) collective-permute-start(f32[32,256]{1,0:T(8,128)S(1)} %add.31), channel_id=1, source_target_pairs={{0,24},{1,25},{2,26},{3,27},{4,28},{5,29},{6,30},{7,31},{8,0},{9,1... | collective-permute-start | bytes 98312 | tf_op jit(solution)/shard_map/ppermute | solution.py:51
  103.6 5.5 %collective-permute-start.18 = (f32[32,256]{1,0:T(8,128)S(1)}, f32[32,256]{1,0:T(8,128)S(1)}, u32[]{:S(2)}, u32[]{:S(2)}) collective-permute-start(f32[32,256]{1,0:T(8,128)S(1)} %add.31), channel_id=1, source_target_pairs={{0,16},{1,17},{2,18},{3,19},{4,20},{5,21},{6,22},{7,23},{8,24},{9,... | collective-permute-start | bytes 98312 | tf_op jit(solution)/shard_map/ppermute | solution.py:51
  103.6 5.5 %collective-permute-start.17 = (f32[32,256]{1,0:T(8,128)S(1)}, f32[32,256]{1,0:T(8,128)S(1)}, u32[]{:S(2)}, u32[]{:S(2)}) collective-permute-start(f32[32,256]{1,0:T(8,128)S(1)} %add.31), channel_id=1, source_target_pairs={{0,8},{1,9},{2,10},{3,11},{4,12},{5,13},{6,14},{7,15},{8,16},{9,17... | collective-permute-start | bytes 98312 | tf_op jit(solution)/shard_map/ppermute | solution.py:51
  104.7 4.5 %collective-permute-start.11 = (f32[64,256]{1,0:T(8,128)}, f32[64,256]{1,0:T(8,128)S(1)}, u32[]{:S(2)}, u32[]{:S(2)}) collective-permute-start(f32[64,256]{1,0:T(8,128)} %get-tuple-element.13.refs_0_), channel_id=1, source_target_pairs={{0,64},{32,96},{64,128},{96,160},{128,192},{160,224},{192,0},{224,... | collective-permute-start | bytes 196616 | tf_op jit(solution)/shard_map/ppermute | solution.py:70
  104.7 6.1 %collective-permute-start.10 = (f32[64,256]{1,0:T(8,128)}, f32[64,256]{1,0:T(8,128)S(1)}, u32[]{:S(2)}, u32[]{:S(2)}) collective-permute-start(f32[64,256]{1,0:T(8,128)} %get-tuple-element.13.refs_0_), channel_id=1, source_target_pairs={{0,128},{32,160},{64,192},{96,224},{128,0},{160,32},{192,64},{224,... | collective-permute-start | bytes 196616 | tf_op jit(solution)/shard_map/ppermute | solution.py:70
  108.3 4.6 %collective-permute-start.9 = (f32[64,256]{1,0:T(8,128)}, f32[64,256]{1,0:T(8,128)}, u32[]{:S(2)}, u32[]{:S(2)}) collective-permute-start(f32[64,256]{1,0:T(8,128)} %get-tuple-element.13.refs_0_), channel_id=1, source_target_pairs={{0,192},{32,224},{64,0},{96,32},{128,64},{160,96},{192,128},{224,1... | collective-permute-start | bytes 196616 | tf_op jit(solution)/shard_map/ppermute | solution.py:70
  109.2 1.6 %copy-start.6 = (f32[64,256]{1,0:T(8,128)}, f32[64,256]{1,0:T(8,128)S(1)}, u32[]{:S(2)}) copy-start(f32[64,256]{1,0:T(8,128)S(1)} %collective-permute-done.11.refs_3_) | copy-start | bytes 196612
  110.8 0.6 copy-start.8
  117.7 23.0 %collective-permute-start.26 = (f32[512,256]{1,0:T(8,128)S(1)}, f32[512,256]{1,0:T(8,128)S(1)}, u32[]{:S(2)}, u32[]{:S(2)}) collective-permute-start(f32[512,256]{1,0:T(8,128)S(1)} %bitcast.27), channel_id=1, source_target_pairs={{0,24},{1,25},{2,26},{3,27},{4,28},{5,29},{6,30},{7,31},{8,0},{9,1... | collective-permute-start | bytes 1572872 | tf_op jit(solution)/shard_map/ppermute | solution.py:51
  117.7 23.0 %collective-permute-start.25 = (f32[512,256]{1,0:T(8,128)S(1)}, f32[512,256]{1,0:T(8,128)S(1)}, u32[]{:S(2)}, u32[]{:S(2)}) collective-permute-start(f32[512,256]{1,0:T(8,128)S(1)} %bitcast.28), channel_id=1, source_target_pairs={{0,16},{1,17},{2,18},{3,19},{4,20},{5,21},{6,22},{7,23},{8,24},{9,... | collective-permute-start | bytes 1572872 | tf_op jit(solution)/shard_map/ppermute | solution.py:51
  118.9 25.3 %collective-permute-start.24 = (f32[512,256]{1,0:T(8,128)S(1)}, f32[512,256]{1,0:T(8,128)S(1)}, u32[]{:S(2)}, u32[]{:S(2)}) collective-permute-start(f32[512,256]{1,0:T(8,128)S(1)} %bitcast.29), channel_id=1, source_target_pairs={{0,8},{1,9},{2,10},{3,11},{4,12},{5,13},{6,14},{7,15},{8,16},{9,17... | collective-permute-start | bytes 1572872 | tf_op jit(solution)/shard_map/ppermute | solution.py:51
  119.9 4.7 %collective-permute-start.22 = (f32[32,256]{1,0:T(8,128)S(1)}, f32[32,256]{1,0:T(8,128)S(1)}, u32[]{:S(2)}, u32[]{:S(2)}) collective-permute-start(f32[32,256]{1,0:T(8,128)S(1)} %add_add_fusion.refs_5_), channel_id=1, source_target_pairs={{0,64},{32,96},{64,128},{96,160},{128,192},{160,224},{192,0},{224,... | collective-permute-start | bytes 98312 | tf_op jit(solution)/shard_map/ppermute | solution.py:70
  121.5 7.1 %collective-permute-start.21 = (f32[32,256]{1,0:T(8,128)S(1)}, f32[32,256]{1,0:T(8,128)S(1)}, u32[]{:S(2)}, u32[]{:S(2)}) collective-permute-start(f32[32,256]{1,0:T(8,128)S(1)} %add_add_fusion.refs_5_), channel_id=1, source_target_pairs={{0,128},{32,160},{64,192},{96,224},{128,0},{160,32},{192,64},{224,... | collective-permute-start | bytes 98312 | tf_op jit(solution)/shard_map/ppermute | solution.py:70
  124.6 4.7 %collective-permute-start.20 = (f32[32,256]{1,0:T(8,128)S(1)}, f32[32,256]{1,0:T(8,128)S(1)}, u32[]{:S(2)}, u32[]{:S(2)}) collective-permute-start(f32[32,256]{1,0:T(8,128)S(1)} %add_add_fusion.refs_5_), channel_id=1, source_target_pairs={{0,192},{32,224},{64,0},{96,32},{128,64},{160,96},{192,128},{224,1... | collective-permute-start | bytes 98312 | tf_op jit(solution)/shard_map/ppermute | solution.py:70
  128.6 1.6 %collective-permute-start.12 = (f32[4,64,256]{2,1,0:T(8,128)S(1)}, f32[4,64,256]{2,1,0:T(8,128)S(1)}, u32[]{:S(2)}, u32[]{:S(2)}) collective-permute-start(f32[4,64,256]{2,1,0:T(8,128)S(1)} %pad_maximum_fusion.1), channel_id=1, source_target_pairs={{0,32},{32,0},{64,96},{96,64},{128,160},{160,128},{192,224},{224,1... | collective-permute-start | bytes 786440 | tf_op jit(solution)/shard_map/ppermute | solution.py:77
  129.3 1.7 %collective-permute-start.23 = (f32[4,32,256]{2,1,0:T(8,128)S(1)}, f32[4,32,256]{2,1,0:T(8,128)S(1)}, u32[]{:S(2)}, u32[]{:S(2)}) collective-permute-start(f32[4,32,256]{2,1,0:T(8,128)S(1)} %pad_maximum_fusion.2), channel_id=1, source_target_pairs={{0,32},{32,0},{64,96},{96,64},{128,160},{160,128},{192,224},{224,1... | collective-permute-start | bytes 393224 | tf_op jit(solution)/shard_map/ppermute | solution.py:77
  130.9 0.8 copy-start.5
  131.8 0.8 copy-start.7
  132.6 0.8 copy-start.9
